TPU v7x, 32 devices: a whole 2x2x4 slice. The times are simulated.
32 devices in a mesh: gz: 8 (over z, y), gy: 4 (over x, core).
Axes of the slice: x: 2, y: 2, z: 4, core: 2. Of those that a mesh axis runs over, the one named last changes fastest.
Arguments:
- fraction: float32 [64, 128, 512], P('gz', 'gy'), may hold values from 0 to 1
- source: float32 [64, 128, 512], P('gz', 'gy'), may hold values from -40 to 40, as said below
- bubble_label: int32 [64, 128, 512], P('gz', 'gy'), may hold values from -1 to 511, as said below
- subdomain: int32 [64, 128, 512], P('gz', 'gy'), may hold values from 0 to 127, as said below
- coarse_inverse: float32 [640, 640], P(('gz', 'gy')), may hold values from -0.2 to 0.2, as said below
Outputs:
- iterate: float32 [64, 128, 512], P('gz', 'gy')
- residual: float32 [64, 128, 512], P('gz', 'gy')
Inputs may be any that keep to these rules, and one draw needn't show every extreme that they name: `source`: vertical factor 1 + 2 z / 64, so magnitudes grow with depth. `bubble_label`: A cell at plane z and row y carries -1 or the number of a bubble of slab block a and row block y // 32 with |a - z // 8| <= 1; the bubbles of slab block a and row block b are numbered (a 4 + b) * 16 + i with i < 16. Rows y with y % 32 == 0 carry -1. `subdomain`: cells of slab block a and row block b carry (a 4 + b) * 4 + i with i < 4; the number does not change along z and y inside a block and never falls along x. `coarse_inverse`: symmetric positive definite.
All inputs are finite; a program needn't handle non-finite values.
Results may differ from a plain program's by a relative error of at most 0.0003.
Values sent between devices are 32-bit elements; how exact they have to be, the bound alone decides.
No kernel may reach another device: no remote copies, remote signals or barrier semaphores. Data moves between devices by JAX's collectives and lax.ppermute only.
A program may use at most 64 MiB of HBM per device.

v0:
```python
from functools import reduce

import jax
import jax.numpy as jnp
from jax import lax
from jax.sharding import PartitionSpec as P

S_DEV = 4
B_DEV = 16
ITERS = 3


surface_tension = 0.5
shift_term = 0.05
gas_drop = 0.75
norm_floor = 0.25
highest = lax.Precision.HIGHEST


def with_halo(block, sides, width):
    for axis, dim in sides:
        count = lax.axis_size(axis)
        forward = [(i, i + 1) for i in range(count - 1)]
        backward = [(target, source) for source, target in forward]
        low = lax.ppermute(
            lax.slice_in_dim(block, block.shape[dim] - width, None, axis=dim), axis, forward
        )
        high = lax.ppermute(lax.slice_in_dim(block, 0, width, axis=dim), axis, backward)
        block = jnp.concatenate([low, block, high], axis=dim)
    return block


def add_all(items):
    return reduce(lambda first, second: first + second, items)


def widen_x(block):
    return jnp.pad(block, [(0, 0)] * (block.ndim - 1) + [(1, 1)])


def six_neighbours(padded):
    return [
        padded[2:, 1:-1, 1:-1],
        padded[:-2, 1:-1, 1:-1],
        padded[1:-1, 2:, 1:-1],
        padded[1:-1, :-2, 1:-1],
        padded[1:-1, 1:-1, 2:],
        padded[1:-1, 1:-1, :-2],
    ]


def normals(padded):
    along = [
        0.5 * (padded[2:, 1:-1, 1:-1] - padded[:-2, 1:-1, 1:-1]),
        0.5 * (padded[1:-1, 2:, 1:-1] - padded[1:-1, :-2, 1:-1]),
        0.5 * (padded[1:-1, 1:-1, 2:] - padded[1:-1, 1:-1, :-2]),
    ]
    length = jnp.maximum(
        jnp.sqrt(along[0] * along[0] + along[1] * along[1] + along[2] * along[2]), norm_floor
    )
    return jnp.stack([member / length for member in along])


def curvature(padded):
    return -(
        0.5 * (padded[0, 2:, 1:-1, 1:-1] - padded[0, :-2, 1:-1, 1:-1])
        + 0.5 * (padded[1, 1:-1, 2:, 1:-1] - padded[1, 1:-1, :-2, 1:-1])
        + 0.5 * (padded[2, 1:-1, 1:-1, 2:] - padded[2, 1:-1, 1:-1, :-2])
    )


def assemble(frac_padded, kappa_padded, source):
    density = 1.0 - gas_drop * frac_padded
    centre = density[1:-1, 1:-1, 1:-1]
    coefs = [2.0 / (centre + other) for other in six_neighbours(density)]
    fraction = frac_padded[1:-1, 1:-1, 1:-1]
    kappa = kappa_padded[1:-1, 1:-1, 1:-1]
    terms = [
        coef * (0.5 * (kappa + kappa_other)) * (frac_other - fraction)
        for coef, frac_other, kappa_other in zip(
            coefs, six_neighbours(frac_padded), six_neighbours(kappa_padded)
        )
    ]
    rhs = source - surface_tension * add_all(terms)
    diagonal = shift_term + add_all(coefs)
    return (coefs, diagonal, rhs)


def operate_padded(padded, coefs, diagonal):
    return diagonal * padded[1:-1, 1:-1, 1:-1] - add_all(
        [coef * other for coef, other in zip(coefs, six_neighbours(padded))]
    )


def factor_planes(diagonal_planes, down_planes):
    inverse = [1.0 / diagonal_planes[0]]
    mults = [None]
    for level in range(1, len(diagonal_planes)):
        mult = down_planes[level] * inverse[level - 1]
        inverse.append(1.0 / (diagonal_planes[level] - mult * down_planes[level]))
        mults.append(mult)
    return (inverse, mults)


def solve_planes(values, inverse, mults, up_planes):
    count = len(values)
    forward = [values[0]]
    for level in range(1, count):
        forward.append(values[level] + mults[level] * forward[level - 1])
    result = [forward[count - 1] * inverse[count - 1]]
    for level in range(count - 2, -1, -1):
        result.insert(0, (forward[level] + up_planes[level] * result[0]) * inverse[level])
    return result


def inside_grid(slab_index, slabs, column_index, columns, planes, rows_here, margin):
    height = jnp.arange(planes + 2 * margin, dtype=jnp.int32) + slab_index * planes - margin
    across = jnp.arange(rows_here + 2 * margin, dtype=jnp.int32) + column_index * rows_here - margin
    keep_z = (height >= 0) & (height < slabs * planes)
    keep_y = (across >= 0) & (across < columns * rows_here)
    return (keep_z[:, None, None] & keep_y[None, :, None]).astype(jnp.float32)


def region_sums(field, flat_bins, slots):
    flat_field = field.reshape(field.shape[0], -1)

    def one_plane(pair):
        plane_bins, plane_values = pair
        onehot = (plane_bins[None, :] == slots[:, None]).astype(jnp.float32)
        return jnp.dot(onehot, plane_values, precision=highest)

    return jnp.sum(lax.map(one_plane, (flat_bins, flat_field)), axis=0)


def region_values(window, flat_bins, slots):

    def one_plane(plane_bins):
        onehot = (plane_bins[None, :] == slots[:, None]).astype(jnp.float32)
        return jnp.dot(window, onehot, precision=highest)

    return lax.map(one_plane, flat_bins)


def on_device(fraction, source, bubble_label, subdomain, coarse_inverse):
    planes = fraction.shape[0]
    rows_here = fraction.shape[1]
    slabs = lax.axis_size("gz")
    columns = lax.axis_size("gy")
    slab_index = lax.axis_index("gz")
    column_index = lax.axis_index("gy")
    devices = slabs * columns
    here = slab_index * columns + column_index
    deep = widen_x(with_halo(fraction, (("gz", 0), ("gy", 1)), 3))
    normal = normals(deep) * inside_grid(
        slab_index, slabs, column_index, columns, planes, rows_here, 2
    )
    kappa = curvature(widen_x(normal)) * inside_grid(
        slab_index, slabs, column_index, columns, planes, rows_here, 1
    )
    frac_padded = deep[2:-2, 2:-2, :]
    kappa_padded = widen_x(kappa)
    coefs, diagonal, rhs = assemble(frac_padded, kappa_padded, source)
    inverse, mults = factor_planes(
        [diagonal[level] for level in range(planes)], [coefs[1][level] for level in range(planes)]
    )
    up_planes = [coefs[0][level] for level in range(planes)]
    owner_slab = bubble_label // B_DEV // columns
    bubble_bin = S_DEV + (owner_slab - slab_index + 1) * B_DEV + bubble_label % B_DEV
    bins = jnp.where(bubble_label >= 0, bubble_bin, subdomain - here * S_DEV)
    flat_bins = bins.reshape(planes, -1)
    slots = jnp.arange(S_DEV + 3 * B_DEV, dtype=jnp.int32)
    device_rows = jnp.arange(devices, dtype=jnp.int32)[:, None]
    blank = jnp.zeros((S_DEV,), jnp.float32)

    def precondition(residual):
        block = jnp.stack(
            solve_planes([residual[level] for level in range(planes)], inverse, mults, up_planes)
        )
        partial_value = region_sums(residual, flat_bins, slots)
        own_row = jnp.concatenate(
            [partial_value[:S_DEV], partial_value[S_DEV + B_DEV : S_DEV + 2 * B_DEV]]
        )
        below_row = jnp.concatenate([blank, partial_value[S_DEV : S_DEV + B_DEV]])
        above_row = jnp.concatenate([blank, partial_value[S_DEV + 2 * B_DEV :]])
        spread = (
            jnp.where(device_rows == here, own_row, 0.0)
            + jnp.where(device_rows == here - columns, below_row, 0.0)
            + jnp.where(device_rows == here + columns, above_row, 0.0)
        ).reshape(-1)
        totals = lax.psum(spread, ("gz", "gy"))
        coarse_own = jnp.dot(coarse_inverse, totals, precision=highest)
        bubble_rows = with_halo(coarse_own[S_DEV:][None, :], (("gz", 0),), 1)
        window = jnp.concatenate(
            [coarse_own[:S_DEV], bubble_rows[0], coarse_own[S_DEV:], bubble_rows[2]]
        )
        correction = region_values(window, flat_bins, slots).reshape(residual.shape)
        direction = block + correction
        product = lax.psum(jnp.sum(residual * direction), ("gz", "gy"))
        return (direction, product)

    iterate = jnp.zeros_like(rhs)
    residual = rhs
    direction, product = precondition(residual)
    search = direction
    for sweep in range(ITERS):
        padded = widen_x(with_halo(search, (("gz", 0), ("gy", 1)), 1))
        image = operate_padded(padded, coefs, diagonal)
        alpha = product / lax.psum(jnp.sum(search * image), ("gz", "gy"))
        iterate = iterate + alpha * search
        residual = residual - alpha * image
        if sweep + 1 < ITERS:
            direction, fresh = precondition(residual)
            search = direction + fresh / product * search
            product = fresh
    return (iterate, residual)


def solution(mesh):
    placed = (
        P("gz", "gy", None),
        P("gz", "gy", None),
        P("gz", "gy", None),
        P("gz", "gy", None),
        P(("gz", "gy"), None),
    )
    return jax.shard_map(
        on_device,
        mesh=mesh,
        in_specs=placed,
        out_specs=(P("gz", "gy", None), P("gz", "gy", None)),
        check_vma=False,
    )
```

profile of v0, /device:TPU:0, one launch (start us, length us, event | category | flops | bytes accessed | tf_op | source)
XLA Modules:
  0.0 645.9 jit_solution(17723499173487809943)
XLA Ops:
  1.8 4.9 collective-permute-start
  11.5 3.4 collective-permute-done.1
  17.7 3.6 collective-permute-done.3
  25.5 3.4 fusion.59
  30.2 32.0 %while.66 = (s32[]{:T(128)}, f32[8,52]{1,0:T(8,128)S(1)}, s32[8,16384]{1,0:T(8,128)}, f32[8,16384]{1,0:T(8,128)}, s32[]{:T(128)}, /*index=5*/s32[]{:T(128)}) while((s32[]{:T(128)}, f32[8,52]{1,0:T(8,128)S(1)}, s32[8,16384]{1,0:T(8,128)}, f32[8,16384]{1,0:T(8,128)}, s32[]{:T(128)}, /*index=5*/s32[]{:T(128)}) %tuple.197), condition=%wide.region_1.2_spmd.clone, body=%wide.region_0.1_spmd.clone.sunk | while | flops 11075586 | bytes 263357 | solution.py:132
  31.3 2.9 fusion.176
  39.3 2.9 fusion.176
  43.3 2.9 fusion.176
  47.3 2.9 fusion.176
  51.3 2.9 fusion.176
  59.3 2.9 fusion.176
  62.7 43.5 %psum.63 = f32[640]{0:T(1024)S(1)} all-reduce(f32[640]{0:T(1024)S(1)} %add.777), channel_id=1, replica_groups=mesh['gz'=8,'gy'=4] {'gz','gy'}, use_global_device_ids=true, to_apply=%region_3.4 | all-reduce | flops 640 | bytes 5120 | tf_op jit(solution)/shard_map/psum | solution.py:190
  106.5 4.2 collective-permute-start.4
  116.3 23.2 %while.67 = (s32[]{:T(128)}, f32[8,16384]{1,0:T(8,128)S(1)}, s32[8,16384]{1,0:T(8,128)}, f32[52]{0:T(128)S(1)}, s32[]{:T(128)}, /*index=5*/s32[]{:T(128)}) while((s32[]{:T(128)}, f32[8,16384]{1,0:T(8,128)S(1)}, s32[8,16384]{1,0:T(8,128)}, f32[52]{0:T(128)S(1)}, s32[]{:T(128)}, /*index=5*/s32[]{:T(128)}) %tuple.192), condition=%wide.region_5.6_spmd.clone, body=%wide.region_4.5_spmd.clone.sunk | while | flops 11075586 | bytes 393501 | solution.py:141
  143.2 5.0 collective-permute-start.7
  152.6 3.6 collective-permute-start.9
  158.1 3.3 multiply_reduce_fusion.4
  161.4 44.1 %all-reduce.12 = (f32[]{:T(128)}, f32[]{:T(128)}) all-reduce(f32[]{:T(128)} %get-tuple-element.231, f32[]{:T(128)} %get-tuple-element.230), channel_id=1, replica_groups=mesh['gz'=8,'gy'=4] {'gz','gy'}, use_global_device_ids=true, to_apply=%region_7.8 | all-reduce | flops 2 | bytes 16 | tf_op jit(solution)/shard_map/psum | solution.py:198
  209.1 32.1 %while.68 = (s32[]{:T(128)}, f32[8,52]{1,0:T(8,128)S(1)}, s32[8,16384]{1,0:T(8,128)}, f32[8,16384]{1,0:T(8,128)}, s32[]{:T(128)}, /*index=5*/s32[]{:T(128)}) while((s32[]{:T(128)}, f32[8,52]{1,0:T(8,128)S(1)}, s32[8,16384]{1,0:T(8,128)}, f32[8,16384]{1,0:T(8,128)}, s32[]{:T(128)}, /*index=5*/s32[]{:T(128)}) %tuple.198), condition=%wide.region_11.12_spmd.clone, body=%wide.region_10.11_spmd.clone.sunk | while | flops 11075586 | bytes 263357 | solution.py:132
  210.2 2.9 fusion.179
  214.2 2.9 fusion.179
  218.2 2.9 fusion.179
  222.2 2.9 fusion.179
  226.2 2.9 fusion.179
  234.2 2.9 fusion.179
  238.2 2.9 fusion.179
  241.7 41.5 %psum.66 = f32[640]{0:T(1024)S(1)} all-reduce(f32[640]{0:T(1024)S(1)} %add.800), channel_id=1, replica_groups=mesh['gz'=8,'gy'=4] {'gz','gy'}, use_global_device_ids=true, to_apply=%region_13.14 | all-reduce | flops 640 | bytes 5120 | tf_op jit(solution)/shard_map/psum | solution.py:190
  283.4 4.2 collective-permute-start.10
  293.2 23.2 %while.69 = (s32[]{:T(128)}, f32[8,16384]{1,0:T(8,128)S(1)}, s32[8,16384]{1,0:T(8,128)}, f32[52]{0:T(128)S(1)}, s32[]{:T(128)}, /*index=5*/s32[]{:T(128)}) while((s32[]{:T(128)}, f32[8,16384]{1,0:T(8,128)S(1)}, s32[8,16384]{1,0:T(8,128)}, f32[52]{0:T(128)S(1)}, s32[]{:T(128)}, /*index=5*/s32[]{:T(128)}) %tuple.194), condition=%wide.region_15.16_spmd.clone, body=%wide.region_14.15_spmd.clone.sunk | while | flops 11075586 | bytes 393501 | solution.py:141
  318.7 40.2 %psum.67 = f32[]{:T(128)} all-reduce(f32[]{:T(128)} %multiply_reduce_fusion.3), channel_id=1, replica_groups=mesh['gz'=8,'gy'=4] {'gz','gy'}, use_global_device_ids=true, to_apply=%region_17.18 | all-reduce | flops 1 | bytes 8 | tf_op jit(solution)/shard_map/psum | solution.py:198
  363.1 5.1 collective-permute-start.13
  372.6 3.6 collective-permute-start.15
  378.2 3.5 multiply_reduce_fusion.2
  381.7 42.9 %psum.68 = f32[]{:T(128)} all-reduce(f32[]{:T(128)} %get-tuple-element.294), channel_id=1, replica_groups=mesh['gz'=8,'gy'=4] {'gz','gy'}, use_global_device_ids=true, to_apply=%region_19.20 | all-reduce | flops 1 | bytes 8 | tf_op jit(solution)/shard_map/psum | solution.py:208
  428.2 32.2 %while.70 = (s32[]{:T(128)}, f32[8,52]{1,0:T(8,128)S(1)}, s32[8,16384]{1,0:T(8,128)}, f32[8,16384]{1,0:T(8,128)}, s32[]{:T(128)}, /*index=5*/s32[]{:T(128)}) while((s32[]{:T(128)}, f32[8,52]{1,0:T(8,128)S(1)}, s32[8,16384]{1,0:T(8,128)}, f32[8,16384]{1,0:T(8,128)}, s32[]{:T(128)}, /*index=5*/s32[]{:T(128)}) %tuple.199), condition=%wide.region_21.22_spmd.clone, body=%wide.region_20.21_spmd.clone.sunk | while | flops 11075586 | bytes 263357 | solution.py:132
  433.5 2.9 fusion.182
  437.5 2.9 fusion.182
  441.5 2.9 fusion.182
  445.5 2.9 fusion.182
  449.5 2.9 fusion.182
  460.9 41.1 %psum.69 = f32[640]{0:T(1024)S(1)} all-reduce(f32[640]{0:T(1024)S(1)} %add.825), channel_id=1, replica_groups=mesh['gz'=8,'gy'=4] {'gz','gy'}, use_global_device_ids=true, to_apply=%region_23.24 | all-reduce | flops 640 | bytes 5120 | tf_op jit(solution)/shard_map/psum | solution.py:190
  502.2 4.2 collective-permute-start.16
  512.0 23.2 %while.71 = (s32[]{:T(128)}, f32[8,16384]{1,0:T(8,128)S(1)}, s32[8,16384]{1,0:T(8,128)}, f32[52]{0:T(128)S(1)}, s32[]{:T(128)}, /*index=5*/s32[]{:T(128)}) while((s32[]{:T(128)}, f32[8,16384]{1,0:T(8,128)S(1)}, s32[8,16384]{1,0:T(8,128)}, f32[52]{0:T(128)S(1)}, s32[]{:T(128)}, /*index=5*/s32[]{:T(128)}) %tuple.196), condition=%wide.region_25.26_spmd.clone, body=%wide.region_24.25_spmd.clone.sunk | while | flops 11075586 | bytes 393501 | solution.py:141
  537.4 40.2 %psum.70 = f32[]{:T(128)} all-reduce(f32[]{:T(128)} %multiply_reduce_fusion.1), channel_id=1, replica_groups=mesh['gz'=8,'gy'=4] {'gz','gy'}, use_global_device_ids=true, to_apply=%region_27.28 | all-reduce | flops 1 | bytes 8 | tf_op jit(solution)/shard_map/psum | solution.py:198
  581.8 5.0 collective-permute-start.19
  590.1 3.0 collective-permute-start.21
  594.4 3.6 multiply_reduce_fusion
  598.0 43.7 %psum.71 = f32[]{:T(128)} all-reduce(f32[]{:T(128)} %get-tuple-element.282), channel_id=1, replica_groups=mesh['gz'=8,'gy'=4] {'gz','gy'}, use_global_device_ids=true, to_apply=%region_29.30 | all-reduce | flops 1 | bytes 8 | tf_op jit(solution)/shard_map/psum | solution.py:208
  (349 shorter events, 184.2 us)
Async XLA Ops:
  0.6 105.6 %copy-start = (f32[20,640]{1,0:T(8,128)S(1)}, f32[20,640]{1,0:T(8,128)}, u32[]{:S(2)}) copy-start(f32[20,640]{1,0:T(8,128)} %param.21) | copy-start | bytes 153604
  1.8 9.6 %collective-permute-start = (f32[3,32,512]{2,1,0:T(8,128)S(1)}, f32[3,32,512]{2,1,0:T(8,128)S(1)}, u32[]{:S(2)}, u32[]{:S(2)}) collective-permute-start(f32[3,32,512]{2,1,0:T(8,128)S(1)} %get-tuple-element.357), channel_id=1, source_target_pairs={{0,4},{4,8},{8,12},{12,16},{16,20},{20,24},{24,28},{1,5},{5,9},{9,... | collective-permute-start | bytes 589832 | tf_op jit(solution)/shard_map/ppermute | solution.py:25
  6.7 8.3 %collective-permute-start.1 = (f32[3,32,512]{2,1,0:T(8,128)S(1)}, f32[3,32,512]{2,1,0:T(8,128)S(1)}, u32[]{:S(2)}, u32[]{:S(2)}) collective-permute-start(f32[3,32,512]{2,1,0:T(8,128)S(1)} %get-tuple-element.356), channel_id=1, source_target_pairs={{4,0},{8,4},{12,8},{16,12},{20,16},{24,20},{28,24},{5,1},{9,5},{13... | collective-permute-start | bytes 589832 | tf_op jit(solution)/shard_map/ppermute | solution.py:28
  11.3 51.2 %copy-start.32 = (pred[32]{0:T(512)(128)(4,1)}, pred[32]{0:T(512)(128)(4,1)S(1)}, u32[]{:S(2)}) copy-start(pred[32]{0:T(512)(128)(4,1)S(1)} %get-tuple-element.373) | copy-start | bytes 100
  11.3 51.2 %copy-start.35 = (pred[32]{0:T(512)(128)(4,1)}, pred[32]{0:T(512)(128)(4,1)S(1)}, u32[]{:S(2)}) copy-start(pred[32]{0:T(512)(128)(4,1)S(1)} %get-tuple-element.374) | copy-start | bytes 100
  15.0 2.6 collective-permute-start.2
  16.3 4.9 collective-permute-start.3
  17.6 44.9 %copy-start.38 = (pred[32]{0:T(512)(128)(4,1)}, pred[32]{0:T(512)(128)(4,1)S(1)}, u32[]{:S(2)}) copy-start(pred[32]{0:T(512)(128)(4,1)S(1)} %iota_compare_fusion.16) | copy-start | bytes 100
  28.9 83.3 %copy-start.3 = (f32[8,32,512]{2,1,0:T(8,128)}, f32[8,32,512]{2,1,0:T(8,128)S(1)}, u32[]{:S(2)}) copy-start(f32[8,32,512]{2,1,0:T(8,128)S(1)} %get-tuple-element.336) | copy-start | bytes 1572868
  28.9 129.2 %copy-start.2 = (f32[8,32,512]{2,1,0:T(8,128)}, f32[8,32,512]{2,1,0:T(8,128)S(1)}, u32[]{:S(2)}) copy-start(f32[8,32,512]{2,1,0:T(8,128)S(1)} %get-tuple-element.335) | copy-start | bytes 1572868
  28.9 349.3 %copy-start.1 = (f32[8,32,512]{2,1,0:T(8,128)}, f32[8,32,512]{2,1,0:T(8,128)S(1)}, u32[]{:S(2)}) copy-start(f32[8,32,512]{2,1,0:T(8,128)S(1)} %get-tuple-element.334) | copy-start | bytes 1572868
  106.5 8.8 %collective-permute-start.4 = (f32[1,16]{1,0:T(1,128)S(1)}, f32[1,16]{1,0:T(1,128)S(1)}, u32[]{:S(2)}, u32[]{:S(2)}) collective-permute-start(f32[1,16]{1,0:T(1,128)S(1)} %get-tuple-element.369), channel_id=1, source_target_pairs={{0,4},{4,8},{8,12},{12,16},{16,20},{20,24},{24,28},{1,5},{5,9},{9,... | collective-permute-start | bytes 200 | tf_op jit(solution)/shard_map/ppermute | solution.py:25
  110.7 5.5 collective-permute-start.5
  141.9 6.6 %collective-permute-start.6 = (f32[1,32,512]{2,1,0:T(8,128)S(1)}, f32[1,32,512]{2,1,0:T(8,128)S(1)}, u32[]{:S(2)}, u32[]{:S(2)}) collective-permute-start(f32[1,32,512]{2,1,0:T(8,128)S(1)} %get-tuple-element.355), channel_id=1, source_target_pairs={{4,0},{8,4},{12,8},{16,12},{20,16},{24,20},{28,24},{5,1},{9,5},{13... | collective-permute-start | bytes 196616 | tf_op jit(solution)/shard_map/ppermute | solution.py:28
  143.2 6.8 %collective-permute-start.7 = (f32[1,32,512]{2,1,0:T(8,128)S(1)}, f32[1,32,512]{2,1,0:T(8,128)S(1)}, u32[]{:S(2)}, u32[]{:S(2)}) collective-permute-start(f32[1,32,512]{2,1,0:T(8,128)S(1)} %get-tuple-element.354), channel_id=1, source_target_pairs={{0,4},{4,8},{8,12},{12,16},{16,20},{20,24},{24,28},{1,5},{5,9},{9,... | collective-permute-start | bytes 196616 | tf_op jit(solution)/shard_map/ppermute | solution.py:25
  151.3 4.9 collective-permute-start.8
  152.6 4.2 collective-permute-start.9
  209.0 32.4 %copy-start.33 = (pred[32]{0:T(512)(128)(4,1)S(1)}, pred[32]{0:T(512)(128)(4,1)}, u32[]{:S(2)}) copy-start(pred[32]{0:T(512)(128)(4,1)} %copy-done.32) | copy-start | bytes 100
  209.0 32.4 %copy-start.36 = (pred[32]{0:T(512)(128)(4,1)S(1)}, pred[32]{0:T(512)(128)(4,1)}, u32[]{:S(2)}) copy-start(pred[32]{0:T(512)(128)(4,1)} %copy-done.35) | copy-start | bytes 100
  209.0 32.4 %copy-start.39 = (pred[32]{0:T(512)(128)(4,1)S(1)}, pred[32]{0:T(512)(128)(4,1)}, u32[]{:S(2)}) copy-start(pred[32]{0:T(512)(128)(4,1)} %copy-done.38) | copy-start | bytes 100
  209.0 79.9 %copy-start.18 = (f32[1,32,512]{2,1,0:T(8,128)S(1)}, f32[1,32,512]{2,1,0:T(8,128)}, u32[]{:S(2)}) copy-start(f32[1,32,512]{2,1,0:T(8,128)} %copy-done.17) | copy-start | bytes 196612
  209.0 79.9 %copy-start.30 = (f32[1,32,512]{2,1,0:T(8,128)S(1)}, f32[1,32,512]{2,1,0:T(8,128)}, u32[]{:S(2)}) copy-start(f32[1,32,512]{2,1,0:T(8,128)} %get-tuple-element.330) | copy-start | bytes 196612
  209.1 79.9 %copy-start.13 = (f32[1,32,512]{2,1,0:T(8,128)S(1)}, f32[1,32,512]{2,1,0:T(8,128)}, u32[]{:S(2)}) copy-start(f32[1,32,512]{2,1,0:T(8,128)} %copy-done.12) | copy-start | bytes 196612
  283.4 7.0 %collective-permute-start.10 = (f32[1,16]{1,0:T(1,128)S(1)}, f32[1,16]{1,0:T(1,128)S(1)}, u32[]{:S(2)}, u32[]{:S(2)}) collective-permute-start(f32[1,16]{1,0:T(1,128)S(1)} %get-tuple-element.364), channel_id=1, source_target_pairs={{0,4},{4,8},{8,12},{12,16},{16,20},{20,24},{24,28},{1,5},{5,9},{9,... | collective-permute-start | bytes 200 | tf_op jit(solution)/shard_map/ppermute | solution.py:25
  287.6 5.5 collective-permute-start.11
  316.4 42.5 %copy-start.5 = (f32[8,16384]{1,0:T(8,128)}, f32[8,16384]{1,0:T(8,128)S(1)}, u32[]{:S(2)}) copy-start(f32[8,16384]{1,0:T(8,128)S(1)} %get-tuple-element.167) | copy-start | bytes 1572868
  361.8 6.7 %collective-permute-start.12 = (f32[1,32,512]{2,1,0:T(8,128)S(1)}, f32[1,32,512]{2,1,0:T(8,128)S(1)}, u32[]{:S(2)}, u32[]{:S(2)}) collective-permute-start(f32[1,32,512]{2,1,0:T(8,128)S(1)} %get-tuple-element.353), channel_id=1, source_target_pairs={{4,0},{8,4},{12,8},{16,12},{20,16},{24,20},{28,24},{5,1},{9,5},{13... | collective-permute-start | bytes 196616 | tf_op jit(solution)/shard_map/ppermute | solution.py:28
  363.1 6.9 %collective-permute-start.13 = (f32[1,32,512]{2,1,0:T(8,128)S(1)}, f32[1,32,512]{2,1,0:T(8,128)S(1)}, u32[]{:S(2)}, u32[]{:S(2)}) collective-permute-start(f32[1,32,512]{2,1,0:T(8,128)S(1)} %get-tuple-element.352), channel_id=1, source_target_pairs={{0,4},{4,8},{8,12},{12,16},{16,20},{20,24},{24,28},{1,5},{5,9},{9,... | collective-permute-start | bytes 196616 | tf_op jit(solution)/shard_map/ppermute | solution.py:25
  371.4 4.9 collective-permute-start.14
  372.6 4.2 collective-permute-start.15
  428.2 32.6 %copy-start.34 = (pred[32]{0:T(512)(128)(4,1)S(1)}, pred[32]{0:T(512)(128)(4,1)}, u32[]{:S(2)}) copy-start(pred[32]{0:T(512)(128)(4,1)} %copy-done.32) | copy-start | bytes 100
  428.2 32.6 %copy-start.37 = (pred[32]{0:T(512)(128)(4,1)S(1)}, pred[32]{0:T(512)(128)(4,1)}, u32[]{:S(2)}) copy-start(pred[32]{0:T(512)(128)(4,1)} %copy-done.35) | copy-start | bytes 100
  428.2 32.6 %copy-start.40 = (pred[32]{0:T(512)(128)(4,1)S(1)}, pred[32]{0:T(512)(128)(4,1)}, u32[]{:S(2)}) copy-start(pred[32]{0:T(512)(128)(4,1)} %copy-done.38) | copy-start | bytes 100
  428.2 79.5 %copy-start.19 = (f32[1,32,512]{2,1,0:T(8,128)S(1)}, f32[1,32,512]{2,1,0:T(8,128)}, u32[]{:S(2)}) copy-start(f32[1,32,512]{2,1,0:T(8,128)} %copy-done.17) | copy-start | bytes 196612
  428.2 80.4 %copy-start.14 = (f32[1,32,512]{2,1,0:T(8,128)S(1)}, f32[1,32,512]{2,1,0:T(8,128)}, u32[]{:S(2)}) copy-start(f32[1,32,512]{2,1,0:T(8,128)} %copy-done.12) | copy-start | bytes 196612
  428.2 80.4 %copy-start.16 = (f32[1,32,512]{2,1,0:T(8,128)S(1)}, f32[1,32,512]{2,1,0:T(8,128)}, u32[]{:S(2)}) copy-start(f32[1,32,512]{2,1,0:T(8,128)} %copy-done.15) | copy-start | bytes 196612
  428.2 80.4 %copy-start.25 = (f32[1,32,512]{2,1,0:T(8,128)S(1)}, f32[1,32,512]{2,1,0:T(8,128)}, u32[]{:S(2)}) copy-start(f32[1,32,512]{2,1,0:T(8,128)} %get-tuple-element.316) | copy-start | bytes 196612
  428.2 80.4 %copy-start.26 = (f32[1,32,512]{2,1,0:T(8,128)S(1)}, f32[1,32,512]{2,1,0:T(8,128)}, u32[]{:S(2)}) copy-start(f32[1,32,512]{2,1,0:T(8,128)} %get-tuple-element.319) | copy-start | bytes 196612
  428.2 80.4 %copy-start.27 = (f32[1,32,512]{2,1,0:T(8,128)S(1)}, f32[1,32,512]{2,1,0:T(8,128)}, u32[]{:S(2)}) copy-start(f32[1,32,512]{2,1,0:T(8,128)} %get-tuple-element.320) | copy-start | bytes 196612
  428.2 80.4 %copy-start.28 = (f32[1,32,512]{2,1,0:T(8,128)S(1)}, f32[1,32,512]{2,1,0:T(8,128)}, u32[]{:S(2)}) copy-start(f32[1,32,512]{2,1,0:T(8,128)} %get-tuple-element.321) | copy-start | bytes 196612
  428.2 80.4 %copy-start.29 = (f32[1,32,512]{2,1,0:T(8,128)S(1)}, f32[1,32,512]{2,1,0:T(8,128)}, u32[]{:S(2)}) copy-start(f32[1,32,512]{2,1,0:T(8,128)} %get-tuple-element.322) | copy-start | bytes 196612
  502.2 7.7 %collective-permute-start.16 = (f32[1,16]{1,0:T(1,128)S(1)}, f32[1,16]{1,0:T(1,128)S(1)}, u32[]{:S(2)}, u32[]{:S(2)}) collective-permute-start(f32[1,16]{1,0:T(1,128)S(1)} %get-tuple-element.359), channel_id=1, source_target_pairs={{0,4},{4,8},{8,12},{12,16},{16,20},{20,24},{24,28},{1,5},{5,9},{9,... | collective-permute-start | bytes 200 | tf_op jit(solution)/shard_map/ppermute | solution.py:25
  506.4 5.5 collective-permute-start.17
  535.2 42.4 %copy-start.4 = (f32[8,16384]{1,0:T(8,128)}, f32[8,16384]{1,0:T(8,128)S(1)}, u32[]{:S(2)}) copy-start(f32[8,16384]{1,0:T(8,128)S(1)} %get-tuple-element.169) | copy-start | bytes 1572868
  580.5 6.6 %collective-permute-start.18 = (f32[1,32,512]{2,1,0:T(8,128)S(1)}, f32[1,32,512]{2,1,0:T(8,128)S(1)}, u32[]{:S(2)}, u32[]{:S(2)}) collective-permute-start(f32[1,32,512]{2,1,0:T(8,128)S(1)} %get-tuple-element.351), channel_id=1, source_target_pairs={{4,0},{8,4},{12,8},{16,12},{20,16},{24,20},{28,24},{5,1},{9,5},{13... | collective-permute-start | bytes 196616 | tf_op jit(solution)/shard_map/ppermute | solution.py:28
  581.8 6.9 %collective-permute-start.19 = (f32[1,32,512]{2,1,0:T(8,128)S(1)}, f32[1,32,512]{2,1,0:T(8,128)S(1)}, u32[]{:S(2)}, u32[]{:S(2)}) collective-permute-start(f32[1,32,512]{2,1,0:T(8,128)S(1)} %get-tuple-element.350), channel_id=1, source_target_pairs={{0,4},{4,8},{8,12},{12,16},{16,20},{20,24},{24,28},{1,5},{5,9},{9,... | collective-permute-start | bytes 196616 | tf_op jit(solution)/shard_map/ppermute | solution.py:25
  588.8 4.3 collective-permute-start.20
  590.1 3.9 collective-permute-start.21
  (15 other events, 38.2 us)
where the time goes:
time: 651 us; the launch traced here: 646 us
  blocking collectives  337 us (52%)
  matrix products  100 us (15%)
  local copies, waits for them, and re-layouts  74.7 us (11%)
  starting transfers between devices  58.5 us (9%)
  other arithmetic  45.7 us (7%)
  waiting for transfers between devices  20.2 us (3%)
  between operations  8.19 us (1%)
    psum x3, blocking collectives, precondition(): totals = lax.psum(spread, ('gz', 'gy'))  126 us
    psum x3, blocking collectives, precondition(): product = lax.psum(jnp.sum(residual * direction), ('gz', 'gy'))  124 us
    psum x2, blocking collectives, on_device(): alpha = product / lax.psum(jnp.sum(search * image), ('gz', 'gy'))  86.6 us
    dot_general x24, matrix products, one_plane(): return jnp.dot(onehot, plane_values, precision=highest)  68.6 us
    dynamic_slice x48, local copies, waits for them, and re-layouts, region_sums(): return jnp.sum(lax.map(one_plane, (flat_bins, flat_field)), axis=0)  52.6 us
    ppermute x11, starting transfers between devices, with_halo(): lax.ppermute(lax.slice_in_dim(block, block.shape[dim] - width, None, axis...  44.1 us
    dot_general x24, matrix products, one_plane(): return jnp.dot(window, onehot, precision=highest)  31.3 us
    ppermute x11, starting transfers between devices, with_halo(): lax.ppermute(lax.slice_in_dim(block, 0, width, axis=dim), axis, backward)  14.4 us
  transfers between devices with their start and end apart: 22, of which 14 were waited for; matrix products, arithmetic and copies ran while one was open for 2% of the time, Pallas kernels for 0%

commit v1 on v0

v1 whole, which is shorter than its diff:
```python
from functools import partial

import jax
import jax.numpy as jnp
from jax import lax
from jax.experimental import pallas as pl
from jax.experimental.pallas import tpu as pltpu
from jax.sharding import PartitionSpec as P

S_DEV = 4
B_DEV = 16
SPAN = S_DEV + B_DEV
LANES = 128
GROUPS = 4
CODES = GROUPS * B_DEV
REGIONS = S_DEV + 3 * B_DEV
SCALARS = 96
DEPTH = 3

surface_tension = 0.5
shift_term = 0.05
gas_drop = 0.75
norm_floor = 0.25
highest = lax.Precision.HIGHEST
f32 = jnp.float32
i32 = jnp.int32
bf16 = jnp.bfloat16


def iota(shape, dim):
    return lax.broadcasted_iota(i32, shape, dim)


def up_rows(field):
    return pltpu.roll(field, field.shape[0] - 1, 0)


def down_rows(field):
    return pltpu.roll(field, 1, 0)


def next_x(field):
    return pltpu.roll(field, field.shape[1] - 1, 1)


def prev_x(field):
    return pltpu.roll(field, 1, 1)


def total(field):
    rows, width = field.shape
    folded = field[:, :LANES]
    for start in range(LANES, width, LANES):
        folded = folded + field[:, start : start + LANES]
    return jnp.sum(folded.reshape(rows // 8, 8, LANES), axis=0)


def octet_sums(values, code):
    group = code // B_DEV
    inner = code % B_DEV
    spread = jnp.concatenate([jnp.where(group == g, values, 0.0) for g in range(GROUPS)], axis=0)
    high = spread.astype(bf16)
    low = (spread - high.astype(f32)).astype(bf16)
    left = jnp.concatenate([high, low], axis=0)
    right = jnp.concatenate(
        [jnp.where(inner == i, 1.0, 0.0) for i in range(B_DEV)], axis=0
    ).astype(bf16)
    return lax.dot_general(left, right, (((1,), (1,)), ((), ())), preferred_element_type=f32)


def region_row(value_ref, code_ref):
    planes, rows, _ = value_ref.shape
    octets = rows // 8

    def step(index, acc):
        plane = index // octets
        start = pl.multiple_of((index % octets) * 8, 8)
        return acc + octet_sums(value_ref[plane, pl.ds(start, 8), :], code_ref[plane, pl.ds(start, 8), :])

    acc = lax.fori_loop(
        0, planes * octets, step, jnp.zeros((2 * GROUPS * 8, B_DEV * 8), f32), unroll=4
    )
    shape = acc.shape
    kept = jnp.where(iota(shape, 0) % 8 == iota(shape, 1) % 8, acc, 0.0)
    folded = jnp.sum(kept.reshape(2 * GROUPS, 8, LANES), axis=1)
    pick = jnp.where(iota((LANES, LANES), 0) // 8 == iota((LANES, LANES), 1) % B_DEV, 1.0, 0.0)
    spread = jnp.dot(folded, pick, precision=highest, preferred_element_type=f32)
    shape = spread.shape
    lane = iota(shape, 1)
    mine = (iota(shape, 0) % GROUPS == lane // B_DEV) & (lane < CODES)
    return jnp.sum(jnp.where(mine, spread, 0.0), axis=0, keepdims=True)


def scalar_row(scalars):
    lane = iota((1, LANES), 1)
    row = jnp.zeros((1, LANES), f32)
    for index, value in enumerate(scalars):
        row = jnp.where(lane == SCALARS + index, value, row)
    return row


def lane_of(row, index):
    return jnp.sum(jnp.where(iota(row.shape, 1) == SCALARS + index, row, 0.0))


def lookup(table, index):
    rows, width = index.shape
    wide = jnp.broadcast_to(table, (rows, LANES))
    return jnp.concatenate(
        [
            jnp.take_along_axis(wide, index[:, start : start + LANES], axis=1)
            for start in range(0, width, LANES)
        ],
        axis=1,
    )


def start_all(copies):
    for copy in copies:
        copy.start()


def wait_all(copies):
    for copy in copies:
        copy.wait()


def send_coarse(row, dest_ref, send_ref):
    wide = jnp.broadcast_to(row, (8, LANES))

    def step(region, acc):
        lane = jnp.where(region < S_DEV, region, region + B_DEV - S_DEV)
        factor = jnp.take_along_axis(wide, jnp.full((8, LANES), lane, i32), axis=1)[0:1, :]
        factor = jnp.concatenate([factor, factor], axis=1)
        return acc + factor * dest_ref[region]

    send_ref[...] = lax.fori_loop(0, REGIONS, step, jnp.zeros(send_ref.shape, f32), unroll=4)


def destinations_kernel(columns, pair_ref, own_ref, near_ref, far_ref, dest_ref, wide_ref):
    devices = own_ref.shape[1]
    even_z = pair_ref[0] == 0
    wide_ref[...] = jnp.zeros(wide_ref.shape, f32)
    low_start = pl.multiple_of(jnp.where(even_z, 2 * B_DEV, 0), B_DEV) + S_DEV
    high_start = pl.multiple_of(jnp.where(even_z, 0, 2 * B_DEV), B_DEV) + S_DEV
    wide_ref[0:S_DEV, :, 0:SPAN] = own_ref[0:S_DEV]
    wide_ref[S_DEV + B_DEV : S_DEV + 2 * B_DEV, :, 0:SPAN] = own_ref[S_DEV:SPAN]
    wide_ref[pl.ds(low_start, B_DEV), :, 0:SPAN] = near_ref[...]
    wide_ref[pl.ds(high_start, B_DEV), :, 0:SPAN] = far_ref[...]
    lane = iota((devices, LANES), 1)

    def place(base, shift, first, count):
        moved = pltpu.roll(base, shift, 1) if shift else base
        return jnp.where((lane >= first) & (lane < first + count), moved, 0.0)

    def from_device(field, step):
        return pltpu.roll(field, (-step) % devices, 0) if step % devices else field

    def one(region, carry):
        base = wide_ref[region]
        bubbles = B_DEV - S_DEV
        table = place(base, 0, 0, S_DEV) + place(base, B_DEV + bubbles, 2 * B_DEV, B_DEV)
        table = table + from_device(
            place(base, S_DEV, S_DEV, S_DEV) + place(base, 2 * B_DEV + bubbles, 3 * B_DEV, B_DEV), columns
        )
        table = table + from_device(
            place(base, 2 * S_DEV, 2 * S_DEV, S_DEV) + place(base, bubbles, B_DEV, B_DEV), -columns
        )
        table = table + from_device(place(base, 3 * S_DEV, 3 * S_DEV, S_DEV), 1)
        table = table + from_device(place(base, 3 * B_DEV + bubbles, 4 * B_DEV, B_DEV), 2 * columns)
        table = table + from_device(place(base, 4 * B_DEV + bubbles, 5 * B_DEV, B_DEV), -2 * columns)
        own_codes = jnp.where((lane < S_DEV) | ((lane >= B_DEV) & (lane < CODES)), table, 0.0)
        dest_ref[region] = jnp.concatenate([table, from_device(own_codes, -1)], axis=1)
        return carry

    lax.fori_loop(0, REGIONS, one, 0)


def write_edges(even_z, even_y, value_ref, z_refs, y_refs, convert=lambda value: value):
    planes, rows, _ = value_ref.shape
    z_refs[0][...] = convert(value_ref[jnp.where(even_z, planes - 1, 0)])
    z_refs[1][...] = convert(value_ref[jnp.where(even_z, 0, planes - 1)])
    for plane in range(planes):
        first = convert(value_ref[plane, 0:1, :])
        last = convert(value_ref[plane, rows - 1 : rows, :])
        y_refs[0][plane : plane + 1, :] = jnp.where(even_y, last, first)
        y_refs[1][plane : plane + 1, :] = jnp.where(even_y, first, last)


def setup_kernel(
    edge_ref, z0_in, z1_in, y0_in, y1_in, k0_in, k1_in, frac_hbm, source_hbm, label_hbm, sub_hbm, dest_hbm,
    ez0_ref, ez1_ref, ey0_ref, ey1_ref, send_ref,
    code_hbm, r_hbm, b_hbm, cz_hbm, cyp_hbm, cym_hbm, cxp_hbm, cxm_hbm, diag_hbm, inv_hbm, mult_hbm,
    frac_ref, source_ref, label_ref, sub_ref, dest_ref,
    code_ref, r_ref, b_ref, cz_ref, cyp_ref, cym_ref, cxp_ref, cxm_ref, diag_ref, inv_ref, mult_ref,
    deep_ref, nz_ref, flat_ref, kap_ref, fz_ref, work_ref, in_sems, out_sems,
):
    planes, rows, width = frac_ref.shape
    tall = rows + 8
    first_z, last_z, first_y, last_y = (edge_ref[i] == 1 for i in range(4))
    base, stride, sub_base = edge_ref[4], edge_ref[5], edge_ref[6]
    even_z, even_y = edge_ref[7] == 0, edge_ref[8] == 0
    pairs = [(frac_hbm, frac_ref), (label_hbm, label_ref), (sub_hbm, sub_ref), (source_hbm, source_ref), (dest_hbm, dest_ref)]
    reads = [pltpu.make_async_copy(a, b, in_sems.at[i]) for i, (a, b) in enumerate(pairs)]
    start_all(reads)
    row = iota((tall, width), 0)
    lane = iota((tall, width), 1)
    inside_y = ((row < rows) | ((row < rows + 4) & jnp.logical_not(last_y))) | (
        (row >= rows + 4) & jnp.logical_not(first_y)
    )
    first_plane = jnp.where(first_z, 0, -planes)
    last_plane = jnp.where(last_z, planes, 2 * planes)

    def right_of(field):
        return jnp.where(lane[: field.shape[0]] == width - 1, 0.0, next_x(field))

    def left_of(field):
        return jnp.where(lane[: field.shape[0]] == 0, 0.0, prev_x(field))

    deep_ref[:, rows:tall, :] = jnp.zeros((planes + 2 * DEPTH, 8, width), f32)
    near_z = jnp.where(even_z, planes + DEPTH, 0)
    far_z = jnp.where(even_z, 0, planes + DEPTH)
    deep_ref[pl.ds(near_z, DEPTH), 0:rows, :] = z0_in[...]
    deep_ref[pl.ds(far_z, DEPTH), 0:rows, :] = z1_in[...]
    high, low = slice(rows, rows + DEPTH), slice(tall - DEPTH, tall)

    def fill_rows(first, second):
        deep_ref[DEPTH : planes + DEPTH, first, :] = y0_in[...]
        deep_ref[DEPTH : planes + DEPTH, second, :] = y1_in[...]
        deep_ref[pl.ds(near_z, DEPTH), first, :] = k0_in[0]
        deep_ref[pl.ds(near_z, DEPTH), second, :] = k0_in[1]
        deep_ref[pl.ds(far_z, DEPTH), first, :] = k1_in[0]
        deep_ref[pl.ds(far_z, DEPTH), second, :] = k1_in[1]

    @pl.when(even_y)
    def _():
        fill_rows(high, low)

    @pl.when(jnp.logical_not(even_y))
    def _():
        fill_rows(low, high)

    reads[0].wait()
    deep_ref[DEPTH : planes + DEPTH, 0:rows, :] = frac_ref[...]

    def mask_plane(index, carry):
        keep = (index - DEPTH >= first_plane) & (index - DEPTH < last_plane)
        deep_ref[index] = jnp.where(inside_y & keep, deep_ref[index], 0.0)
        return carry

    lax.fori_loop(0, planes + 2 * DEPTH, mask_plane, 0)

    def normal_plane(index, carry):
        keep = (index - 2 >= first_plane) & (index - 2 < last_plane)
        here = deep_ref[index + 1]
        gz = 0.5 * (deep_ref[index + 2] - deep_ref[index])
        gy = 0.5 * (up_rows(here) - down_rows(here))
        gx = 0.5 * (right_of(here) - left_of(here))
        length = jnp.maximum(jnp.sqrt(gz * gz + gy * gy + gx * gx), norm_floor)
        scale = jnp.where(inside_y & keep, 1.0 / length, 0.0)
        ny = gy * scale
        nx = gx * scale
        nz_ref[index] = gz * scale
        flat_ref[index] = 0.5 * (up_rows(ny) - down_rows(ny)) + 0.5 * (right_of(nx) - left_of(nx))
        return carry

    lax.fori_loop(0, planes + 4, normal_plane, 0)

    def kappa_plane(index, carry):
        keep = (index - 1 >= first_plane) & (index - 1 < last_plane)
        value = -(0.5 * (nz_ref[index + 2] - nz_ref[index]) + flat_ref[index + 1])
        kap_ref[index] = jnp.where(inside_y & keep, value, 0.0)
        return carry

    lax.fori_loop(0, planes + 2, kappa_plane, 0)
    mid = pl.ds(0, rows)

    def z_face(index, carry):
        f_low = deep_ref[index + 2, mid, :]
        f_high = deep_ref[index + 3, mid, :]
        coef = 2.0 / ((1.0 - gas_drop * f_low) + (1.0 - gas_drop * f_high))
        cz_ref[index] = coef
        mean = 0.5 * (kap_ref[index, mid, :] + kap_ref[index + 1, mid, :])
        fz_ref[index] = coef * mean * (f_high - f_low)
        return carry

    lax.fori_loop(0, planes + 1, z_face, 0)
    row_mid = row[:rows]
    lane_mid = lane[:rows]
    wait_all(reads[1:])

    def assemble_plane(plane, carry):
        inv_before, g_before = carry
        f = deep_ref[plane + 3]
        k = kap_ref[plane + 1]
        d = 1.0 - gas_drop * f
        f_up = up_rows(f)
        cy = 2.0 / (d + (1.0 - gas_drop * f_up))
        fy = cy * (0.5 * (k + up_rows(k))) * (f_up - f)
        cyp, cym = cy[:rows], down_rows(cy)[:rows]
        sum_y = fy[:rows] - down_rows(fy)[:rows]
        f, k, d = f[:rows], k[:rows], d[:rows]
        f_right = right_of(f)
        cxp = 2.0 / (d + (1.0 - gas_drop * f_right))
        fx = cxp * (0.5 * (k + right_of(k))) * (f_right - f)
        outer = 2.0 / (d + 1.0)
        cxm = jnp.where(lane_mid == 0, outer, prev_x(cxp))
        fx_before = jnp.where(lane_mid == 0, outer * (0.5 * k) * f, prev_x(fx))
        terms = fz_ref[plane + 1] - fz_ref[plane] + sum_y + (fx - fx_before)
        rhs = source_ref[plane] - surface_tension * terms
        down = cz_ref[plane]
        diagonal = shift_term + (cz_ref[plane + 1] + down + cyp + cym + cxp + cxm)
        mult = down * inv_before
        inv = 1.0 / (diagonal - mult * down)
        g = rhs + mult * g_before
        r_ref[plane] = rhs
        diag_ref[plane] = diagonal
        mult_ref[plane] = mult
        inv_ref[plane] = inv
        work_ref[plane] = g
        cyp_ref[plane] = jnp.where((row_mid == rows - 1) & last_y, 0.0, cyp)
        cym_ref[plane] = jnp.where((row_mid == 0) & first_y, 0.0, cym)
        cxp_ref[plane] = jnp.where(lane_mid == width - 1, 0.0, cxp)
        cxm_ref[plane] = jnp.where(lane_mid == 0, 0.0, cxm)
        label = label_ref[plane]
        offset = label - base
        below = offset < 0
        above = offset >= stride
        group = jnp.where(below, 1, jnp.where(above, 3, 2))
        inner = jnp.where(below, offset + stride, jnp.where(above, offset - stride, offset))
        code = jnp.where(label >= 0, group * B_DEV + inner, sub_ref[plane] - sub_base)
        code_ref[plane] = code & (CODES - 1)
        return (inv, g)

    blank = jnp.zeros((rows, width), f32)
    lax.fori_loop(0, planes, assemble_plane, (blank, blank))

    def backward(step, after):
        plane = planes - 1 - step
        value = (work_ref[plane] + cz_ref[plane + 1] * after) * inv_ref[plane]
        b_ref[plane] = value
        return value

    lax.fori_loop(0, planes, backward, blank)
    cz_ref[0] = jnp.where(first_z, 0.0, cz_ref[0])
    cz_ref[planes] = jnp.where(last_z, 0.0, cz_ref[planes])
    pairs = [
        (code_ref, code_hbm), (r_ref, r_hbm), (b_ref, b_hbm), (cz_ref, cz_hbm), (cyp_ref, cyp_hbm), (cym_ref, cym_hbm),
        (cxp_ref, cxp_hbm), (cxm_ref, cxm_hbm), (diag_ref, diag_hbm), (inv_ref, inv_hbm), (mult_ref, mult_hbm),
    ]
    writes = [pltpu.make_async_copy(a, b, out_sems.at[i]) for i, (a, b) in enumerate(pairs)]
    start_all(writes)
    write_edges(even_z, even_y, b_ref, [ez0_ref.at[0], ez1_ref.at[0]], [ey0_ref.at[0], ey1_ref.at[0]])
    write_edges(
        even_z, even_y, code_ref, [ez0_ref.at[1], ez1_ref.at[1]], [ey0_ref.at[1], ey1_ref.at[1]],
        convert=lambda value: value.astype(f32),
    )
    send_coarse(region_row(r_ref, code_ref), dest_ref, send_ref)
    wait_all(writes)


def scalars_of(sums):
    alphas, betas, curves = [], [None], []
    for step, row in enumerate(sums):
        gamma = lane_of(row, 0)
        if step == 0:
            curve = lane_of(row, 1)
        else:
            beta = gamma / lane_of(sums[step - 1], 0)
            betas.append(beta)
            curve = lane_of(row, 1) + beta * (lane_of(row, 2) + beta * curves[-1])
        curves.append(curve)
        alphas.append(gamma / curve)
    return alphas, betas


def step_kernel(stage, *refs):
    refs = list(refs)

    def take(count):
        out = refs[:count]
        del refs[:count]
        return out

    (edge_ref,) = take(1)
    parts = take(stage + 1)
    halos = [take(4) for _ in range(stage + 1)]
    last = stage == 2
    states = (("b", "r"), ("b", "u0", "r", "w0", "z0"), ("b", "u0", "u1", "r", "w0", "w1", "z0", "z1"))[stage]
    first_names = ("code", "b") + tuple(name for name in states if name[0] == "u")
    later_names = tuple(name for name in states if name not in first_names)
    matrix_names = ("cz", "cyp", "cym", "cxp", "cxm", "diag") + (() if last else ("inv", "mult", "dest"))
    names = first_names + matrix_names[:6] + later_names + matrix_names[6:]
    sources = dict(zip(names, take(len(names))))
    out_names = (("z", "w", "u"), ("z", "w", "u", "bn", "rn"), ("z", "w", "p", "s", "rn"))[stage]
    if not last:
        edges_z, edges_y = take(2), take(2)
    (send_ref,) = take(1)
    sinks = dict(zip(out_names, take(len(out_names))))
    held = dict(zip(names, take(len(names))))
    pad_ref, side_ref = take(2)
    made = {"z": pad_ref.at[pl.ds(1, pad_ref.shape[0] - 2)]}
    for name in out_names[1:]:
        (made[name],) = take(1)
    if not last:
        (work_ref,) = take(1)
    in_sems, out_sems = take(2)

    reads = {name: pltpu.make_async_copy(sources[name], held[name], in_sems.at[i]) for i, name in enumerate(names)}
    start_all(reads.values())
    writes = {name: pltpu.make_async_copy(made[name], sinks[name], out_sems.at[i]) for i, name in enumerate(out_names)}
    code_ref = held["code"]
    planes, rows, width = code_ref.shape
    even_z, even_y = edge_ref[7] == 0, edge_ref[8] == 0

    sums = [jnp.sum(part[...], axis=0, keepdims=True) for part in parts]
    alphas, betas = scalars_of([row[:, :LANES] for row in sums[1:]])
    table = sums[0]
    if stage >= 1:
        table = table - alphas[0] * sums[1]
    if stage == 2:
        table = table - alphas[1] * (sums[2] + betas[1] * sums[1])
    near, side = table[:, :LANES], table[:, LANES:]

    def combine(values):
        out = values[0]
        if stage >= 1:
            out = out - alphas[0] * values[1]
        if stage == 2:
            out = out - alphas[1] * (values[2] + betas[1] * values[1])
        return out

    for slot in range(2):
        upper = even_z if slot == 0 else jnp.logical_not(even_z)
        index = halos[0][slot][1].astype(i32)
        high = jnp.where(index < B_DEV, index + S_DEV, index + B_DEV)
        low = jnp.where(
            index < B_DEV, index + 2 * S_DEV, jnp.where(index < 2 * B_DEV, index + 4 * B_DEV, index - B_DEV)
        )
        block = combine([halos[0][slot][0]] + [halo[slot][...] for halo in halos[1:]])
        pad_ref[jnp.where(upper, planes + 1, 0)] = block + lookup(near, jnp.where(upper, high, low))
        upper = even_y if slot == 0 else jnp.logical_not(even_y)
        index = halos[0][2 + slot][1].astype(i32)
        block = combine([halos[0][2 + slot][0]] + [halo[2 + slot][...] for halo in halos[1:]])
        found = jnp.where(
            upper, lookup(near, (index & (B_DEV - 1)) + 3 * S_DEV), lookup(side, index)
        )
        side_ref[jnp.where(upper, 1, 0)] = block + found

    for name in first_names:
        reads[name].wait()

    def direction(plane, carry):
        block = held["b"][plane]
        if stage == 1:
            block = block - alphas[0] * held["u0"][plane]
            made["bn"][plane] = block
        if stage == 2:
            block = block - alphas[1] * (held["u1"][plane] + betas[1] * held["u0"][plane])
        pad_ref[plane + 1] = block + lookup(near, code_ref[plane])
        return carry

    lax.fori_loop(0, planes, direction, 0)
    writes["z"].start()
    for name in names:
        if name not in first_names and name != "dest":
            reads[name].wait()
    row = iota((rows, width), 0)

    def image_plane(plane, carry):
        sums, before = carry
        here = pad_ref[plane + 1]
        north = jnp.where(row == rows - 1, side_ref[1, pl.ds(plane, 1), :], up_rows(here))
        south = jnp.where(row == 0, side_ref[0, pl.ds(plane, 1), :], down_rows(here))
        image = held["diag"][plane] * here - (
            held["cz"][plane + 1] * pad_ref[plane + 2]
            + held["cz"][plane] * pad_ref[plane]
            + held["cyp"][plane] * north
            + held["cym"][plane] * south
            + held["cxp"][plane] * next_x(here)
            + held["cxm"][plane] * prev_x(here)
        )
        made["w"][plane] = image
        residual = held["r"][plane]
        if stage == 1:
            old_z, old_w = held["z0"][plane], held["w0"][plane]
            residual = residual - alphas[0] * old_w
            made["rn"][plane] = residual
        if stage == 2:
            old_z = held["z1"][plane] + betas[1] * held["z0"][plane]
            old_w = held["w1"][plane] + betas[1] * held["w0"][plane]
            made["p"][plane] = old_z
            made["s"][plane] = old_w
            residual = residual - alphas[1] * old_w
            made["rn"][plane] = residual
        found = [total(residual * here), total(here * image)]
        if stage >= 1:
            found.append(total(here * old_w + old_z * image))
        if not last:
            before = image + held["mult"][plane] * before
            work_ref[plane] = before
        return tuple(old + new for old, new in zip(sums, found)), before

    blank = jnp.zeros((8, LANES), f32)
    empty = jnp.zeros((rows, width), f32)
    dots, _ = lax.fori_loop(
        0, planes, image_plane, ((blank,) * (3 if stage else 2), blank if last else empty)
    )
    for name in out_names[1:]:
        if name != "u":
            writes[name].start()
    row = scalar_row([jnp.sum(value) for value in dots])
    if last:
        send_ref[...] = jnp.broadcast_to(row, send_ref.shape)
    else:

        def backward(step, after):
            plane = planes - 1 - step
            value = (work_ref[plane] + held["cz"][plane + 1] * after) * held["inv"][plane]
            made["u"][plane] = value
            return value

        lax.fori_loop(0, planes, backward, empty)
        writes["u"].start()
        write_edges(even_z, even_y, made["u"], edges_z, edges_y)
        reads["dest"].wait()
        send_coarse(region_row(made["w"], code_ref), held["dest"], send_ref)
        send_ref[:, :LANES] = send_ref[:, :LANES] + row
    wait_all(writes.values())


def final_kernel(
    d0_ref, d1_ref, d2_ref, r_hbm, w_hbm, s_hbm, z0_hbm, p_hbm, z_hbm, x_out, r_out,
    r_ref, w_ref, s_ref, z0_ref, p_ref, z_ref, x_ref, in_sems, out_sems,
):
    pairs = [(z0_hbm, z0_ref), (p_hbm, p_ref), (z_hbm, z_ref), (r_hbm, r_ref), (w_hbm, w_ref), (s_hbm, s_ref)]
    reads = [pltpu.make_async_copy(a, b, in_sems.at[i]) for i, (a, b) in enumerate(pairs)]
    start_all(reads)
    sums = [jnp.sum(ref[:, :LANES], axis=0, keepdims=True) for ref in (d0_ref, d1_ref, d2_ref)]
    alphas, betas = scalars_of(sums)
    mixed = alphas[2] * betas[2]
    along = alphas[1] + mixed
    wait_all(reads[:3])
    x_ref[...] = alphas[0] * z0_ref[...] + along * p_ref[...] + alphas[2] * z_ref[...]
    x_write = pltpu.make_async_copy(x_ref, x_out, out_sems.at[0])
    x_write.start()
    wait_all(reads[3:])
    r_ref[...] = r_ref[...] - (alphas[2] * w_ref[...] + mixed * s_ref[...])
    r_write = pltpu.make_async_copy(r_ref, r_out, out_sems.at[1])
    r_write.start()
    x_write.wait()
    r_write.wait()


def in_hbm(shape):
    return ("hbm", shape)


def call(kernel, outs, scratch, args, name):
    spaces = {"smem": pltpu.SMEM, "vmem": pltpu.VMEM, "hbm": pltpu.HBM}

    def specs(items):
        return [pl.BlockSpec(memory_space=spaces[space]) for space, _ in items]

    return pl.pallas_call(
        kernel,
        out_shape=[shape for _, shape in outs],
        in_specs=specs(args),
        out_specs=specs(outs),
        scratch_shapes=scratch,
        compiler_params=pltpu.CompilerParams(vmem_limit_bytes=48 * 1024 * 1024),
        name=name,
    )(*(value for _, value in args))


def swaps(axis, first):
    count = lax.axis_size(axis)
    pairs = []
    for i in range(first, count + first, 2):
        low, high = i % count, (i + 1) % count
        pairs += [(low, high), (high, low)]
    return pairs


def swap(block, axis, first):
    return lax.ppermute(block, axis, swaps(axis, first))


def on_device(fraction, source, bubble_label, subdomain, coarse_inverse):
    planes, rows, width = fraction.shape
    slabs = lax.axis_size("gz")
    columns = lax.axis_size("gy")
    devices = slabs * columns
    slab = lax.axis_index("gz")
    column = lax.axis_index("gy")
    here = slab * columns + column
    even_z = slab % 2 == 0
    even_y = column % 2 == 0
    field = jax.ShapeDtypeStruct((planes, rows, width), f32)

    def shape(*dims, dtype=f32):
        return jax.ShapeDtypeStruct(dims, dtype)

    def vmem(*dims, dtype=f32):
        return pltpu.VMEM(dims, dtype)

    def like(items):
        return [vmem(*value.shape, dtype=value.dtype) for value in items]

    def semaphores(count):
        return pltpu.SemaphoreType.DMA((count,))

    def tag(space, items):
        return [(space, item) for item in items]

    top = lax.dynamic_slice_in_dim(fraction, jnp.where(even_z, planes - DEPTH, 0), DEPTH, 0)
    bottom = lax.dynamic_slice_in_dim(fraction, jnp.where(even_z, 0, planes - DEPTH), DEPTH, 0)
    left, right = fraction[:, :DEPTH], fraction[:, rows - DEPTH :]
    y_in = [
        swap(jnp.where(even_y, right, left), "gy", 0),
        swap(jnp.where(even_y, left, right), "gy", 1),
    ]
    z_in = [swap(top, "gz", 0), swap(bottom, "gz", 1)]
    corner = jnp.stack(y_in)
    corner_top = jnp.where(even_z, corner[:, planes - DEPTH :], corner[:, :DEPTH])
    corner_bottom = jnp.where(even_z, corner[:, :DEPTH], corner[:, planes - DEPTH :])
    corner_in = [swap(corner_top, "gz", 0), swap(corner_bottom, "gz", 1)]
    bubbles = coarse_inverse[S_DEV:]
    coarse_in = [swap(bubbles, "gz", 0), swap(bubbles, "gz", 1)]
    edge = jnp.stack(
        [
            (slab == 0).astype(i32),
            (slab == slabs - 1).astype(i32),
            (column == 0).astype(i32),
            (column == columns - 1).astype(i32),
            here * B_DEV,
            jnp.int32(columns * B_DEV),
            here * S_DEV,
            slab % 2,
            column % 2,
        ]
    )

    def spread(matrix):
        return matrix.reshape(matrix.shape[0], devices, SPAN)

    dest_shape = shape(REGIONS, devices, 2 * LANES)
    (dest,) = call(
        partial(destinations_kernel, columns),
        tag("vmem", [dest_shape]),
        [vmem(REGIONS, devices, LANES)],
        tag("smem", [(slab % 2).reshape(1)]) + tag("vmem", [spread(coarse_inverse)] + [spread(m) for m in coarse_in]),
        "destinations",
    )
    codes = shape(planes, rows, width, dtype=i32)
    faces = shape(planes + 1, rows, width)
    inputs = [fraction, source, bubble_label, subdomain, dest]
    made = [codes, field, field, faces] + [field] * 7
    tall = rows + 8
    wide = shape(devices, 2 * LANES)
    first_edges = [shape(2, rows, width)] * 2 + [shape(2, planes, width)] * 2
    later_edges = [shape(rows, width)] * 2 + [shape(planes, width)] * 2
    *sent, send, code, r0, b0, cz, cyp, cym, cxp, cxm, diag, inv, mult = call(
        setup_kernel,
        tag("vmem", first_edges + [wide]) + tag("hbm", made),
        like(inputs)
        + like(made)
        + [
            vmem(planes + 2 * DEPTH, tall, width),
            vmem(planes + 4, tall, width),
            vmem(planes + 4, tall, width),
            vmem(planes + 2, tall, width),
            vmem(planes + 1, rows, width),
            vmem(planes, rows, width),
            semaphores(len(inputs)),
            semaphores(len(made)),
        ],
        tag("smem", [edge]) + tag("vmem", z_in + y_in + corner_in) + tag("hbm", inputs),
        "setup",
    )

    def exchange(parts):
        return lax.all_to_all(parts, ("gz", "gy"), 0, 0)

    def halos(sent):
        return [swap(sent[0], "gz", 0), swap(sent[1], "gz", 1), swap(sent[2], "gy", 0), swap(sent[3], "gy", 1)]

    def step(stage, parts, edges, first, later):
        last = stage == 2
        matrix = [cz, cyp, cym, cxp, cxm, diag]
        operands = [code] + first + matrix + later + ([] if last else [inv, mult, dest])
        outs = [field] * (3, 5, 5)[stage]
        ends = [] if last else later_edges
        scratch = like(operands) + [vmem(planes + 2, rows, width), vmem(2, planes, width)] + like(outs[1:])
        if not last:
            scratch.append(vmem(planes, rows, width))
        scratch += [semaphores(len(operands)), semaphores(len(outs))]
        results = call(
            partial(step_kernel, stage),
            tag("vmem", ends + [shape(devices, LANES) if last else wide]) + tag("hbm", outs),
            scratch,
            tag("smem", [edge]) + tag("vmem", parts + edges) + tag("hbm", operands),
            f"step{stage}",
        )
        return results[: len(ends)], results[len(ends)], results[len(ends) + 1 :]

    edges = halos(sent)
    parts = [exchange(send)]
    sent, send, (z0, w0, u0) = step(0, parts, edges, [b0], [r0])
    edges = edges + halos(sent)
    parts = parts + [exchange(send)]
    sent, send, (z1, w1, u1, b1, r1) = step(1, parts, edges, [b0, u0], [r0, w0, z0])
    edges = edges + halos(sent)
    parts = parts + [exchange(send)]
    _, send, (z2, w2, p1, s1, r2) = step(2, parts, edges, [b1, u0, u1], [r1, w0, w1, z0, z1])
    parts = parts + [exchange(send)]
    return tuple(
        call(
            final_kernel,
            tag("hbm", [field, field]),
            like([field] * 7) + [semaphores(6), semaphores(2)],
            tag("vmem", parts[1:]) + tag("hbm", [r2, w2, s1, z0, p1, z2]),
            "finish",
        )
    )


def solution(mesh):
    placed = (
        P("gz", "gy", None),
        P("gz", "gy", None),
        P("gz", "gy", None),
        P("gz", "gy", None),
        P(("gz", "gy"), None),
    )
    return jax.shard_map(
        on_device,
        mesh=mesh,
        in_specs=placed,
        out_specs=(P("gz", "gy", None), P("gz", "gy", None)),
        check_vma=False,
    )
```

time: 651 us -> 136 us (0.21)
  blocking collectives: 337 us -> 8.89 us
  matrix products: 100 us -> 0 us
  local copies, waits for them, and re-layouts: 74.7 us -> 24 us
  other arithmetic: 45.7 us -> 1.02 us
  Pallas kernels: 0 us -> 40.4 us
  starting transfers between devices: 58.5 us -> 37.1 us
  between operations: 8.19 us -> 0.98 us
    psum x8 -> x0, blocking collectives: 337 us -> none  [the longest x3 126 us: precondition(): totals = lax.psum(spread, ('gz', 'gy'))]
    dot_general x51 -> x0, matrix products: 100 us -> none  [the longest x24 68.6 us: one_plane(): return jnp.dot(onehot, plane_values, precision=highest)]
    dynamic_slice x48 -> x1, local copies, waits for them, and re-layouts: 52.6 us -> 1.05 us  [on_device(): lax.dynamic_slice_in_dim(fraction, jnp.where(even_z, 0, planes - DEPTH),...]
    pallas_call x0 -> x6, Pallas kernels: none -> 40.4 us  [call(): pl.pallas_call(kernel, out_shape=[shape for _, shape in outs], in_specs=s...]
    ppermute x22 -> x20, starting transfers between devices: 58.5 us -> 26.4 us  [swap(): return lax.ppermute(block, axis, swaps(axis, first))]
    all_to_all x0 -> x3, waiting for transfers between devices: none -> 16 us  [exchange(): return lax.all_to_all(parts, ('gz', 'gy'), 0, 0)]
    reduce_sum x8 -> x0, other arithmetic: 15 us -> none  [the longest x3 10.4 us: on_device(): alpha = product / lax.psum(jnp.sum(search * image), ('gz', 'gy'))]
    ppermute x22 -> x20, waiting for transfers between devices: 20.2 us -> 6.47 us  [swap(): return lax.ppermute(block, axis, swaps(axis, first))]
  transfers between devices with their start and end apart: 22 -> 23, of which waited for: 14 -> 4; matrix products, arithmetic and copies ran while one was open for 2% -> 5% of each run, Pallas kernels for 0% -> 4%
where the time goes in v1:
time: 136 us; the launch traced here: 135 us
  Pallas kernels  40.4 us (30%)
  starting transfers between devices  37.1 us (27%)
  local copies, waits for them, and re-layouts  24 us (18%)
  waiting for transfers between devices  22.4 us (16%)
  blocking collectives  8.89 us (7%)
    pallas_call x6, Pallas kernels, call(): pl.pallas_call(kernel, out_shape=[shape for _, shape in outs], in_specs=s...  40.4 us
    ppermute x20, starting transfers between devices, swap(): return lax.ppermute(block, axis, swaps(axis, first))  26.4 us
    unnamed x57, local copies, waits for them, and re-layouts  18.3 us
    all_to_all x3, waiting for transfers between devices, exchange(): return lax.all_to_all(parts, ('gz', 'gy'), 0, 0)  16 us
    all_to_all x3, starting transfers between devices, exchange(): return lax.all_to_all(parts, ('gz', 'gy'), 0, 0)  10.7 us
    all_to_all x1, blocking collectives, exchange(): return lax.all_to_all(parts, ('gz', 'gy'), 0, 0)  8.89 us
    ppermute x20, waiting for transfers between devices, swap(): return lax.ppermute(block, axis, swaps(axis, first))  6.47 us
  transfers between devices with their start and end apart: 23, of which 4 were waited for; matrix products, arithmetic and copies ran while one was open for 5% of the time, Pallas kernels for 4%

profile of v1, /device:TPU:0, one launch (start us, length us, event | category | flops | bytes accessed | tf_op | source)
XLA Modules:
  0.0 134.8 jit_solution(17300802617285327799)
XLA Ops:
  0.6 1.0 slice_select_fusion
  1.6 2.5 %collective-permute-start.3 = (f32[8,3,512]{2,1,0:T(4,128)S(1)}, f32[8,3,512]{2,1,0:T(4,128)S(1)}, u32[]{:S(2)}, u32[]{:S(2)}) collective-permute-start(f32[8,3,512]{2,1,0:T(4,128)S(1)} %get-tuple-element.82), channel_id=1, source_target_pairs={{1,2},{2,1},{3,0},{0,3},{5,6},{6,5},{7,4},{4,7},{9,10},{10,9},{11,... | collective-permute-start | bytes 147464 | tf_op jit(solution)/shard_map/ppermute | solution.py:586
  4.1 0.7 collective-permute-start.2
  4.8 1.0 constant_dynamic-slice_fusion
  5.8 4.6 %collective-permute-start.1 = (f32[3,32,512]{2,1,0:T(8,128)S(1)}, f32[3,32,512]{2,1,0:T(8,128)S(1)}, u32[]{:S(2)}, u32[]{:S(2)}) collective-permute-start(f32[3,32,512]{2,1,0:T(8,128)S(1)} %get-tuple-element.84), channel_id=1, source_target_pairs={{4,8},{8,4},{12,16},{16,12},{20,24},{24,20},{28,0},{0,28},{5,9},{9... | collective-permute-start | bytes 589832 | tf_op jit(solution)/shard_map/ppermute | solution.py:586
  10.5 0.8 slice.21
  11.3 1.9 %collective-permute-start.7 = (f32[16,640]{1,0:T(8,128)S(1)}, f32[16,640]{1,0:T(8,128)S(1)}, u32[]{:S(2)}, u32[]{:S(2)}) collective-permute-start(f32[16,640]{1,0:T(8,128)S(1)} %slice.21), channel_id=1, source_target_pairs={{4,8},{8,4},{12,16},{16,12},{20,24},{24,20},{28,0},{0,28},{5,9},{9... | collective-permute-start | bytes 122888 | tf_op jit(solution)/shard_map/ppermute | solution.py:586
  13.4 2.7 %collective-permute-start.5 = (f32[2,3,3,512]{3,2,1,0:T(4,128)S(1)}, f32[2,3,3,512]{3,2,1,0:T(4,128)S(1)}, u32[]{:S(2)}, u32[]{:S(2)}) collective-permute-start(f32[2,3,3,512]{3,2,1,0:T(4,128)S(1)} %get-tuple-element.86), channel_id=1, source_target_pairs={{4,8},{8,4},{12,16},{16,12},{20,24},{24,20},{28,0},{0,28},{5,9},{9... | collective-permute-start | bytes 110600 | tf_op jit(solution)/shard_map/ppermute | solution.py:586
  16.1 6.4 %collective-permute-done.6 = f32[16,640]{1,0:T(8,128)S(1)} collective-permute-done((f32[16,640]{1,0:T(8,128)S(1)}, f32[16,640]{1,0:T(8,128)S(1)}, u32[]{:S(2)}, u32[]{:S(2)}) %collective-permute-start.6) | collective-permute-done | bytes 40992 | tf_op jit(solution)/shard_map/ppermute | solution.py:586
  22.6 1.2 reshape.22.own_ref
  24.4 5.5 %destinations.1.dest_hbm.refs_17_.refs_25_ = f32[52,32,256]{2,1,0:T(8,128)S(1)} custom-call(s32[1]{0:T(128)} %bitcast.6.pair_ref, f32[20,32,20]{2,1,0:T(8,128)S(1)} %reshape.22.own_ref, f32[16,32,20]{2,1,0:T(8,128)S(1)} %reshape.23.near_ref, f32[16,32,20]{2,1,0:T(8,128)S(1)} %reshape.24.far_ref), custom_call_target="tpu_custom_call" | custom-call | tf_op jit(solution)/shard_map/destinations/pallas_call | solution.py:565
  29.9 1.2 copy-done
  32.5 0.9 copy-done.22
  33.4 0.8 copy-done.24
  34.2 12.3 %setup.1 = (f32[2,32,512]{2,1,0:T(8,128)}, f32[2,32,512]{2,1,0:T(8,128)}, f32[2,8,512]{2,1,0:T(8,128)S(1)}, f32[2,8,512]{2,1,0:T(8,128)S(1)}, f32[32,256]{1,0:T(...) custom-call(s32[9]{0:T(128)S(1)} %stack.60.edge_ref.refs_0_, ...), custom_call_target="tpu_custom_call" | custom-call | tf_op jit(solution)/shard_map/setup/pallas_call | solution.py:565
  46.5 0.8 copy-done.11
  47.3 0.8 copy-done.12
  48.1 0.8 copy-done.15
  50.1 2.1 %collective-permute-start.8 = (f32[2,32,512]{2,1,0:T(8,128)}, f32[2,32,512]{2,1,0:T(8,128)S(1)}, u32[]{:S(2)}, u32[]{:S(2)}) collective-permute-start(f32[2,32,512]{2,1,0:T(8,128)} %get-tuple-element.43), channel_id=1, source_target_pairs={{0,4},{4,0},{8,12},{12,8},{16,20},{20,16},{24,28},{28,24},{1,5},{5... | collective-permute-start | bytes 393224 | tf_op jit(solution)/shard_map/ppermute | solution.py:586
  52.2 1.8 %collective-permute-start.9 = (f32[2,32,512]{2,1,0:T(8,128)}, f32[2,32,512]{2,1,0:T(8,128)S(1)}, u32[]{:S(2)}, u32[]{:S(2)}) collective-permute-start(f32[2,32,512]{2,1,0:T(8,128)} %get-tuple-element.44), channel_id=1, source_target_pairs={{4,8},{8,4},{12,16},{16,12},{20,24},{24,20},{28,0},{0,28},{5,9},{9... | collective-permute-start | bytes 393224 | tf_op jit(solution)/shard_map/ppermute | solution.py:586
  54.6 3.4 %all-to-all-start = ((f32[32,1,256]{2,1,0:T(1,128)}), f32[32,1,256]{2,1,0:T(1,128)}, u32[]{:S(2)}, u32[]{:S(2)}) async-start(f32[32,1,256]{2,1,0:T(1,128)} %copy.7), calls=%async_computation | async-start | bytes 65536 | tf_op jit(solution)/shard_map/all_to_all | solution.py:683
  58.3 1.6 %collective-permute-start.11 = (f32[2,8,512]{2,1,0:T(8,128)}, f32[2,8,512]{2,1,0:T(8,128)S(1)}, u32[]{:S(2)}, u32[]{:S(2)}) collective-permute-start(f32[2,8,512]{2,1,0:T(8,128)} %copy-done.25), channel_id=1, source_target_pairs={{1,2},{2,1},{3,0},{0,3},{5,6},{6,5},{7,4},{4,7},{9,10},{10,9},{11,... | collective-permute-start | bytes 98312 | tf_op jit(solution)/shard_map/ppermute | solution.py:586
  59.9 5.4 %all-to-all-done = f32[32,1,256]{2,1,0:T(1,128)} async-done(((f32[32,1,256]{2,1,0:T(1,128)}), f32[32,1,256]{2,1,0:T(1,128)}, u32[]{:S(2)}, u32[]{:S(2)}) %all-to-all-start) | async-done | bytes 32800 | tf_op jit(solution)/shard_map/all_to_all | solution.py:683
  65.3 0.8 copy.19
  66.1 1.0 copy-done.13
  67.1 8.0 %step0.1 = (f32[32,512]{1,0:T(8,128)}, f32[32,512]{1,0:T(8,128)}, f32[8,512]{1,0:T(8,128)S(1)}, f32[8,512]{1,0:T(8,128)S(1)}, f32[32,256]{1,0:T(8,128)S(1)}, /*i...) custom-call(s32[9]{0:T(128)S(1)} %stack.60.edge_ref.refs_0_, f32[32,256]{1,0:T(8,128)S(1)} %bitcast.26, ...), custom_call_target="tpu_custom_call" | custom-call | tf_op jit(solution)/shard_map/step0/pallas_call | solution.py:565
  75.2 0.8 copy-done.5
  76.0 0.8 copy-done.7
  76.8 0.8 copy-done.8
  78.1 1.5 %collective-permute-start.13 = (f32[32,512]{1,0:T(8,128)}, f32[32,512]{1,0:T(8,128)S(1)}, u32[]{:S(2)}, u32[]{:S(2)}) collective-permute-start(f32[32,512]{1,0:T(8,128)} %get-tuple-element.60), channel_id=1, source_target_pairs={{4,8},{8,4},{12,16},{16,12},{20,24},{24,20},{28,0},{0,28},{5,9},{9... | collective-permute-start | bytes 196616 | tf_op jit(solution)/shard_map/ppermute | solution.py:586
  80.3 3.7 %all-to-all-start.1 = ((f32[32,1,256]{2,1,0:T(1,128)}), f32[32,1,256]{2,1,0:T(1,128)S(1)}, u32[]{:S(2)}, u32[]{:S(2)}) async-start(f32[32,1,256]{2,1,0:T(1,128)} %copy.8), calls=%async_computation.1 | async-start | bytes 65536 | tf_op jit(solution)/shard_map/all_to_all | solution.py:683
  84.3 1.6 %collective-permute-start.15 = (f32[8,512]{1,0:T(8,128)S(1)}, f32[8,512]{1,0:T(8,128)S(1)}, u32[]{:S(2)}, u32[]{:S(2)}) collective-permute-start(f32[8,512]{1,0:T(8,128)S(1)} %get-tuple-element.62), channel_id=1, source_target_pairs={{1,2},{2,1},{3,0},{0,3},{5,6},{6,5},{7,4},{4,7},{9,10},{10,9},{11,... | collective-permute-start | bytes 49160 | tf_op jit(solution)/shard_map/ppermute | solution.py:586
  85.9 5.3 %all-to-all-done.1 = f32[32,1,256]{2,1,0:T(1,128)S(1)} async-done(((f32[32,1,256]{2,1,0:T(1,128)}), f32[32,1,256]{2,1,0:T(1,128)S(1)}, u32[]{:S(2)}, u32[]{:S(2)}) %all-to-all-start.1) | async-done | bytes 32800 | tf_op jit(solution)/shard_map/all_to_all | solution.py:683
  91.3 1.0 copy-done.9
  92.3 1.0 copy-done.14
  93.3 8.4 %step1.1 = (f32[32,512]{1,0:T(8,128)S(1)}, f32[32,512]{1,0:T(8,128)S(1)}, f32[8,512]{1,0:T(8,128)S(1)}, f32[8,512]{1,0:T(8,128)S(1)}, f32[32,256]{1,0:T(8,128)S(...) custom-call(s32[9]{0:T(128)S(1)} %stack.60.edge_ref.refs_0_, ...), custom_call_target="tpu_custom_call" | custom-call | tf_op jit(solution)/shard_map/step1/pallas_call | solution.py:565
  101.7 0.8 copy-done.16
  102.5 0.8 copy-done.17
  103.3 0.8 copy-done.18
  104.1 0.8 copy-done.20
  105.5 1.5 %collective-permute-start.17 = (f32[32,512]{1,0:T(8,128)S(1)}, f32[32,512]{1,0:T(8,128)S(1)}, u32[]{:S(2)}, u32[]{:S(2)}) collective-permute-start(f32[32,512]{1,0:T(8,128)S(1)} %get-tuple-element.68), channel_id=1, source_target_pairs={{4,8},{8,4},{12,16},{16,12},{20,24},{24,20},{28,0},{0,28},{5,9},{9... | collective-permute-start | bytes 196616 | tf_op jit(solution)/shard_map/ppermute | solution.py:586
  107.6 3.7 %all-to-all-start.2 = ((f32[32,1,256]{2,1,0:T(1,128)}), f32[32,1,256]{2,1,0:T(1,128)S(1)}, u32[]{:S(2)}, u32[]{:S(2)}) async-start(f32[32,1,256]{2,1,0:T(1,128)} %copy.9), calls=%async_computation.2 | async-start | bytes 65536 | tf_op jit(solution)/shard_map/all_to_all | solution.py:683
  111.6 1.6 %collective-permute-start.19 = (f32[8,512]{1,0:T(8,128)S(1)}, f32[8,512]{1,0:T(8,128)S(1)}, u32[]{:S(2)}, u32[]{:S(2)}) collective-permute-start(f32[8,512]{1,0:T(8,128)S(1)} %get-tuple-element.70), channel_id=1, source_target_pairs={{1,2},{2,1},{3,0},{0,3},{5,6},{6,5},{7,4},{4,7},{9,10},{10,9},{11,... | collective-permute-start | bytes 49160 | tf_op jit(solution)/shard_map/ppermute | solution.py:586
  113.3 5.3 %all-to-all-done.2 = f32[32,1,256]{2,1,0:T(1,128)S(1)} async-done(((f32[32,1,256]{2,1,0:T(1,128)}), f32[32,1,256]{2,1,0:T(1,128)S(1)}, u32[]{:S(2)}, u32[]{:S(2)}) %all-to-all-start.2) | async-done | bytes 32800 | tf_op jit(solution)/shard_map/all_to_all | solution.py:683
  118.6 1.0 copy-done.19
  119.7 4.6 %step2.1 = (f32[32,128]{1,0:T(8,128)S(1)}, f32[8,32,512]{2,1,0:T(8,128)S(1)}, f32[8,32,512]{2,1,0:T(8,128)S(1)}, f32[8,32,512]{2,1,0:T(8,128)S(1)}, f32[8,32,512...) custom-call(s32[9]{0:T(128)S(1)} %stack.60.edge_ref.refs_0_, f32[32,256]{1,0:T(8,128)S(1)} %bitcast.28, f32[32,256]{1,0:T(8,128)S(1)} %bitcast.30, ...), custom_call_target="tpu_custom_call" | custom-call | tf_op jit(solution)/shard_map/step2/pallas_call | solution.py:565
  124.3 8.9 %all_to_all.44 = f32[32,1,128]{2,1,0:T(1,128)S(1)} all-to-all(f32[32,1,128]{2,1,0:T(1,128)S(1)} %bitcast.40), channel_id=1, replica_groups=mesh['gz'=8,'gy'=4] {'gz','gy'}, dimensions={0} | all-to-all | bytes 32768 | tf_op jit(solution)/shard_map/all_to_all | solution.py:683
  133.2 1.6 %finish.1 = (f32[8,32,512]{2,1,0:T(8,128)}, f32[8,32,512]{2,1,0:T(8,128)}) custom-call(f32[32,256]{1,0:T(8,128)S(1)} %bitcast.31, f32[32,256]{1,0:T(8,128)S(1)} %bitcast.33, f32[32,128]{1,0:T(8,128)S(1)} %bitcast.36, f32[8,32,512]{2,1,0:T(8,128)S(1)} %get-tuple-element.77.r_hbm, f32[8,32,512]{2,1,0:T(8,128)S(1)} %get-tuple-element.78.w_hbm, ...), custom_call_target="tpu_custom_call" | custom-call | tf_op jit(solution)/shard_map/finish/pallas_call | solution.py:565
  (73 shorter events, 7.4 us)
Async XLA Ops:
  1.6 11.6 %collective-permute-start.3 = (f32[8,3,512]{2,1,0:T(4,128)S(1)}, f32[8,3,512]{2,1,0:T(4,128)S(1)}, u32[]{:S(2)}, u32[]{:S(2)}) collective-permute-start(f32[8,3,512]{2,1,0:T(4,128)S(1)} %get-tuple-element.82), channel_id=1, source_target_pairs={{1,2},{2,1},{3,0},{0,3},{5,6},{6,5},{7,4},{4,7},{9,10},{10,9},{11,... | collective-permute-start | bytes 147464 | tf_op jit(solution)/shard_map/ppermute | solution.py:586
  4.1 9.3 %collective-permute-start.2 = (f32[8,3,512]{2,1,0:T(4,128)S(1)}, f32[8,3,512]{2,1,0:T(4,128)S(1)}, u32[]{:S(2)}, u32[]{:S(2)}) collective-permute-start(f32[8,3,512]{2,1,0:T(4,128)S(1)} %get-tuple-element.83), channel_id=1, source_target_pairs={{0,1},{1,0},{2,3},{3,2},{4,5},{5,4},{6,7},{7,6},{8,9},{9,8},{10,11... | collective-permute-start | bytes 147464 | tf_op jit(solution)/shard_map/ppermute | solution.py:586
  5.8 25.9 %collective-permute-start.1 = (f32[3,32,512]{2,1,0:T(8,128)S(1)}, f32[3,32,512]{2,1,0:T(8,128)S(1)}, u32[]{:S(2)}, u32[]{:S(2)}) collective-permute-start(f32[3,32,512]{2,1,0:T(8,128)S(1)} %get-tuple-element.84), channel_id=1, source_target_pairs={{4,8},{8,4},{12,16},{16,12},{20,24},{24,20},{28,0},{0,28},{5,9},{9... | collective-permute-start | bytes 589832 | tf_op jit(solution)/shard_map/ppermute | solution.py:586
  10.5 21.3 %collective-permute-start = (f32[3,32,512]{2,1,0:T(8,128)S(1)}, f32[3,32,512]{2,1,0:T(8,128)S(1)}, u32[]{:S(2)}, u32[]{:S(2)}) collective-permute-start(f32[3,32,512]{2,1,0:T(8,128)S(1)} %get-tuple-element.85), channel_id=1, source_target_pairs={{0,4},{4,0},{8,12},{12,8},{16,20},{20,16},{24,28},{28,24},{1,5},{5... | collective-permute-start | bytes 589832 | tf_op jit(solution)/shard_map/ppermute | solution.py:586
  11.3 12.8 %collective-permute-start.7 = (f32[16,640]{1,0:T(8,128)S(1)}, f32[16,640]{1,0:T(8,128)S(1)}, u32[]{:S(2)}, u32[]{:S(2)}) collective-permute-start(f32[16,640]{1,0:T(8,128)S(1)} %slice.21), channel_id=1, source_target_pairs={{4,8},{8,4},{12,16},{16,12},{20,24},{24,20},{28,0},{0,28},{5,9},{9... | collective-permute-start | bytes 122888 | tf_op jit(solution)/shard_map/ppermute | solution.py:586
  13.2 9.3 %collective-permute-start.6 = (f32[16,640]{1,0:T(8,128)S(1)}, f32[16,640]{1,0:T(8,128)S(1)}, u32[]{:S(2)}, u32[]{:S(2)}) collective-permute-start(f32[16,640]{1,0:T(8,128)S(1)} %slice.21), channel_id=1, source_target_pairs={{0,4},{4,0},{8,12},{12,8},{16,20},{20,16},{24,28},{28,24},{1,5},{5... | collective-permute-start | bytes 122888 | tf_op jit(solution)/shard_map/ppermute | solution.py:586
  13.4 17.7 %collective-permute-start.5 = (f32[2,3,3,512]{3,2,1,0:T(4,128)S(1)}, f32[2,3,3,512]{3,2,1,0:T(4,128)S(1)}, u32[]{:S(2)}, u32[]{:S(2)}) collective-permute-start(f32[2,3,3,512]{3,2,1,0:T(4,128)S(1)} %get-tuple-element.86), channel_id=1, source_target_pairs={{4,8},{8,4},{12,16},{16,12},{20,24},{24,20},{28,0},{0,28},{5,9},{9... | collective-permute-start | bytes 110600 | tf_op jit(solution)/shard_map/ppermute | solution.py:586
  22.6 8.6 %collective-permute-start.4 = (f32[2,3,3,512]{3,2,1,0:T(4,128)S(1)}, f32[2,3,3,512]{3,2,1,0:T(4,128)S(1)}, u32[]{:S(2)}, u32[]{:S(2)}) collective-permute-start(f32[2,3,3,512]{3,2,1,0:T(4,128)S(1)} %get-tuple-element.87), channel_id=1, source_target_pairs={{0,4},{4,0},{8,12},{12,8},{16,20},{20,16},{24,28},{28,24},{1,5},{5... | collective-permute-start | bytes 110600 | tf_op jit(solution)/shard_map/ppermute | solution.py:586
  29.9 1.2 copy-start
  31.2 0.6 copy-start.23
  31.8 0.7 copy-start.21
  32.5 0.9 copy-start.22
  33.4 0.8 copy-start.24
  46.5 0.8 copy-start.11
  47.3 0.8 copy-start.12
  48.1 0.8 copy-start.15
  50.1 25.1 %copy-start.2 = (f32[8,32,512]{2,1,0:T(8,128)}, f32[8,32,512]{2,1,0:T(8,128)S(1)}, u32[]{:S(2)}) copy-start(f32[8,32,512]{2,1,0:T(8,128)S(1)} %get-tuple-element.52.refs_11_.refs_17_.refs_23_) | copy-start | bytes 1572868
  50.1 25.1 %copy-start.3 = (f32[8,32,512]{2,1,0:T(8,128)}, f32[8,32,512]{2,1,0:T(8,128)S(1)}, u32[]{:S(2)}) copy-start(f32[8,32,512]{2,1,0:T(8,128)S(1)} %get-tuple-element.53.refs_12_.refs_18_.refs_24_) | copy-start | bytes 1572868
  50.1 25.1 %copy-start.4 = (f32[8,32,512]{2,1,0:T(8,128)}, f32[8,32,512]{2,1,0:T(8,128)S(1)}, u32[]{:S(2)}) copy-start(f32[8,32,512]{2,1,0:T(8,128)S(1)} %get-tuple-element.54.refs_13_.refs_19_.refs_25_) | copy-start | bytes 1572868
  50.1 41.1 %copy-start.1 = (f32[8,32,512]{2,1,0:T(8,128)}, f32[8,32,512]{2,1,0:T(8,128)S(1)}, u32[]{:S(2)}) copy-start(f32[8,32,512]{2,1,0:T(8,128)S(1)} %get-tuple-element.51.refs_10_.refs_16_.refs_22_) | copy-start | bytes 1572868
  50.1 16.0 %collective-permute-start.8 = (f32[2,32,512]{2,1,0:T(8,128)}, f32[2,32,512]{2,1,0:T(8,128)S(1)}, u32[]{:S(2)}, u32[]{:S(2)}) collective-permute-start(f32[2,32,512]{2,1,0:T(8,128)} %get-tuple-element.43), channel_id=1, source_target_pairs={{0,4},{4,0},{8,12},{12,8},{16,20},{20,16},{24,28},{28,24},{1,5},{5... | collective-permute-start | bytes 393224 | tf_op jit(solution)/shard_map/ppermute | solution.py:586
  52.2 13.9 %collective-permute-start.9 = (f32[2,32,512]{2,1,0:T(8,128)}, f32[2,32,512]{2,1,0:T(8,128)S(1)}, u32[]{:S(2)}, u32[]{:S(2)}) collective-permute-start(f32[2,32,512]{2,1,0:T(8,128)} %get-tuple-element.44), channel_id=1, source_target_pairs={{4,8},{8,4},{12,16},{16,12},{20,24},{24,20},{28,0},{0,28},{5,9},{9... | collective-permute-start | bytes 393224 | tf_op jit(solution)/shard_map/ppermute | solution.py:586
  54.6 10.6 %all-to-all-start = ((f32[32,1,256]{2,1,0:T(1,128)}), f32[32,1,256]{2,1,0:T(1,128)}, u32[]{:S(2)}, u32[]{:S(2)}) async-start(f32[32,1,256]{2,1,0:T(1,128)} %copy.7), calls=%async_computation | async-start | bytes 65536 | tf_op jit(solution)/shard_map/all_to_all | solution.py:683
  58.1 8.0 %collective-permute-start.10 = (f32[2,8,512]{2,1,0:T(8,128)}, f32[2,8,512]{2,1,0:T(8,128)S(1)}, u32[]{:S(2)}, u32[]{:S(2)}) collective-permute-start(f32[2,8,512]{2,1,0:T(8,128)} %copy-done.26), channel_id=1, source_target_pairs={{0,1},{1,0},{2,3},{3,2},{4,5},{5,4},{6,7},{7,6},{8,9},{9,8},{10,11... | collective-permute-start | bytes 98312 | tf_op jit(solution)/shard_map/ppermute | solution.py:586
  58.3 7.8 %collective-permute-start.11 = (f32[2,8,512]{2,1,0:T(8,128)}, f32[2,8,512]{2,1,0:T(8,128)S(1)}, u32[]{:S(2)}, u32[]{:S(2)}) collective-permute-start(f32[2,8,512]{2,1,0:T(8,128)} %copy-done.25), channel_id=1, source_target_pairs={{1,2},{2,1},{3,0},{0,3},{5,6},{6,5},{7,4},{4,7},{9,10},{10,9},{11,... | collective-permute-start | bytes 98312 | tf_op jit(solution)/shard_map/ppermute | solution.py:586
  66.1 1.0 copy-start.13
  75.2 0.8 copy-start.5
  76.0 0.8 copy-start.7
  76.8 0.8 copy-start.8
  77.6 13.6 %collective-permute-start.12 = (f32[32,512]{1,0:T(8,128)}, f32[32,512]{1,0:T(8,128)S(1)}, u32[]{:S(2)}, u32[]{:S(2)}) collective-permute-start(f32[32,512]{1,0:T(8,128)} %get-tuple-element.59), channel_id=1, source_target_pairs={{0,4},{4,0},{8,12},{12,8},{16,20},{20,16},{24,28},{28,24},{1,5},{5... | collective-permute-start | bytes 196616 | tf_op jit(solution)/shard_map/ppermute | solution.py:586
  78.1 13.1 %collective-permute-start.13 = (f32[32,512]{1,0:T(8,128)}, f32[32,512]{1,0:T(8,128)S(1)}, u32[]{:S(2)}, u32[]{:S(2)}) collective-permute-start(f32[32,512]{1,0:T(8,128)} %get-tuple-element.60), channel_id=1, source_target_pairs={{4,8},{8,4},{12,16},{16,12},{20,24},{24,20},{28,0},{0,28},{5,9},{9... | collective-permute-start | bytes 196616 | tf_op jit(solution)/shard_map/ppermute | solution.py:586
  80.3 10.9 %all-to-all-start.1 = ((f32[32,1,256]{2,1,0:T(1,128)}), f32[32,1,256]{2,1,0:T(1,128)S(1)}, u32[]{:S(2)}, u32[]{:S(2)}) async-start(f32[32,1,256]{2,1,0:T(1,128)} %copy.8), calls=%async_computation.1 | async-start | bytes 65536 | tf_op jit(solution)/shard_map/all_to_all | solution.py:683
  84.0 7.3 %collective-permute-start.14 = (f32[8,512]{1,0:T(8,128)S(1)}, f32[8,512]{1,0:T(8,128)S(1)}, u32[]{:S(2)}, u32[]{:S(2)}) collective-permute-start(f32[8,512]{1,0:T(8,128)S(1)} %get-tuple-element.61), channel_id=1, source_target_pairs={{0,1},{1,0},{2,3},{3,2},{4,5},{5,4},{6,7},{7,6},{8,9},{9,8},{10,11... | collective-permute-start | bytes 49160 | tf_op jit(solution)/shard_map/ppermute | solution.py:586
  84.3 6.9 %collective-permute-start.15 = (f32[8,512]{1,0:T(8,128)S(1)}, f32[8,512]{1,0:T(8,128)S(1)}, u32[]{:S(2)}, u32[]{:S(2)}) collective-permute-start(f32[8,512]{1,0:T(8,128)S(1)} %get-tuple-element.62), channel_id=1, source_target_pairs={{1,2},{2,1},{3,0},{0,3},{5,6},{6,5},{7,4},{4,7},{9,10},{10,9},{11,... | collective-permute-start | bytes 49160 | tf_op jit(solution)/shard_map/ppermute | solution.py:586
  91.3 1.0 copy-start.9
  92.3 1.0 copy-start.14
  93.3 25.3 %copy-start.10 = (f32[8,32,512]{2,1,0:T(8,128)S(1)}, f32[8,32,512]{2,1,0:T(8,128)}, u32[]{:S(2)}) copy-start(f32[8,32,512]{2,1,0:T(8,128)} %copy-done.8) | copy-start | bytes 1572868
  101.7 0.8 copy-start.16
  102.5 0.8 copy-start.17
  103.3 0.8 copy-start.18
  104.1 0.8 copy-start.20
  104.9 13.7 %collective-permute-start.16 = (f32[32,512]{1,0:T(8,128)S(1)}, f32[32,512]{1,0:T(8,128)S(1)}, u32[]{:S(2)}, u32[]{:S(2)}) collective-permute-start(f32[32,512]{1,0:T(8,128)S(1)} %get-tuple-element.67), channel_id=1, source_target_pairs={{0,4},{4,0},{8,12},{12,8},{16,20},{20,16},{24,28},{28,24},{1,5},{5... | collective-permute-start | bytes 196616 | tf_op jit(solution)/shard_map/ppermute | solution.py:586
  105.5 13.1 %collective-permute-start.17 = (f32[32,512]{1,0:T(8,128)S(1)}, f32[32,512]{1,0:T(8,128)S(1)}, u32[]{:S(2)}, u32[]{:S(2)}) collective-permute-start(f32[32,512]{1,0:T(8,128)S(1)} %get-tuple-element.68), channel_id=1, source_target_pairs={{4,8},{8,4},{12,16},{16,12},{20,24},{24,20},{28,0},{0,28},{5,9},{9... | collective-permute-start | bytes 196616 | tf_op jit(solution)/shard_map/ppermute | solution.py:586
  107.6 10.9 %all-to-all-start.2 = ((f32[32,1,256]{2,1,0:T(1,128)}), f32[32,1,256]{2,1,0:T(1,128)S(1)}, u32[]{:S(2)}, u32[]{:S(2)}) async-start(f32[32,1,256]{2,1,0:T(1,128)} %copy.9), calls=%async_computation.2 | async-start | bytes 65536 | tf_op jit(solution)/shard_map/all_to_all | solution.py:683
  111.3 7.3 %collective-permute-start.18 = (f32[8,512]{1,0:T(8,128)S(1)}, f32[8,512]{1,0:T(8,128)S(1)}, u32[]{:S(2)}, u32[]{:S(2)}) collective-permute-start(f32[8,512]{1,0:T(8,128)S(1)} %get-tuple-element.69), channel_id=1, source_target_pairs={{0,1},{1,0},{2,3},{3,2},{4,5},{5,4},{6,7},{7,6},{8,9},{9,8},{10,11... | collective-permute-start | bytes 49160 | tf_op jit(solution)/shard_map/ppermute | solution.py:586
  111.6 6.9 %collective-permute-start.19 = (f32[8,512]{1,0:T(8,128)S(1)}, f32[8,512]{1,0:T(8,128)S(1)}, u32[]{:S(2)}, u32[]{:S(2)}) collective-permute-start(f32[8,512]{1,0:T(8,128)S(1)} %get-tuple-element.70), channel_id=1, source_target_pairs={{1,2},{2,1},{3,0},{0,3},{5,6},{6,5},{7,4},{4,7},{9,10},{10,9},{11,... | collective-permute-start | bytes 49160 | tf_op jit(solution)/shard_map/ppermute | solution.py:586
  118.6 1.0 copy-start.19
  119.7 13.6 %copy-start.6 = (f32[8,32,512]{2,1,0:T(8,128)S(1)}, f32[8,32,512]{2,1,0:T(8,128)}, u32[]{:S(2)}) copy-start(f32[8,32,512]{2,1,0:T(8,128)} %copy-done.5) | copy-start | bytes 1572868
  (2 other events, 1.2 us)

commit v2 on v1

--- a/solution.py
+++ b/solution.py
@@ -1,3 +1,4 @@
+import math
 from functools import partial
 
 import jax
@@ -16,6 +17,7 @@
 REGIONS = S_DEV + 3 * B_DEV
 SCALARS = 96
 DEPTH = 3
+PIECE = 16
 
 surface_tension = 0.5
 shift_term = 0.05
@@ -55,35 +57,39 @@
     return jnp.sum(folded.reshape(rows // 8, 8, LANES), axis=0)
 
 
-def octet_sums(values, code):
-    group = code // B_DEV
-    inner = code % B_DEV
-    spread = jnp.concatenate([jnp.where(group == g, values, 0.0) for g in range(GROUPS)], axis=0)
-    high = spread.astype(bf16)
-    low = (spread - high.astype(f32)).astype(bf16)
-    left = jnp.concatenate([high, low], axis=0)
-    right = jnp.concatenate(
-        [jnp.where(inner == i, 1.0, 0.0) for i in range(B_DEV)], axis=0
-    ).astype(bf16)
-    return lax.dot_general(left, right, (((1,), (1,)), ((), ())), preferred_element_type=f32)
+def piece_sums(values, code):
+    group = (code // B_DEV).astype(f32).astype(bf16)
+    inner = (code % B_DEV).astype(f32).astype(bf16)
+    high = values.astype(bf16)
+    low = (values - high.astype(f32)).astype(bf16)
+    zero, one = jnp.zeros_like(high), jnp.ones_like(high)
+    left = [jnp.where(group == g, part, zero) for part in (high, low) for g in range(GROUPS)]
+    right = [jnp.where(inner == i, one, zero) for i in range(B_DEV)]
+    return lax.dot_general(
+        jnp.concatenate(left, axis=0),
+        jnp.concatenate(right, axis=0),
+        (((1,), (1,)), ((), ())),
+        preferred_element_type=f32,
+    )
 
 
 def region_row(value_ref, code_ref):
     planes, rows, _ = value_ref.shape
-    octets = rows // 8
+    pieces = rows // PIECE
 
     def step(index, acc):
-        plane = index // octets
-        start = pl.multiple_of((index % octets) * 8, 8)
-        return acc + octet_sums(value_ref[plane, pl.ds(start, 8), :], code_ref[plane, pl.ds(start, 8), :])
+        plane = index // pieces
+        piece = pl.ds(pl.multiple_of((index % pieces) * PIECE, PIECE), PIECE)
+        return acc + piece_sums(value_ref[plane, piece, :], code_ref[plane, piece, :])
 
     acc = lax.fori_loop(
-        0, planes * octets, step, jnp.zeros((2 * GROUPS * 8, B_DEV * 8), f32), unroll=4
+        0, planes * pieces, step, jnp.zeros((2 * GROUPS * PIECE, B_DEV * PIECE), f32), unroll=planes * pieces
     )
     shape = acc.shape
-    kept = jnp.where(iota(shape, 0) % 8 == iota(shape, 1) % 8, acc, 0.0)
-    folded = jnp.sum(kept.reshape(2 * GROUPS, 8, LANES), axis=1)
-    pick = jnp.where(iota((LANES, LANES), 0) // 8 == iota((LANES, LANES), 1) % B_DEV, 1.0, 0.0)
+    kept = jnp.where(iota(shape, 0) % PIECE == iota(shape, 1) % PIECE, acc, 0.0)
+    folded = jnp.sum(kept.reshape(2 * GROUPS, PIECE, shape[1]), axis=1)
+    shape = (shape[1], LANES)
+    pick = jnp.where(iota(shape, 0) // PIECE == iota(shape, 1) % B_DEV, 1.0, 0.0)
     spread = jnp.dot(folded, pick, precision=highest, preferred_element_type=f32)
     shape = spread.shape
     lane = iota(shape, 1)
@@ -125,19 +131,18 @@
         copy.wait()
 
 
-def send_coarse(row, dest_ref, send_ref):
+def coarse_parts(row, dest_ref):
     wide = jnp.broadcast_to(row, (8, LANES))
 
     def step(region, acc):
         lane = jnp.where(region < S_DEV, region, region + B_DEV - S_DEV)
         factor = jnp.take_along_axis(wide, jnp.full((8, LANES), lane, i32), axis=1)[0:1, :]
-        factor = jnp.concatenate([factor, factor], axis=1)
         return acc + factor * dest_ref[region]
 
-    send_ref[...] = lax.fori_loop(0, REGIONS, step, jnp.zeros(send_ref.shape, f32), unroll=4)
-
-
-def destinations_kernel(columns, pair_ref, own_ref, near_ref, far_ref, dest_ref, wide_ref):
+    return lax.fori_loop(0, REGIONS, step, jnp.zeros(dest_ref.shape[1:], f32), unroll=4)
+
+
+def destinations_kernel(columns, pair_ref, own_ref, near_ref, far_ref, dest_hbm, wide_ref, dest_ref, sems):
     devices = own_ref.shape[1]
     even_z = pair_ref[0] == 0
     wide_ref[...] = jnp.zeros(wide_ref.shape, f32)
@@ -170,10 +175,14 @@
         table = table + from_device(place(base, 3 * B_DEV + bubbles, 4 * B_DEV, B_DEV), 2 * columns)
         table = table + from_device(place(base, 4 * B_DEV + bubbles, 5 * B_DEV, B_DEV), -2 * columns)
         own_codes = jnp.where((lane < S_DEV) | ((lane >= B_DEV) & (lane < CODES)), table, 0.0)
-        dest_ref[region] = jnp.concatenate([table, from_device(own_codes, -1)], axis=1)
+        dest_ref[region, pl.ds(0, devices, stride=2), :] = table
+        dest_ref[region, pl.ds(1, devices, stride=2), :] = from_device(own_codes, -1)
         return carry
 
-    lax.fori_loop(0, REGIONS, one, 0)
+    lax.fori_loop(0, REGIONS, one, 0, unroll=4)
+    write = pltpu.make_async_copy(dest_ref, dest_hbm, sems.at[0])
+    write.start()
+    write.wait()
 
 
 def write_edges(even_z, even_y, value_ref, z_refs, y_refs, convert=lambda value: value):
@@ -185,6 +194,23 @@
         last = convert(value_ref[plane, rows - 1 : rows, :])
         y_refs[0][plane : plane + 1, :] = jnp.where(even_y, last, first)
         y_refs[1][plane : plane + 1, :] = jnp.where(even_y, first, last)
+
+
+def slices_kernel(edge_ref, frac_hbm, coarse_hbm, z0_ref, z1_ref, y0_ref, y1_ref, bubble_ref, frac_ref, coarse_ref, sems):
+    planes, rows, _ = frac_ref.shape
+    copies = [
+        pltpu.make_async_copy(frac_hbm, frac_ref, sems.at[0]),
+        pltpu.make_async_copy(coarse_hbm, coarse_ref, sems.at[1]),
+    ]
+    start_all(copies)
+    even_z, even_y = edge_ref[7] == 0, edge_ref[8] == 0
+    wait_all(copies)
+    bubble_ref[...] = coarse_ref[S_DEV:SPAN, :]
+    z0_ref[...] = frac_ref[pl.ds(jnp.where(even_z, planes - DEPTH, 0), DEPTH)]
+    z1_ref[...] = frac_ref[pl.ds(jnp.where(even_z, 0, planes - DEPTH), DEPTH)]
+    first, last = frac_ref[:, 0:DEPTH, :], frac_ref[:, rows - DEPTH : rows, :]
+    y0_ref[...] = jnp.where(even_y, last, first)
+    y1_ref[...] = jnp.where(even_y, first, last)
 
 
 def setup_kernel(
@@ -256,8 +282,8 @@
         gz = 0.5 * (deep_ref[index + 2] - deep_ref[index])
         gy = 0.5 * (up_rows(here) - down_rows(here))
         gx = 0.5 * (right_of(here) - left_of(here))
-        length = jnp.maximum(jnp.sqrt(gz * gz + gy * gy + gx * gx), norm_floor)
-        scale = jnp.where(inside_y & keep, 1.0 / length, 0.0)
+        scale = jnp.minimum(lax.rsqrt(gz * gz + gy * gy + gx * gx), 1.0 / norm_floor)
+        scale = jnp.where(inside_y & keep, scale, 0.0)
         ny = gy * scale
         nx = gx * scale
         nz_ref[index] = gz * scale
@@ -303,7 +329,7 @@
         f_right = right_of(f)
         cxp = 2.0 / (d + (1.0 - gas_drop * f_right))
         fx = cxp * (0.5 * (k + right_of(k))) * (f_right - f)
-        outer = 2.0 / (d + 1.0)
+        outer = jnp.concatenate([2.0 / (d[:, :LANES] + 1.0), jnp.zeros((rows, width - LANES), f32)], axis=1)
         cxm = jnp.where(lane_mid == 0, outer, prev_x(cxp))
         fx_before = jnp.where(lane_mid == 0, outer * (0.5 * k) * f, prev_x(fx))
         terms = fz_ref[plane + 1] - fz_ref[plane] + sum_y + (fx - fx_before)
@@ -355,8 +381,20 @@
         even_z, even_y, code_ref, [ez0_ref.at[1], ez1_ref.at[1]], [ey0_ref.at[1], ey1_ref.at[1]],
         convert=lambda value: value.astype(f32),
     )
-    send_coarse(region_row(r_ref, code_ref), dest_ref, send_ref)
+    send_ref[...] = coarse_parts(region_row(r_ref, code_ref), dest_ref)
     wait_all(writes)
+
+
+def table_rows(parts):
+    folded = jnp.sum(parts.reshape(parts.shape[0] // 8, 8, LANES), axis=0)
+    even = iota(folded.shape, 0) % 2 == 0
+    return jnp.concatenate(
+        [
+            jnp.sum(jnp.where(even, folded, 0.0), axis=0, keepdims=True),
+            jnp.sum(jnp.where(even, 0.0, folded), axis=0, keepdims=True),
+        ],
+        axis=0,
+    )
 
 
 def scalars_of(sums):
@@ -413,14 +451,14 @@
     planes, rows, width = code_ref.shape
     even_z, even_y = edge_ref[7] == 0, edge_ref[8] == 0
 
-    sums = [jnp.sum(part[...], axis=0, keepdims=True) for part in parts]
-    alphas, betas = scalars_of([row[:, :LANES] for row in sums[1:]])
+    sums = [table_rows(part[...]) for part in parts]
+    alphas, betas = scalars_of([row[0:1] for row in sums[1:]])
     table = sums[0]
     if stage >= 1:
         table = table - alphas[0] * sums[1]
     if stage == 2:
         table = table - alphas[1] * (sums[2] + betas[1] * sums[1])
-    near, side = table[:, :LANES], table[:, LANES:]
+    near, side = table[0:1], table[1:2]
 
     def combine(values):
         out = values[0]
@@ -524,8 +562,8 @@
         writes["u"].start()
         write_edges(even_z, even_y, made["u"], edges_z, edges_y)
         reads["dest"].wait()
-        send_coarse(region_row(made["w"], code_ref), held["dest"], send_ref)
-        send_ref[:, :LANES] = send_ref[:, :LANES] + row
+        parts = coarse_parts(region_row(made["w"], code_ref), held["dest"])
+        send_ref[...] = parts + jnp.where(iota(parts.shape, 0) % 2 == 0, row, 0.0)
     wait_all(writes.values())
 
 
@@ -536,7 +574,7 @@
     pairs = [(z0_hbm, z0_ref), (p_hbm, p_ref), (z_hbm, z_ref), (r_hbm, r_ref), (w_hbm, w_ref), (s_hbm, s_ref)]
     reads = [pltpu.make_async_copy(a, b, in_sems.at[i]) for i, (a, b) in enumerate(pairs)]
     start_all(reads)
-    sums = [jnp.sum(ref[:, :LANES], axis=0, keepdims=True) for ref in (d0_ref, d1_ref, d2_ref)]
+    sums = [table_rows(d0_ref[...])[0:1], table_rows(d1_ref[...])[0:1], jnp.sum(d2_ref[...], axis=0, keepdims=True)]
     alphas, betas = scalars_of(sums)
     mixed = alphas[2] * betas[2]
     along = alphas[1] + mixed
@@ -552,25 +590,26 @@
     r_write.wait()
 
 
-def in_hbm(shape):
-    return ("hbm", shape)
-
-
 def call(kernel, outs, scratch, args, name):
     spaces = {"smem": pltpu.SMEM, "vmem": pltpu.VMEM, "hbm": pltpu.HBM}
 
     def specs(items):
         return [pl.BlockSpec(memory_space=spaces[space]) for space, _ in items]
 
+    held = sum(4 * math.prod(ref.shape) for ref in scratch)
+    made = [pltpu.HBM(out.shape, out.dtype) if space == "hbm" else out for space, out in outs]
+    operands = [
+        pltpu.with_memory_space_constraint(value, pltpu.HBM) if space == "hbm" else value for space, value in args
+    ]
     return pl.pallas_call(
         kernel,
-        out_shape=[shape for _, shape in outs],
+        out_shape=made,
         in_specs=specs(args),
         out_specs=specs(outs),
         scratch_shapes=scratch,
-        compiler_params=pltpu.CompilerParams(vmem_limit_bytes=48 * 1024 * 1024),
+        compiler_params=pltpu.CompilerParams(vmem_limit_bytes=held + 12 * 1024 * 1024),
         name=name,
-    )(*(value for _, value in args))
+    )(*operands)
 
 
 def swaps(axis, first):
@@ -613,20 +652,6 @@
     def tag(space, items):
         return [(space, item) for item in items]
 
-    top = lax.dynamic_slice_in_dim(fraction, jnp.where(even_z, planes - DEPTH, 0), DEPTH, 0)
-    bottom = lax.dynamic_slice_in_dim(fraction, jnp.where(even_z, 0, planes - DEPTH), DEPTH, 0)
-    left, right = fraction[:, :DEPTH], fraction[:, rows - DEPTH :]
-    y_in = [
-        swap(jnp.where(even_y, right, left), "gy", 0),
-        swap(jnp.where(even_y, left, right), "gy", 1),
-    ]
-    z_in = [swap(top, "gz", 0), swap(bottom, "gz", 1)]
-    corner = jnp.stack(y_in)
-    corner_top = jnp.where(even_z, corner[:, planes - DEPTH :], corner[:, :DEPTH])
-    corner_bottom = jnp.where(even_z, corner[:, :DEPTH], corner[:, planes - DEPTH :])
-    corner_in = [swap(corner_top, "gz", 0), swap(corner_bottom, "gz", 1)]
-    bubbles = coarse_inverse[S_DEV:]
-    coarse_in = [swap(bubbles, "gz", 0), swap(bubbles, "gz", 1)]
     edge = jnp.stack(
         [
             (slab == 0).astype(i32),
@@ -641,14 +666,29 @@
         ]
     )
 
+    top, bottom, *sides, bubbles = call(
+        slices_kernel,
+        tag("vmem", [shape(DEPTH, rows, width)] * 2 + [shape(planes, DEPTH, width)] * 2 + [shape(B_DEV, devices * SPAN)]),
+        [vmem(planes, rows, width), vmem(SPAN, devices * SPAN), semaphores(2)],
+        tag("smem", [edge]) + tag("hbm", [fraction, coarse_inverse]),
+        "slices",
+    )
+    coarse_in = [swap(bubbles, "gz", 0), swap(bubbles, "gz", 1)]
+    y_in = [swap(sides[0], "gy", 0), swap(sides[1], "gy", 1)]
+    z_in = [swap(top, "gz", 0), swap(bottom, "gz", 1)]
+    corner = jnp.stack(y_in)
+    corner_top = jnp.where(even_z, corner[:, planes - DEPTH :], corner[:, :DEPTH])
+    corner_bottom = jnp.where(even_z, corner[:, :DEPTH], corner[:, planes - DEPTH :])
+    corner_in = [swap(corner_top, "gz", 0), swap(corner_bottom, "gz", 1)]
+
     def spread(matrix):
         return matrix.reshape(matrix.shape[0], devices, SPAN)
 
-    dest_shape = shape(REGIONS, devices, 2 * LANES)
+    dest_shape = shape(REGIONS, 2 * devices, LANES)
     (dest,) = call(
         partial(destinations_kernel, columns),
-        tag("vmem", [dest_shape]),
-        [vmem(REGIONS, devices, LANES)],
+        tag("hbm", [dest_shape]),
+        [vmem(REGIONS, devices, LANES)] + like([dest_shape]) + [semaphores(1)],
         tag("smem", [(slab % 2).reshape(1)]) + tag("vmem", [spread(coarse_inverse)] + [spread(m) for m in coarse_in]),
         "destinations",
     )
@@ -657,7 +697,7 @@
     inputs = [fraction, source, bubble_label, subdomain, dest]
     made = [codes, field, field, faces] + [field] * 7
     tall = rows + 8
-    wide = shape(devices, 2 * LANES)
+    wide = shape(2 * devices, LANES)
     first_edges = [shape(2, rows, width)] * 2 + [shape(2, planes, width)] * 2
     later_edges = [shape(rows, width)] * 2 + [shape(planes, width)] * 2
     *sent, send, code, r0, b0, cz, cyp, cym, cxp, cxm, diag, inv, mult = call(
@@ -680,7 +720,8 @@
     )
 
     def exchange(parts):
-        return lax.all_to_all(parts, ("gz", "gy"), 0, 0)
+        blocks = parts.reshape(devices, -1, LANES)
+        return lax.all_to_all(blocks, ("gz", "gy"), 0, 0).reshape(parts.shape)
 
     def halos(sent):
         return [swap(sent[0], "gz", 0), swap(sent[1], "gz", 1), swap(sent[2], "gy", 0), swap(sent[3], "gy", 1)]

time: 136 us -> 115 us (0.85)
  local copies, waits for them, and re-layouts: 24 us -> 1.82 us
  Pallas kernels: 40.4 us -> 42.9 us
  starting transfers between devices: 37.1 us -> 39.5 us
  waiting for transfers between devices: 22.4 us -> 20.1 us
    unnamed x57 -> x0, local copies, waits for them, and re-layouts: 18.3 us -> none
    all_to_all x3, waiting for transfers between devices: 16 us -> 11.1 us  [exchange(): return lax.all_to_all(blocks, ('gz', 'gy'), 0, 0).reshape(parts.shape)]
    ppermute x20, starting transfers between devices: 26.4 us -> 29.6 us  [swap(): return lax.ppermute(block, axis, swaps(axis, first))]
    pallas_call x6 -> x7, Pallas kernels: 40.4 us -> 42.9 us  [call(): pl.pallas_call(kernel, out_shape=made, in_specs=specs(args), out_specs=sp...]
    ppermute x20, waiting for transfers between devices: 6.47 us -> 8.93 us  [swap(): return lax.ppermute(block, axis, swaps(axis, first))]
    all_to_all x3 -> x0, local copies, waits for them, and re-layouts: 1.93 us -> none  [exchange(): return lax.all_to_all(parts, ('gz', 'gy'), 0, 0)]
  transfers between devices with their start and end apart: 23 -> 23, of which waited for: 4 -> 7; matrix products, arithmetic and copies ran while one was open for 5% -> 2% of each run, Pallas kernels for 4% -> 3%
where the time goes in v2:
time: 115 us; the launch traced here: 114 us
  Pallas kernels  42.9 us (37%)
  starting transfers between devices  39.5 us (34%)
  waiting for transfers between devices  20.1 us (17%)
  blocking collectives  8.99 us (8%)
  local copies, waits for them, and re-layouts  1.82 us (2%)
    pallas_call x7, Pallas kernels, call(): pl.pallas_call(kernel, out_shape=made, in_specs=specs(args), out_specs=sp...  42.9 us
    ppermute x20, starting transfers between devices, swap(): return lax.ppermute(block, axis, swaps(axis, first))  29.6 us
    all_to_all x3, waiting for transfers between devices, exchange(): return lax.all_to_all(blocks, ('gz', 'gy'), 0, 0).reshape(parts.shape)  11.1 us
    all_to_all x3, starting transfers between devices, exchange(): return lax.all_to_all(blocks, ('gz', 'gy'), 0, 0).reshape(parts.shape)  9.94 us
    all_to_all x1, blocking collectives, exchange(): return lax.all_to_all(blocks, ('gz', 'gy'), 0, 0).reshape(parts.shape)  8.99 us
    ppermute x20, waiting for transfers between devices, swap(): return lax.ppermute(block, axis, swaps(axis, first))  8.93 us
  transfers between devices with their start and end apart: 23, of which 7 were waited for; matrix products, arithmetic and copies ran while one was open for 2% of the time, Pallas kernels for 3%

profile of v2, /device:TPU:0, one launch (start us, length us, event | category | flops | bytes accessed | tf_op | source)
XLA Modules:
  0.0 114.2 jit_solution(10449417054684994580)
XLA Ops:
  0.7 0.1 stack.60.edge_ref.refs_0_
  0.7 1.7 %slices.1 = (f32[3,32,512]{2,1,0:T(8,128)S(1)}, f32[3,32,512]{2,1,0:T(8,128)S(1)}, f32[8,3,512]{2,1,0:T(4,128)S(1)}, f32[8,3,512]{2,1,0:T(4,128)S(1)}, f32[16,640]{1,0:T(8,128)S(1)}) custom-call(s32[9]{0:T(128)S(1)} %stack.60.edge_ref.refs_0_, f32[8,32,512]{2,1,0:T(8,128)} %frac_hbm.3, f32[20,640]{1,0:T(8,128)} %coarse_hbm.1), custom_call_target="tpu_custom_call" | custom-call | tf_op jit(solution)/shard_map/slices/pallas_call | solution.py:604
  2.4 0.6 collective-permute-start.2
  3.0 2.6 %collective-permute-start.3 = (f32[8,3,512]{2,1,0:T(4,128)S(1)}, f32[8,3,512]{2,1,0:T(4,128)S(1)}, u32[]{:S(2)}, u32[]{:S(2)}) collective-permute-start(f32[8,3,512]{2,1,0:T(4,128)S(1)} %get-tuple-element.50), channel_id=1, source_target_pairs={{1,2},{2,1},{3,0},{0,3},{5,6},{6,5},{7,4},{4,7},{9,10},{10,9},{11,... | collective-permute-start | bytes 147464 | tf_op jit(solution)/shard_map/ppermute | solution.py:625
  5.6 1.5 %collective-permute-start = (f32[3,32,512]{2,1,0:T(8,128)S(1)}, f32[3,32,512]{2,1,0:T(8,128)S(1)}, u32[]{:S(2)}, u32[]{:S(2)}) collective-permute-start(f32[3,32,512]{2,1,0:T(8,128)S(1)} %get-tuple-element.47), channel_id=1, source_target_pairs={{0,4},{4,0},{8,12},{12,8},{16,20},{20,16},{24,28},{28,24},{1,5},{5... | collective-permute-start | bytes 589832 | tf_op jit(solution)/shard_map/ppermute | solution.py:625
  7.1 3.5 %collective-permute-start.1 = (f32[3,32,512]{2,1,0:T(8,128)S(1)}, f32[3,32,512]{2,1,0:T(8,128)S(1)}, u32[]{:S(2)}, u32[]{:S(2)}) collective-permute-start(f32[3,32,512]{2,1,0:T(8,128)S(1)} %get-tuple-element.48), channel_id=1, source_target_pairs={{4,8},{8,4},{12,16},{16,12},{20,24},{24,20},{28,0},{0,28},{5,9},{9... | collective-permute-start | bytes 589832 | tf_op jit(solution)/shard_map/ppermute | solution.py:625
  10.6 1.2 %collective-permute-start.7 = (f32[16,640]{1,0:T(8,128)S(1)}, f32[16,640]{1,0:T(8,128)S(1)}, u32[]{:S(2)}, u32[]{:S(2)}) collective-permute-start(f32[16,640]{1,0:T(8,128)S(1)} %get-tuple-element.51), channel_id=1, source_target_pairs={{4,8},{8,4},{12,16},{16,12},{20,24},{24,20},{28,0},{0,28},{5,9},{9... | collective-permute-start | bytes 122888 | tf_op jit(solution)/shard_map/ppermute | solution.py:625
  11.8 0.0 collective-permute-done.3.y1_in
  11.9 3.6 %collective-permute-start.5 = (f32[2,3,3,512]{3,2,1,0:T(4,128)S(1)}, f32[2,3,3,512]{3,2,1,0:T(4,128)S(1)}, u32[]{:S(2)}, u32[]{:S(2)}) collective-permute-start(f32[2,3,3,512]{3,2,1,0:T(4,128)S(1)} %get-tuple-element.92), channel_id=1, source_target_pairs={{4,8},{8,4},{12,16},{16,12},{20,24},{24,20},{28,0},{0,28},{5,9},{9... | collective-permute-start | bytes 110600 | tf_op jit(solution)/shard_map/ppermute | solution.py:625
  15.5 4.0 %collective-permute-done.6 = f32[16,640]{1,0:T(8,128)S(1)} collective-permute-done((f32[16,640]{1,0:T(8,128)S(1)}, f32[16,640]{1,0:T(8,128)S(1)}, u32[]{:S(2)}, u32[]{:S(2)}) %collective-permute-start.6) | collective-permute-done | bytes 40992 | tf_op jit(solution)/shard_map/ppermute | solution.py:625
  19.5 1.5 %collective-permute-start.4 = (f32[2,3,3,512]{3,2,1,0:T(4,128)S(1)}, f32[2,3,3,512]{3,2,1,0:T(4,128)S(1)}, u32[]{:S(2)}, u32[]{:S(2)}) collective-permute-start(f32[2,3,3,512]{3,2,1,0:T(4,128)S(1)} %get-tuple-element.93), channel_id=1, source_target_pairs={{0,4},{4,0},{8,12},{12,8},{16,20},{20,16},{24,28},{28,24},{1,5},{5... | collective-permute-start | bytes 110600 | tf_op jit(solution)/shard_map/ppermute | solution.py:625
  21.0 1.2 %reshape.38.own_ref = f32[20,32,20]{2,1,0:T(8,128)S(1)} reshape(f32[20,640]{1,0:T(8,128)} %coarse_hbm.1) | data formatting | bytes 102400 | tf_op jit(solution)/shard_map/reshape | solution.py:685
  22.2 0.3 reshape.39.near_ref
  22.5 0.3 reshape.40.far_ref
  22.8 3.9 %destinations.1.dest_hbm.refs_17_.refs_25_ = f32[52,64,128]{2,1,0:T(8,128)} custom-call(s32[1]{0:T(128)} %bitcast.6.pair_ref, f32[20,32,20]{2,1,0:T(8,128)S(1)} %reshape.38.own_ref, f32[16,32,20]{2,1,0:T(8,128)S(1)} %reshape.39.near_ref, f32[16,32,20]{2,1,0:T(8,128)S(1)} %reshape.40.far_ref), custom_call_target="tpu_custom_call" | custom-call | tf_op jit(solution)/shard_map/destinations/pallas_call | solution.py:604
  26.6 0.0 collective-permute-done.4.k0_in
  26.6 0.0 collective-permute-done.z0_in
  26.7 11.6 %setup.1 = (f32[2,32,512]{2,1,0:T(8,128)S(1)}, f32[2,32,512]{2,1,0:T(8,128)S(1)}, f32[2,8,512]{2,1,0:T(8,128)S(1)}, f32[2,8,512]{2,1,0:T(8,128)S(1)}, f32[64,128...) custom-call(s32[9]{0:T(128)S(1)} %stack.60.edge_ref.refs_0_, ...), custom_call_target="tpu_custom_call" | custom-call | tf_op jit(solution)/shard_map/setup/pallas_call | solution.py:604
  38.3 0.6 collective-permute-start.8
  38.9 4.6 %collective-permute-start.9 = (f32[2,32,512]{2,1,0:T(8,128)S(1)}, f32[2,32,512]{2,1,0:T(8,128)S(1)}, u32[]{:S(2)}, u32[]{:S(2)}) collective-permute-start(f32[2,32,512]{2,1,0:T(8,128)S(1)} %get-tuple-element.54), channel_id=1, source_target_pairs={{4,8},{8,4},{12,16},{16,12},{20,24},{24,20},{28,0},{0,28},{5,9},{9... | collective-permute-start | bytes 393224 | tf_op jit(solution)/shard_map/ppermute | solution.py:625
  43.4 2.5 %all-to-all-start = ((f32[32,2,128]{2,1,0:T(2,128)}), f32[32,2,128]{2,1,0:T(2,128)S(1)}, u32[]{:S(2)}, u32[]{:S(2)}) async-start(f32[32,2,128]{2,1,0:T(2,128)} %bitcast.10), calls=%async_computation | async-start | bytes 65536 | tf_op jit(solution)/shard_map/all_to_all | solution.py:724
  46.0 0.2 collective-permute-start.10
  46.2 1.6 %collective-permute-start.11 = (f32[2,8,512]{2,1,0:T(8,128)S(1)}, f32[2,8,512]{2,1,0:T(8,128)S(1)}, u32[]{:S(2)}, u32[]{:S(2)}) collective-permute-start(f32[2,8,512]{2,1,0:T(8,128)S(1)} %get-tuple-element.56), channel_id=1, source_target_pairs={{1,2},{2,1},{3,0},{0,3},{5,6},{6,5},{7,4},{4,7},{9,10},{10,9},{11,... | collective-permute-start | bytes 98312 | tf_op jit(solution)/shard_map/ppermute | solution.py:625
  47.8 0.0 collective-permute-done.10.refs_4_.refs_5_.refs_6_
  47.8 1.7 %collective-permute-done.11.refs_5_.refs_6_.refs_7_ = f32[2,8,512]{2,1,0:T(8,128)S(1)} collective-permute-done((f32[2,8,512]{2,1,0:T(8,128)S(1)}, f32[2,8,512]{2,1,0:T(8,128)S(1)}, u32[]{:S(2)}, u32[]{:S(2)}) %collective-permute-start.11) | collective-permute-done | bytes 32800 | tf_op jit(solution)/shard_map/ppermute | solution.py:625
  49.5 3.7 %all-to-all-done = f32[32,2,128]{2,1,0:T(2,128)S(1)} async-done(((f32[32,2,128]{2,1,0:T(2,128)}), f32[32,2,128]{2,1,0:T(2,128)S(1)}, u32[]{:S(2)}, u32[]{:S(2)}) %all-to-all-start) | async-done | bytes 32800 | tf_op jit(solution)/shard_map/all_to_all | solution.py:724
  53.2 0.0 collective-permute-done.8.refs_2_.refs_3_.refs_4_
  53.2 0.0 collective-permute-done.9.refs_3_.refs_4_.refs_5_
  53.2 8.0 %step0.1 = (f32[32,512]{1,0:T(8,128)S(1)}, f32[32,512]{1,0:T(8,128)S(1)}, f32[8,512]{1,0:T(8,128)S(1)}, f32[8,512]{1,0:T(8,128)S(1)}, f32[64,128]{1,0:T(8,128)},...) custom-call(s32[9]{0:T(128)S(1)} %stack.60.edge_ref.refs_0_, f32[64,128]{1,0:T(8,128)S(1)} %bitcast.20, ...), custom_call_target="tpu_custom_call" | custom-call | tf_op jit(solution)/shard_map/step0/pallas_call | solution.py:604
  61.2 0.6 collective-permute-start.12
  61.9 1.4 %collective-permute-start.13 = (f32[32,512]{1,0:T(8,128)S(1)}, f32[32,512]{1,0:T(8,128)S(1)}, u32[]{:S(2)}, u32[]{:S(2)}) collective-permute-start(f32[32,512]{1,0:T(8,128)S(1)} %get-tuple-element.70), channel_id=1, source_target_pairs={{4,8},{8,4},{12,16},{16,12},{20,24},{24,20},{28,0},{0,28},{5,9},{9... | collective-permute-start | bytes 196616 | tf_op jit(solution)/shard_map/ppermute | solution.py:625
  63.3 3.7 %all-to-all-start.1 = ((f32[32,2,128]{2,1,0:T(2,128)}), f32[32,2,128]{2,1,0:T(2,128)S(1)}, u32[]{:S(2)}, u32[]{:S(2)}) async-start(f32[32,2,128]{2,1,0:T(2,128)} %bitcast.12), calls=%async_computation.1 | async-start | bytes 65536 | tf_op jit(solution)/shard_map/all_to_all | solution.py:724
  67.0 0.3 collective-permute-start.14
  67.4 1.6 %collective-permute-start.15 = (f32[8,512]{1,0:T(8,128)S(1)}, f32[8,512]{1,0:T(8,128)S(1)}, u32[]{:S(2)}, u32[]{:S(2)}) collective-permute-start(f32[8,512]{1,0:T(8,128)S(1)} %get-tuple-element.72), channel_id=1, source_target_pairs={{1,2},{2,1},{3,0},{0,3},{5,6},{6,5},{7,4},{4,7},{9,10},{10,9},{11,... | collective-permute-start | bytes 49160 | tf_op jit(solution)/shard_map/ppermute | solution.py:625
  69.0 0.0 collective-permute-done.14.refs_9_.refs_10_
  69.0 1.6 %collective-permute-done.15.refs_10_.refs_11_ = f32[8,512]{1,0:T(8,128)S(1)} collective-permute-done((f32[8,512]{1,0:T(8,128)S(1)}, f32[8,512]{1,0:T(8,128)S(1)}, u32[]{:S(2)}, u32[]{:S(2)}) %collective-permute-start.15) | collective-permute-done | bytes 16416 | tf_op jit(solution)/shard_map/ppermute | solution.py:625
  70.6 3.7 %all-to-all-done.1 = f32[32,2,128]{2,1,0:T(2,128)S(1)} async-done(((f32[32,2,128]{2,1,0:T(2,128)}), f32[32,2,128]{2,1,0:T(2,128)S(1)}, u32[]{:S(2)}, u32[]{:S(2)}) %all-to-all-start.1) | async-done | bytes 32800 | tf_op jit(solution)/shard_map/all_to_all | solution.py:724
  74.3 8.6 %step1.1 = (f32[32,512]{1,0:T(8,128)S(1)}, f32[32,512]{1,0:T(8,128)S(1)}, f32[8,512]{1,0:T(8,128)S(1)}, f32[8,512]{1,0:T(8,128)S(1)}, f32[64,128]{1,0:T(8,128)},...) custom-call(s32[9]{0:T(128)S(1)} %stack.60.edge_ref.refs_0_, ...), custom_call_target="tpu_custom_call" | custom-call | tf_op jit(solution)/shard_map/step1/pallas_call | solution.py:604
  82.9 0.6 collective-permute-start.16
  83.5 1.5 %collective-permute-start.17 = (f32[32,512]{1,0:T(8,128)S(1)}, f32[32,512]{1,0:T(8,128)S(1)}, u32[]{:S(2)}, u32[]{:S(2)}) collective-permute-start(f32[32,512]{1,0:T(8,128)S(1)} %get-tuple-element.78), channel_id=1, source_target_pairs={{4,8},{8,4},{12,16},{16,12},{20,24},{24,20},{28,0},{0,28},{5,9},{9... | collective-permute-start | bytes 196616 | tf_op jit(solution)/shard_map/ppermute | solution.py:625
  85.0 3.7 %all-to-all-start.2 = ((f32[32,2,128]{2,1,0:T(2,128)}), f32[32,2,128]{2,1,0:T(2,128)S(1)}, u32[]{:S(2)}, u32[]{:S(2)}) async-start(f32[32,2,128]{2,1,0:T(2,128)} %bitcast.14), calls=%async_computation.2 | async-start | bytes 65536 | tf_op jit(solution)/shard_map/all_to_all | solution.py:724
  88.7 0.3 collective-permute-start.18
  89.0 1.6 %collective-permute-start.19 = (f32[8,512]{1,0:T(8,128)S(1)}, f32[8,512]{1,0:T(8,128)S(1)}, u32[]{:S(2)}, u32[]{:S(2)}) collective-permute-start(f32[8,512]{1,0:T(8,128)S(1)} %get-tuple-element.80), channel_id=1, source_target_pairs={{1,2},{2,1},{3,0},{0,3},{5,6},{6,5},{7,4},{4,7},{9,10},{10,9},{11,... | collective-permute-start | bytes 49160 | tf_op jit(solution)/shard_map/ppermute | solution.py:625
  90.7 1.6 %collective-permute-done.19.refs_15_ = f32[8,512]{1,0:T(8,128)S(1)} collective-permute-done((f32[8,512]{1,0:T(8,128)S(1)}, f32[8,512]{1,0:T(8,128)S(1)}, u32[]{:S(2)}, u32[]{:S(2)}) %collective-permute-start.19) | collective-permute-done | bytes 16416 | tf_op jit(solution)/shard_map/ppermute | solution.py:625
  92.2 3.7 %all-to-all-done.2 = f32[32,2,128]{2,1,0:T(2,128)S(1)} async-done(((f32[32,2,128]{2,1,0:T(2,128)}), f32[32,2,128]{2,1,0:T(2,128)S(1)}, u32[]{:S(2)}, u32[]{:S(2)}) %all-to-all-start.2) | async-done | bytes 32800 | tf_op jit(solution)/shard_map/all_to_all | solution.py:724
  96.0 6.4 %step2.1 = (f32[32,128]{1,0:T(8,128)S(1)}, f32[8,32,512]{2,1,0:T(8,128)}, f32[8,32,512]{2,1,0:T(8,128)}, f32[8,32,512]{2,1,0:T(8,128)}, f32[8,32,512]{2,1,0:T(8,128)}, /*index=5*/f32[8,32,512]{2,1,0:T(8,128)}) custom-call(s32[9]{0:T(128)S(1)} %stack.60.edge_ref.refs_0_, f32[64,128]{1,0:T(8,128)S(1)} %bitcast.22, f32[64,128]{1,0:T(8,128)S(1)} %bitcast.24, ...), custom_call_target="tpu_custom_call" | custom-call | tf_op jit(solution)/shard_map/step2/pallas_call | solution.py:604
  102.4 9.0 %all_to_all.20 = f32[32,1,128]{2,1,0:T(1,128)S(1)} all-to-all(f32[32,1,128]{2,1,0:T(1,128)S(1)} %bitcast.31), channel_id=1, replica_groups=mesh['gz'=8,'gy'=4] {'gz','gy'}, dimensions={0} | all-to-all | bytes 32768 | tf_op jit(solution)/shard_map/all_to_all | solution.py:724
  111.4 2.8 %finish.1 = (f32[8,32,512]{2,1,0:T(8,128)}, f32[8,32,512]{2,1,0:T(8,128)}) custom-call(f32[64,128]{1,0:T(8,128)S(1)} %bitcast.25, f32[64,128]{1,0:T(8,128)S(1)} %bitcast.27, f32[32,128]{1,0:T(8,128)S(1)} %bitcast.30, f32[8,32,512]{2,1,0:T(8,128)} %get-tuple-element.87.r_hbm, f32[8,32,512]{2,1,0:T(8,128)} %get-tuple-element.88.w_hbm, ...), custom_call_target="tpu_custom_call" | custom-call | tf_op jit(solution)/shard_map/finish/pallas_call | solution.py:604
  (11 shorter events, 0.1 us)
Async XLA Ops:
  2.4 9.4 %collective-permute-start.2 = (f32[8,3,512]{2,1,0:T(4,128)S(1)}, f32[8,3,512]{2,1,0:T(4,128)S(1)}, u32[]{:S(2)}, u32[]{:S(2)}) collective-permute-start(f32[8,3,512]{2,1,0:T(4,128)S(1)} %get-tuple-element.49), channel_id=1, source_target_pairs={{0,1},{1,0},{2,3},{3,2},{4,5},{5,4},{6,7},{7,6},{8,9},{9,8},{10,11... | collective-permute-start | bytes 147464 | tf_op jit(solution)/shard_map/ppermute | solution.py:625
  3.0 8.8 %collective-permute-start.3 = (f32[8,3,512]{2,1,0:T(4,128)S(1)}, f32[8,3,512]{2,1,0:T(4,128)S(1)}, u32[]{:S(2)}, u32[]{:S(2)}) collective-permute-start(f32[8,3,512]{2,1,0:T(4,128)S(1)} %get-tuple-element.50), channel_id=1, source_target_pairs={{1,2},{2,1},{3,0},{0,3},{5,6},{6,5},{7,4},{4,7},{9,10},{10,9},{11,... | collective-permute-start | bytes 147464 | tf_op jit(solution)/shard_map/ppermute | solution.py:625
  5.6 21.1 %collective-permute-start = (f32[3,32,512]{2,1,0:T(8,128)S(1)}, f32[3,32,512]{2,1,0:T(8,128)S(1)}, u32[]{:S(2)}, u32[]{:S(2)}) collective-permute-start(f32[3,32,512]{2,1,0:T(8,128)S(1)} %get-tuple-element.47), channel_id=1, source_target_pairs={{0,4},{4,0},{8,12},{12,8},{16,20},{20,16},{24,28},{28,24},{1,5},{5... | collective-permute-start | bytes 589832 | tf_op jit(solution)/shard_map/ppermute | solution.py:625
  7.1 19.6 %collective-permute-start.1 = (f32[3,32,512]{2,1,0:T(8,128)S(1)}, f32[3,32,512]{2,1,0:T(8,128)S(1)}, u32[]{:S(2)}, u32[]{:S(2)}) collective-permute-start(f32[3,32,512]{2,1,0:T(8,128)S(1)} %get-tuple-element.48), channel_id=1, source_target_pairs={{4,8},{8,4},{12,16},{16,12},{20,24},{24,20},{28,0},{0,28},{5,9},{9... | collective-permute-start | bytes 589832 | tf_op jit(solution)/shard_map/ppermute | solution.py:625
  10.6 11.8 %collective-permute-start.7 = (f32[16,640]{1,0:T(8,128)S(1)}, f32[16,640]{1,0:T(8,128)S(1)}, u32[]{:S(2)}, u32[]{:S(2)}) collective-permute-start(f32[16,640]{1,0:T(8,128)S(1)} %get-tuple-element.51), channel_id=1, source_target_pairs={{4,8},{8,4},{12,16},{16,12},{20,24},{24,20},{28,0},{0,28},{5,9},{9... | collective-permute-start | bytes 122888 | tf_op jit(solution)/shard_map/ppermute | solution.py:625
  11.8 7.7 %collective-permute-start.6 = (f32[16,640]{1,0:T(8,128)S(1)}, f32[16,640]{1,0:T(8,128)S(1)}, u32[]{:S(2)}, u32[]{:S(2)}) collective-permute-start(f32[16,640]{1,0:T(8,128)S(1)} %get-tuple-element.51), channel_id=1, source_target_pairs={{0,4},{4,0},{8,12},{12,8},{16,20},{20,16},{24,28},{28,24},{1,5},{5... | collective-permute-start | bytes 122888 | tf_op jit(solution)/shard_map/ppermute | solution.py:625
  11.9 14.8 %collective-permute-start.5 = (f32[2,3,3,512]{3,2,1,0:T(4,128)S(1)}, f32[2,3,3,512]{3,2,1,0:T(4,128)S(1)}, u32[]{:S(2)}, u32[]{:S(2)}) collective-permute-start(f32[2,3,3,512]{3,2,1,0:T(4,128)S(1)} %get-tuple-element.92), channel_id=1, source_target_pairs={{4,8},{8,4},{12,16},{16,12},{20,24},{24,20},{28,0},{0,28},{5,9},{9... | collective-permute-start | bytes 110600 | tf_op jit(solution)/shard_map/ppermute | solution.py:625
  19.5 7.2 %collective-permute-start.4 = (f32[2,3,3,512]{3,2,1,0:T(4,128)S(1)}, f32[2,3,3,512]{3,2,1,0:T(4,128)S(1)}, u32[]{:S(2)}, u32[]{:S(2)}) collective-permute-start(f32[2,3,3,512]{3,2,1,0:T(4,128)S(1)} %get-tuple-element.93), channel_id=1, source_target_pairs={{0,4},{4,0},{8,12},{12,8},{16,20},{20,16},{24,28},{28,24},{1,5},{5... | collective-permute-start | bytes 110600 | tf_op jit(solution)/shard_map/ppermute | solution.py:625
  38.3 14.9 %collective-permute-start.8 = (f32[2,32,512]{2,1,0:T(8,128)S(1)}, f32[2,32,512]{2,1,0:T(8,128)S(1)}, u32[]{:S(2)}, u32[]{:S(2)}) collective-permute-start(f32[2,32,512]{2,1,0:T(8,128)S(1)} %get-tuple-element.53), channel_id=1, source_target_pairs={{0,4},{4,0},{8,12},{12,8},{16,20},{20,16},{24,28},{28,24},{1,5},{5... | collective-permute-start | bytes 393224 | tf_op jit(solution)/shard_map/ppermute | solution.py:625
  38.9 14.4 %collective-permute-start.9 = (f32[2,32,512]{2,1,0:T(8,128)S(1)}, f32[2,32,512]{2,1,0:T(8,128)S(1)}, u32[]{:S(2)}, u32[]{:S(2)}) collective-permute-start(f32[2,32,512]{2,1,0:T(8,128)S(1)} %get-tuple-element.54), channel_id=1, source_target_pairs={{4,8},{8,4},{12,16},{16,12},{20,24},{24,20},{28,0},{0,28},{5,9},{9... | collective-permute-start | bytes 393224 | tf_op jit(solution)/shard_map/ppermute | solution.py:625
  43.4 9.8 %all-to-all-start = ((f32[32,2,128]{2,1,0:T(2,128)}), f32[32,2,128]{2,1,0:T(2,128)S(1)}, u32[]{:S(2)}, u32[]{:S(2)}) async-start(f32[32,2,128]{2,1,0:T(2,128)} %bitcast.10), calls=%async_computation | async-start | bytes 65536 | tf_op jit(solution)/shard_map/all_to_all | solution.py:724
  46.0 1.8 %collective-permute-start.10 = (f32[2,8,512]{2,1,0:T(8,128)S(1)}, f32[2,8,512]{2,1,0:T(8,128)S(1)}, u32[]{:S(2)}, u32[]{:S(2)}) collective-permute-start(f32[2,8,512]{2,1,0:T(8,128)S(1)} %get-tuple-element.55), channel_id=1, source_target_pairs={{0,1},{1,0},{2,3},{3,2},{4,5},{5,4},{6,7},{7,6},{8,9},{9,8},{10,11... | collective-permute-start | bytes 98312 | tf_op jit(solution)/shard_map/ppermute | solution.py:625
  46.2 3.4 %collective-permute-start.11 = (f32[2,8,512]{2,1,0:T(8,128)S(1)}, f32[2,8,512]{2,1,0:T(8,128)S(1)}, u32[]{:S(2)}, u32[]{:S(2)}) collective-permute-start(f32[2,8,512]{2,1,0:T(8,128)S(1)} %get-tuple-element.56), channel_id=1, source_target_pairs={{1,2},{2,1},{3,0},{0,3},{5,6},{6,5},{7,4},{4,7},{9,10},{10,9},{11,... | collective-permute-start | bytes 98312 | tf_op jit(solution)/shard_map/ppermute | solution.py:625
  61.2 13.1 %collective-permute-start.12 = (f32[32,512]{1,0:T(8,128)S(1)}, f32[32,512]{1,0:T(8,128)S(1)}, u32[]{:S(2)}, u32[]{:S(2)}) collective-permute-start(f32[32,512]{1,0:T(8,128)S(1)} %get-tuple-element.69), channel_id=1, source_target_pairs={{0,4},{4,0},{8,12},{12,8},{16,20},{20,16},{24,28},{28,24},{1,5},{5... | collective-permute-start | bytes 196616 | tf_op jit(solution)/shard_map/ppermute | solution.py:625
  61.9 12.4 %collective-permute-start.13 = (f32[32,512]{1,0:T(8,128)S(1)}, f32[32,512]{1,0:T(8,128)S(1)}, u32[]{:S(2)}, u32[]{:S(2)}) collective-permute-start(f32[32,512]{1,0:T(8,128)S(1)} %get-tuple-element.70), channel_id=1, source_target_pairs={{4,8},{8,4},{12,16},{16,12},{20,24},{24,20},{28,0},{0,28},{5,9},{9... | collective-permute-start | bytes 196616 | tf_op jit(solution)/shard_map/ppermute | solution.py:625
  63.3 11.0 %all-to-all-start.1 = ((f32[32,2,128]{2,1,0:T(2,128)}), f32[32,2,128]{2,1,0:T(2,128)S(1)}, u32[]{:S(2)}, u32[]{:S(2)}) async-start(f32[32,2,128]{2,1,0:T(2,128)} %bitcast.12), calls=%async_computation.1 | async-start | bytes 65536 | tf_op jit(solution)/shard_map/all_to_all | solution.py:724
  67.0 2.0 %collective-permute-start.14 = (f32[8,512]{1,0:T(8,128)S(1)}, f32[8,512]{1,0:T(8,128)S(1)}, u32[]{:S(2)}, u32[]{:S(2)}) collective-permute-start(f32[8,512]{1,0:T(8,128)S(1)} %get-tuple-element.71), channel_id=1, source_target_pairs={{0,1},{1,0},{2,3},{3,2},{4,5},{5,4},{6,7},{7,6},{8,9},{9,8},{10,11... | collective-permute-start | bytes 49160 | tf_op jit(solution)/shard_map/ppermute | solution.py:625
  67.4 3.2 %collective-permute-start.15 = (f32[8,512]{1,0:T(8,128)S(1)}, f32[8,512]{1,0:T(8,128)S(1)}, u32[]{:S(2)}, u32[]{:S(2)}) collective-permute-start(f32[8,512]{1,0:T(8,128)S(1)} %get-tuple-element.72), channel_id=1, source_target_pairs={{1,2},{2,1},{3,0},{0,3},{5,6},{6,5},{7,4},{4,7},{9,10},{10,9},{11,... | collective-permute-start | bytes 49160 | tf_op jit(solution)/shard_map/ppermute | solution.py:625
  82.9 13.0 %collective-permute-start.16 = (f32[32,512]{1,0:T(8,128)S(1)}, f32[32,512]{1,0:T(8,128)S(1)}, u32[]{:S(2)}, u32[]{:S(2)}) collective-permute-start(f32[32,512]{1,0:T(8,128)S(1)} %get-tuple-element.77), channel_id=1, source_target_pairs={{0,4},{4,0},{8,12},{12,8},{16,20},{20,16},{24,28},{28,24},{1,5},{5... | collective-permute-start | bytes 196616 | tf_op jit(solution)/shard_map/ppermute | solution.py:625
  83.5 12.4 %collective-permute-start.17 = (f32[32,512]{1,0:T(8,128)S(1)}, f32[32,512]{1,0:T(8,128)S(1)}, u32[]{:S(2)}, u32[]{:S(2)}) collective-permute-start(f32[32,512]{1,0:T(8,128)S(1)} %get-tuple-element.78), channel_id=1, source_target_pairs={{4,8},{8,4},{12,16},{16,12},{20,24},{24,20},{28,0},{0,28},{5,9},{9... | collective-permute-start | bytes 196616 | tf_op jit(solution)/shard_map/ppermute | solution.py:625
  85.0 10.9 %all-to-all-start.2 = ((f32[32,2,128]{2,1,0:T(2,128)}), f32[32,2,128]{2,1,0:T(2,128)S(1)}, u32[]{:S(2)}, u32[]{:S(2)}) async-start(f32[32,2,128]{2,1,0:T(2,128)} %bitcast.14), calls=%async_computation.2 | async-start | bytes 65536 | tf_op jit(solution)/shard_map/all_to_all | solution.py:724
  88.7 2.0 %collective-permute-start.18 = (f32[8,512]{1,0:T(8,128)S(1)}, f32[8,512]{1,0:T(8,128)S(1)}, u32[]{:S(2)}, u32[]{:S(2)}) collective-permute-start(f32[8,512]{1,0:T(8,128)S(1)} %get-tuple-element.79), channel_id=1, source_target_pairs={{0,1},{1,0},{2,3},{3,2},{4,5},{5,4},{6,7},{7,6},{8,9},{9,8},{10,11... | collective-permute-start | bytes 49160 | tf_op jit(solution)/shard_map/ppermute | solution.py:625
  89.0 3.2 %collective-permute-start.19 = (f32[8,512]{1,0:T(8,128)S(1)}, f32[8,512]{1,0:T(8,128)S(1)}, u32[]{:S(2)}, u32[]{:S(2)}) collective-permute-start(f32[8,512]{1,0:T(8,128)S(1)} %get-tuple-element.80), channel_id=1, source_target_pairs={{1,2},{2,1},{3,0},{0,3},{5,6},{6,5},{7,4},{4,7},{9,10},{10,9},{11,... | collective-permute-start | bytes 49160 | tf_op jit(solution)/shard_map/ppermute | solution.py:625

commit v3 on v2

--- a/solution.py
+++ b/solution.py
@@ -7,6 +7,7 @@
 from jax.experimental import pallas as pl
 from jax.experimental.pallas import tpu as pltpu
 from jax.sharding import PartitionSpec as P
+
 
 S_DEV = 4
 B_DEV = 16
@@ -26,6 +27,7 @@
 highest = lax.Precision.HIGHEST
 f32 = jnp.float32
 i32 = jnp.int32
+i8 = jnp.int8
 bf16 = jnp.bfloat16
 
 
@@ -75,15 +77,15 @@
 
 def region_row(value_ref, code_ref):
     planes, rows, _ = value_ref.shape
-    pieces = rows // PIECE
-
-    def step(index, acc):
-        plane = index // pieces
-        piece = pl.ds(pl.multiple_of((index % pieces) * PIECE, PIECE), PIECE)
-        return acc + piece_sums(value_ref[plane, piece, :], code_ref[plane, piece, :])
+
+    def step(plane, acc):
+        code = code_ref[plane].astype(i32)
+        for start in range(0, rows, PIECE):
+            acc = acc + piece_sums(value_ref[plane, start : start + PIECE, :], code[start : start + PIECE])
+        return acc
 
     acc = lax.fori_loop(
-        0, planes * pieces, step, jnp.zeros((2 * GROUPS * PIECE, B_DEV * PIECE), f32), unroll=planes * pieces
+        0, planes, step, jnp.zeros((2 * GROUPS * PIECE, B_DEV * PIECE), f32), unroll=planes
     )
     shape = acc.shape
     kept = jnp.where(iota(shape, 0) % PIECE == iota(shape, 1) % PIECE, acc, 0.0)
@@ -216,9 +218,8 @@
 def setup_kernel(
     edge_ref, z0_in, z1_in, y0_in, y1_in, k0_in, k1_in, frac_hbm, source_hbm, label_hbm, sub_hbm, dest_hbm,
     ez0_ref, ez1_ref, ey0_ref, ey1_ref, send_ref,
-    code_hbm, r_hbm, b_hbm, cz_hbm, cyp_hbm, cym_hbm, cxp_hbm, cxm_hbm, diag_hbm, inv_hbm, mult_hbm,
-    frac_ref, source_ref, label_ref, sub_ref, dest_ref,
-    code_ref, r_ref, b_ref, cz_ref, cyp_ref, cym_ref, cxp_ref, cxm_ref, diag_ref, inv_ref, mult_ref,
+    code_ref, cz_ref, cy_ref, cx_ref, inv_ref, south_ref, r_hbm, diag_hbm,
+    frac_ref, source_ref, label_ref, sub_ref, dest_ref, r_ref, diag_ref, b_ref,
     deep_ref, nz_ref, flat_ref, kap_ref, fz_ref, work_ref, in_sems, out_sems,
 ):
     planes, rows, width = frac_ref.shape
@@ -341,13 +342,11 @@
         g = rhs + mult * g_before
         r_ref[plane] = rhs
         diag_ref[plane] = diagonal
-        mult_ref[plane] = mult
         inv_ref[plane] = inv
         work_ref[plane] = g
-        cyp_ref[plane] = jnp.where((row_mid == rows - 1) & last_y, 0.0, cyp)
-        cym_ref[plane] = jnp.where((row_mid == 0) & first_y, 0.0, cym)
-        cxp_ref[plane] = jnp.where(lane_mid == width - 1, 0.0, cxp)
-        cxm_ref[plane] = jnp.where(lane_mid == 0, 0.0, cxm)
+        cy_ref[plane] = jnp.where((row_mid == rows - 1) & last_y, 0.0, cyp)
+        south_ref[pl.ds(plane, 1), :] = jnp.where(first_y, 0.0, cym[0:1, :])
+        cx_ref[plane] = jnp.where(lane_mid == width - 1, 0.0, cxp)
         label = label_ref[plane]
         offset = label - base
         below = offset < 0
@@ -355,7 +354,7 @@
         group = jnp.where(below, 1, jnp.where(above, 3, 2))
         inner = jnp.where(below, offset + stride, jnp.where(above, offset - stride, offset))
         code = jnp.where(label >= 0, group * B_DEV + inner, sub_ref[plane] - sub_base)
-        code_ref[plane] = code & (CODES - 1)
+        code_ref[plane] = (code & (CODES - 1)).astype(i8)
         return (inv, g)
 
     blank = jnp.zeros((rows, width), f32)
@@ -370,15 +369,15 @@
     lax.fori_loop(0, planes, backward, blank)
     cz_ref[0] = jnp.where(first_z, 0.0, cz_ref[0])
     cz_ref[planes] = jnp.where(last_z, 0.0, cz_ref[planes])
-    pairs = [
-        (code_ref, code_hbm), (r_ref, r_hbm), (b_ref, b_hbm), (cz_ref, cz_hbm), (cyp_ref, cyp_hbm), (cym_ref, cym_hbm),
-        (cxp_ref, cxp_hbm), (cxm_ref, cxm_hbm), (diag_ref, diag_hbm), (inv_ref, inv_hbm), (mult_ref, mult_hbm),
+    writes = [
+        pltpu.make_async_copy(r_ref, r_hbm, out_sems.at[0]), pltpu.make_async_copy(diag_ref, diag_hbm, out_sems.at[1])
     ]
-    writes = [pltpu.make_async_copy(a, b, out_sems.at[i]) for i, (a, b) in enumerate(pairs)]
     start_all(writes)
     write_edges(even_z, even_y, b_ref, [ez0_ref.at[0], ez1_ref.at[0]], [ey0_ref.at[0], ey1_ref.at[0]])
+    for plane in range(planes):
+        label_ref[plane] = code_ref[plane].astype(i32)
     write_edges(
-        even_z, even_y, code_ref, [ez0_ref.at[1], ez1_ref.at[1]], [ey0_ref.at[1], ey1_ref.at[1]],
+        even_z, even_y, label_ref, [ez0_ref.at[1], ez1_ref.at[1]], [ey0_ref.at[1], ey1_ref.at[1]],
         convert=lambda value: value.astype(f32),
     )
     send_ref[...] = coarse_parts(region_row(r_ref, code_ref), dest_ref)
@@ -423,31 +422,27 @@
     (edge_ref,) = take(1)
     parts = take(stage + 1)
     halos = [take(4) for _ in range(stage + 1)]
+    code_ref, cz_ref, cy_ref, cx_ref, inv_ref, south_ref = take(6)
     last = stage == 2
-    states = (("b", "r"), ("b", "u0", "r", "w0", "z0"), ("b", "u0", "u1", "r", "w0", "w1", "z0", "z1"))[stage]
-    first_names = ("code", "b") + tuple(name for name in states if name[0] == "u")
-    later_names = tuple(name for name in states if name not in first_names)
-    matrix_names = ("cz", "cyp", "cym", "cxp", "cxm", "diag") + (() if last else ("inv", "mult", "dest"))
-    names = first_names + matrix_names[:6] + later_names + matrix_names[6:]
+    names = (("r",), ("r", "w0", "z0"), ("r", "w1", "w0", "z1", "z0"))[stage] + (("diag",) if last else ("diag", "dest"))
     sources = dict(zip(names, take(len(names))))
-    out_names = (("z", "w", "u"), ("z", "w", "u", "bn", "rn"), ("z", "w", "p", "s", "rn"))[stage]
+    out_names = (("z", "w"), ("rn", "z", "w"), ("rn", "s", "p", "z", "w"))[stage]
     if not last:
         edges_z, edges_y = take(2), take(2)
     (send_ref,) = take(1)
     sinks = dict(zip(out_names, take(len(out_names))))
     held = dict(zip(names, take(len(names))))
-    pad_ref, side_ref = take(2)
-    made = {"z": pad_ref.at[pl.ds(1, pad_ref.shape[0] - 2)]}
-    for name in out_names[1:]:
+    pad_ref, side_ref, work_ref, w_ref = take(4)
+    made = {"z": pad_ref.at[pl.ds(1, pad_ref.shape[0] - 2)], "w": w_ref}
+    for name in out_names[:-2]:
         (made[name],) = take(1)
     if not last:
-        (work_ref,) = take(1)
+        (u_ref,) = take(1)
     in_sems, out_sems = take(2)
 
     reads = {name: pltpu.make_async_copy(sources[name], held[name], in_sems.at[i]) for i, name in enumerate(names)}
     start_all(reads.values())
     writes = {name: pltpu.make_async_copy(made[name], sinks[name], out_sems.at[i]) for i, name in enumerate(out_names)}
-    code_ref = held["code"]
     planes, rows, width = code_ref.shape
     even_z, even_y = edge_ref[7] == 0, edge_ref[8] == 0
 
@@ -485,68 +480,72 @@
         )
         side_ref[jnp.where(upper, 1, 0)] = block + found
 
-    for name in first_names:
-        reads[name].wait()
-
-    def direction(plane, carry):
-        block = held["b"][plane]
+    for name in names:
+        if name not in ("diag", "dest"):
+            reads[name].wait()
+    empty = jnp.zeros((rows, width), f32)
+
+    def residual(plane, before):
+        value = held["r"][plane]
         if stage == 1:
-            block = block - alphas[0] * held["u0"][plane]
-            made["bn"][plane] = block
+            value = value - alphas[0] * held["w0"][plane]
+            made["rn"][plane] = value
         if stage == 2:
-            block = block - alphas[1] * (held["u1"][plane] + betas[1] * held["u0"][plane])
-        pad_ref[plane + 1] = block + lookup(near, code_ref[plane])
-        return carry
-
-    lax.fori_loop(0, planes, direction, 0)
+            image = held["w1"][plane] + betas[1] * held["w0"][plane]
+            made["s"][plane] = image
+            made["p"][plane] = held["z1"][plane] + betas[1] * held["z0"][plane]
+            value = value - alphas[1] * image
+            made["rn"][plane] = value
+        value = value + cz_ref[plane] * before
+        work_ref[plane] = value
+        return value * inv_ref[plane]
+
+    lax.fori_loop(0, planes, residual, empty)
+    for name in out_names[:-2]:
+        writes[name].start()
+
+    def direction(step, after):
+        plane = planes - 1 - step
+        value = (work_ref[plane] + cz_ref[plane + 1] * after) * inv_ref[plane]
+        pad_ref[plane + 1] = value + lookup(near, code_ref[plane].astype(i32))
+        return value
+
+    lax.fori_loop(0, planes, direction, empty)
     writes["z"].start()
-    for name in names:
-        if name not in first_names and name != "dest":
-            reads[name].wait()
+    reads["diag"].wait()
     row = iota((rows, width), 0)
 
     def image_plane(plane, carry):
         sums, before = carry
         here = pad_ref[plane + 1]
+        cy, cx = cy_ref[plane], cx_ref[plane]
         north = jnp.where(row == rows - 1, side_ref[1, pl.ds(plane, 1), :], up_rows(here))
-        south = jnp.where(row == 0, side_ref[0, pl.ds(plane, 1), :], down_rows(here))
+        below = south_ref[pl.ds(plane, 1), :] * side_ref[0, pl.ds(plane, 1), :]
+        south = jnp.where(row == 0, below, down_rows(cy * here))
         image = held["diag"][plane] * here - (
-            held["cz"][plane + 1] * pad_ref[plane + 2]
-            + held["cz"][plane] * pad_ref[plane]
-            + held["cyp"][plane] * north
-            + held["cym"][plane] * south
-            + held["cxp"][plane] * next_x(here)
-            + held["cxm"][plane] * prev_x(here)
+            cz_ref[plane + 1] * pad_ref[plane + 2]
+            + cz_ref[plane] * pad_ref[plane]
+            + (cy * north + south)
+            + (cx * next_x(here) + prev_x(cx * here))
         )
-        made["w"][plane] = image
-        residual = held["r"][plane]
+        w_ref[plane] = image
+        new = made["rn"] if stage else held["r"]
+        found = [total(new[plane] * here), total(here * image)]
         if stage == 1:
-            old_z, old_w = held["z0"][plane], held["w0"][plane]
-            residual = residual - alphas[0] * old_w
-            made["rn"][plane] = residual
+            found.append(total(here * held["w0"][plane] + held["z0"][plane] * image))
         if stage == 2:
-            old_z = held["z1"][plane] + betas[1] * held["z0"][plane]
-            old_w = held["w1"][plane] + betas[1] * held["w0"][plane]
-            made["p"][plane] = old_z
-            made["s"][plane] = old_w
-            residual = residual - alphas[1] * old_w
-            made["rn"][plane] = residual
-        found = [total(residual * here), total(here * image)]
-        if stage >= 1:
-            found.append(total(here * old_w + old_z * image))
+            found.append(total(here * made["s"][plane] + made["p"][plane] * image))
         if not last:
-            before = image + held["mult"][plane] * before
+            before = image + cz_ref[plane] * before
             work_ref[plane] = before
+            before = before * inv_ref[plane]
         return tuple(old + new for old, new in zip(sums, found)), before
 
     blank = jnp.zeros((8, LANES), f32)
-    empty = jnp.zeros((rows, width), f32)
     dots, _ = lax.fori_loop(
         0, planes, image_plane, ((blank,) * (3 if stage else 2), blank if last else empty)
     )
-    for name in out_names[1:]:
-        if name != "u":
-            writes[name].start()
+    writes["w"].start()
     row = scalar_row([jnp.sum(value) for value in dots])
     if last:
         send_ref[...] = jnp.broadcast_to(row, send_ref.shape)
@@ -554,15 +553,14 @@
 
         def backward(step, after):
             plane = planes - 1 - step
-            value = (work_ref[plane] + held["cz"][plane + 1] * after) * held["inv"][plane]
-            made["u"][plane] = value
+            value = (work_ref[plane] + cz_ref[plane + 1] * after) * inv_ref[plane]
+            u_ref[plane] = value
             return value
 
         lax.fori_loop(0, planes, backward, empty)
-        writes["u"].start()
-        write_edges(even_z, even_y, made["u"], edges_z, edges_y)
+        write_edges(even_z, even_y, u_ref, edges_z, edges_y)
         reads["dest"].wait()
-        parts = coarse_parts(region_row(made["w"], code_ref), held["dest"])
+        parts = coarse_parts(region_row(w_ref, code_ref), held["dest"])
         send_ref[...] = parts + jnp.where(iota(parts.shape, 0) % 2 == 0, row, 0.0)
     wait_all(writes.values())
 
@@ -590,16 +588,17 @@
     r_write.wait()
 
 
-def call(kernel, outs, scratch, args, name):
-    spaces = {"smem": pltpu.SMEM, "vmem": pltpu.VMEM, "hbm": pltpu.HBM}
+def call(kernel, outs, scratch, args):
+    spaces = {"smem": pltpu.SMEM, "vmem": pltpu.VMEM, "kept": pltpu.VMEM, "hbm": pltpu.HBM}
 
     def specs(items):
         return [pl.BlockSpec(memory_space=spaces[space]) for space, _ in items]
 
     held = sum(4 * math.prod(ref.shape) for ref in scratch)
-    made = [pltpu.HBM(out.shape, out.dtype) if space == "hbm" else out for space, out in outs]
+    places = {"hbm": pltpu.HBM, "kept": pltpu.VMEM}
+    made = [places[space](out.shape, out.dtype) if space in places else out for space, out in outs]
     operands = [
-        pltpu.with_memory_space_constraint(value, pltpu.HBM) if space == "hbm" else value for space, value in args
+        pltpu.with_memory_space_constraint(value, places[space]) if space in places else value for space, value in args
     ]
     return pl.pallas_call(
         kernel,
@@ -608,7 +607,6 @@
         out_specs=specs(outs),
         scratch_shapes=scratch,
         compiler_params=pltpu.CompilerParams(vmem_limit_bytes=held + 12 * 1024 * 1024),
-        name=name,
     )(*operands)
 
 
@@ -625,7 +623,7 @@
     return lax.ppermute(block, axis, swaps(axis, first))
 
 
-def on_device(fraction, source, bubble_label, subdomain, coarse_inverse):
+def solve(fraction, source, bubble_label, subdomain, coarse_inverse):
     planes, rows, width = fraction.shape
     slabs = lax.axis_size("gz")
     columns = lax.axis_size("gy")
@@ -634,7 +632,6 @@
     column = lax.axis_index("gy")
     here = slab * columns + column
     even_z = slab % 2 == 0
-    even_y = column % 2 == 0
     field = jax.ShapeDtypeStruct((planes, rows, width), f32)
 
     def shape(*dims, dtype=f32):
@@ -671,7 +668,6 @@
         tag("vmem", [shape(DEPTH, rows, width)] * 2 + [shape(planes, DEPTH, width)] * 2 + [shape(B_DEV, devices * SPAN)]),
         [vmem(planes, rows, width), vmem(SPAN, devices * SPAN), semaphores(2)],
         tag("smem", [edge]) + tag("hbm", [fraction, coarse_inverse]),
-        "slices",
     )
     coarse_in = [swap(bubbles, "gz", 0), swap(bubbles, "gz", 1)]
     y_in = [swap(sides[0], "gy", 0), swap(sides[1], "gy", 1)]
@@ -685,26 +681,27 @@
         return matrix.reshape(matrix.shape[0], devices, SPAN)
 
     dest_shape = shape(REGIONS, 2 * devices, LANES)
+    spread_in = [spread(m) for m in [coarse_inverse] + coarse_in]
     (dest,) = call(
         partial(destinations_kernel, columns),
         tag("hbm", [dest_shape]),
         [vmem(REGIONS, devices, LANES)] + like([dest_shape]) + [semaphores(1)],
-        tag("smem", [(slab % 2).reshape(1)]) + tag("vmem", [spread(coarse_inverse)] + [spread(m) for m in coarse_in]),
-        "destinations",
-    )
-    codes = shape(planes, rows, width, dtype=i32)
+        tag("smem", [(slab % 2).reshape(1)]) + tag("vmem", spread_in),
+    )
+    codes = shape(planes, rows, width, dtype=i8)
     faces = shape(planes + 1, rows, width)
     inputs = [fraction, source, bubble_label, subdomain, dest]
-    made = [codes, field, field, faces] + [field] * 7
     tall = rows + 8
     wide = shape(2 * devices, LANES)
     first_edges = [shape(2, rows, width)] * 2 + [shape(2, planes, width)] * 2
     later_edges = [shape(rows, width)] * 2 + [shape(planes, width)] * 2
-    *sent, send, code, r0, b0, cz, cyp, cym, cxp, cxm, diag, inv, mult = call(
+    outs = tag("vmem", first_edges + [wide])
+    outs += tag("kept", [codes, faces, field, field, field, shape(planes, width)]) + tag("hbm", [field, field])
+    *sent, send, code, cz, cy, cx, inv, south, r0, diag = call(
         setup_kernel,
-        tag("vmem", first_edges + [wide]) + tag("hbm", made),
+        outs,
         like(inputs)
-        + like(made)
+        + like([field, field, field])
         + [
             vmem(planes + 2 * DEPTH, tall, width),
             vmem(planes + 4, tall, width),
@@ -713,11 +710,11 @@
             vmem(planes + 1, rows, width),
             vmem(planes, rows, width),
             semaphores(len(inputs)),
-            semaphores(len(made)),
+            semaphores(2),
         ],
         tag("smem", [edge]) + tag("vmem", z_in + y_in + corner_in) + tag("hbm", inputs),
-        "setup",
-    )
+    )
+    matrix = [code, cz, cy, cx, inv, south]
 
     def exchange(parts):
         blocks = parts.reshape(devices, -1, LANES)
@@ -726,34 +723,36 @@
     def halos(sent):
         return [swap(sent[0], "gz", 0), swap(sent[1], "gz", 1), swap(sent[2], "gy", 0), swap(sent[3], "gy", 1)]
 
-    def step(stage, parts, edges, first, later):
+    def share(sent, send):
+        edges = halos(sent)
+        parts = [exchange(send)]
+        return edges, parts
+
+    def step(stage, parts, edges, state):
         last = stage == 2
-        matrix = [cz, cyp, cym, cxp, cxm, diag]
-        operands = [code] + first + matrix + later + ([] if last else [inv, mult, dest])
-        outs = [field] * (3, 5, 5)[stage]
+        operands = state + ([diag] if last else [diag, dest])
+        outs = [field] * (2, 3, 5)[stage]
         ends = [] if last else later_edges
-        scratch = like(operands) + [vmem(planes + 2, rows, width), vmem(2, planes, width)] + like(outs[1:])
+        scratch = like(operands) + [vmem(planes + 2, rows, width), vmem(2, planes, width)] + like([field] * len(outs))
         if not last:
-            scratch.append(vmem(planes, rows, width))
+            scratch += like([field])
         scratch += [semaphores(len(operands)), semaphores(len(outs))]
         results = call(
             partial(step_kernel, stage),
             tag("vmem", ends + [shape(devices, LANES) if last else wide]) + tag("hbm", outs),
             scratch,
-            tag("smem", [edge]) + tag("vmem", parts + edges) + tag("hbm", operands),
-            f"step{stage}",
+            tag("smem", [edge]) + tag("vmem", parts + edges) + tag("kept", matrix) + tag("hbm", operands),
         )
         return results[: len(ends)], results[len(ends)], results[len(ends) + 1 :]
 
-    edges = halos(sent)
-    parts = [exchange(send)]
-    sent, send, (z0, w0, u0) = step(0, parts, edges, [b0], [r0])
-    edges = edges + halos(sent)
-    parts = parts + [exchange(send)]
-    sent, send, (z1, w1, u1, b1, r1) = step(1, parts, edges, [b0, u0], [r0, w0, z0])
-    edges = edges + halos(sent)
-    parts = parts + [exchange(send)]
-    _, send, (z2, w2, p1, s1, r2) = step(2, parts, edges, [b1, u0, u1], [r1, w0, w1, z0, z1])
+    edges, parts = share(sent, send)
+    sent, send, (z0, w0) = step(0, parts, edges, [r0])
+    more_edges, more_parts = share(sent, send)
+    edges, parts = edges + more_edges, parts + more_parts
+    sent, send, (r1, z1, w1) = step(1, parts, edges, [r0, w0, z0])
+    more_edges, more_parts = share(sent, send)
+    edges, parts = edges + more_edges, parts + more_parts
+    _, send, (r2, s1, p1, z2, w2) = step(2, parts, edges, [r1, w1, w0, z1, z0])
     parts = parts + [exchange(send)]
     return tuple(
         call(
@@ -761,7 +760,6 @@
             tag("hbm", [field, field]),
             like([field] * 7) + [semaphores(6), semaphores(2)],
             tag("vmem", parts[1:]) + tag("hbm", [r2, w2, s1, z0, p1, z2]),
-            "finish",
         )
     )
 
@@ -775,7 +773,7 @@
         P(("gz", "gy"), None),
     )
     return jax.shard_map(
-        on_device,
+        solve,
         mesh=mesh,
         in_specs=placed,
         out_specs=(P("gz", "gy", None), P("gz", "gy", None)),

time: 115 us -> 111 us (0.965)
  Pallas kernels: 42.9 us -> 39.6 us
    pallas_call x7, Pallas kernels: 42.9 us -> 39.6 us  [call(): pl.pallas_call(kernel, out_shape=made, in_specs=specs(args), out_specs=sp...]
where the time goes in v3:
time: 111 us
  Pallas kernels  39.6 us (36%)
  starting transfers between devices  39.5 us (36%)
  waiting for transfers between devices  20.1 us (18%)
  blocking collectives  8.97 us (8%)
  local copies, waits for them, and re-layouts  1.82 us (2%)
    pallas_call x7, Pallas kernels, call(): pl.pallas_call(kernel, out_shape=made, in_specs=specs(args), out_specs=sp...  39.6 us
    ppermute x20, starting transfers between devices, swap(): return lax.ppermute(block, axis, swaps(axis, first))  29.5 us
    all_to_all x3, waiting for transfers between devices, exchange(): return lax.all_to_all(blocks, ('gz', 'gy'), 0, 0).reshape(parts.shape)  11.2 us
    all_to_all x3, starting transfers between devices, exchange(): return lax.all_to_all(blocks, ('gz', 'gy'), 0, 0).reshape(parts.shape)  9.96 us
    all_to_all x1, blocking collectives, exchange(): return lax.all_to_all(blocks, ('gz', 'gy'), 0, 0).reshape(parts.shape)  8.97 us
    ppermute x20, waiting for transfers between devices, swap(): return lax.ppermute(block, axis, swaps(axis, first))  8.93 us
  transfers between devices with their start and end apart: 23, of which 7 were waited for; matrix products, arithmetic and copies ran while one was open for 2% of the time, Pallas kernels for 3%

profile of v3, /device:TPU:0, one launch (start us, length us, event | category | flops | bytes accessed | tf_op | source)
XLA Modules:
  0.0 110.8 jit_solution(6151520477527262686)
XLA Ops:
  0.7 0.1 stack.60.edge_ref.refs_0_
  0.7 1.7 %shard_map.68 = (f32[3,32,512]{2,1,0:T(8,128)S(1)}, f32[3,32,512]{2,1,0:T(8,128)S(1)}, f32[8,3,512]{2,1,0:T(4,128)S(1)}, f32[8,3,512]{2,1,0:T(4,128)S(1)}, f32[16,640]{1,0:T(8,128)S(1)}) custom-call(s32[9]{0:T(128)S(1)} %stack.60.edge_ref.refs_0_, f32[8,32,512]{2,1,0:T(8,128)} %frac_hbm.3, f32[20,640]{1,0:T(8,128)} %coarse_hbm.1), custom_call_target="tpu_custom_call" | custom-call | tf_op jit(solution)/shard_map/pallas_call | solution.py:603
  2.4 0.6 collective-permute-start.2
  3.0 2.6 %collective-permute-start.3 = (f32[8,3,512]{2,1,0:T(4,128)S(1)}, f32[8,3,512]{2,1,0:T(4,128)S(1)}, u32[]{:S(2)}, u32[]{:S(2)}) collective-permute-start(f32[8,3,512]{2,1,0:T(4,128)S(1)} %get-tuple-element.44), channel_id=1, source_target_pairs={{1,2},{2,1},{3,0},{0,3},{5,6},{6,5},{7,4},{4,7},{9,10},{10,9},{11,... | collective-permute-start | bytes 147464 | tf_op jit(solution)/shard_map/ppermute | solution.py:623
  5.6 1.5 %collective-permute-start = (f32[3,32,512]{2,1,0:T(8,128)S(1)}, f32[3,32,512]{2,1,0:T(8,128)S(1)}, u32[]{:S(2)}, u32[]{:S(2)}) collective-permute-start(f32[3,32,512]{2,1,0:T(8,128)S(1)} %get-tuple-element.41), channel_id=1, source_target_pairs={{0,4},{4,0},{8,12},{12,8},{16,20},{20,16},{24,28},{28,24},{1,5},{5... | collective-permute-start | bytes 589832 | tf_op jit(solution)/shard_map/ppermute | solution.py:623
  7.1 3.5 %collective-permute-start.1 = (f32[3,32,512]{2,1,0:T(8,128)S(1)}, f32[3,32,512]{2,1,0:T(8,128)S(1)}, u32[]{:S(2)}, u32[]{:S(2)}) collective-permute-start(f32[3,32,512]{2,1,0:T(8,128)S(1)} %get-tuple-element.42), channel_id=1, source_target_pairs={{4,8},{8,4},{12,16},{16,12},{20,24},{24,20},{28,0},{0,28},{5,9},{9... | collective-permute-start | bytes 589832 | tf_op jit(solution)/shard_map/ppermute | solution.py:623
  10.6 1.2 %collective-permute-start.7 = (f32[16,640]{1,0:T(8,128)S(1)}, f32[16,640]{1,0:T(8,128)S(1)}, u32[]{:S(2)}, u32[]{:S(2)}) collective-permute-start(f32[16,640]{1,0:T(8,128)S(1)} %get-tuple-element.45), channel_id=1, source_target_pairs={{4,8},{8,4},{12,16},{16,12},{20,24},{24,20},{28,0},{0,28},{5,9},{9... | collective-permute-start | bytes 122888 | tf_op jit(solution)/shard_map/ppermute | solution.py:623
  11.8 0.0 collective-permute-done.2.y0_in
  11.9 3.6 %collective-permute-start.5 = (f32[2,3,3,512]{3,2,1,0:T(4,128)S(1)}, f32[2,3,3,512]{3,2,1,0:T(4,128)S(1)}, u32[]{:S(2)}, u32[]{:S(2)}) collective-permute-start(f32[2,3,3,512]{3,2,1,0:T(4,128)S(1)} %get-tuple-element.80), channel_id=1, source_target_pairs={{4,8},{8,4},{12,16},{16,12},{20,24},{24,20},{28,0},{0,28},{5,9},{9... | collective-permute-start | bytes 110600 | tf_op jit(solution)/shard_map/ppermute | solution.py:623
  15.5 4.0 %collective-permute-done.6 = f32[16,640]{1,0:T(8,128)S(1)} collective-permute-done((f32[16,640]{1,0:T(8,128)S(1)}, f32[16,640]{1,0:T(8,128)S(1)}, u32[]{:S(2)}, u32[]{:S(2)}) %collective-permute-start.6) | collective-permute-done | bytes 40992 | tf_op jit(solution)/shard_map/ppermute | solution.py:623
  19.5 1.5 %collective-permute-start.4 = (f32[2,3,3,512]{3,2,1,0:T(4,128)S(1)}, f32[2,3,3,512]{3,2,1,0:T(4,128)S(1)}, u32[]{:S(2)}, u32[]{:S(2)}) collective-permute-start(f32[2,3,3,512]{3,2,1,0:T(4,128)S(1)} %get-tuple-element.81), channel_id=1, source_target_pairs={{0,4},{4,0},{8,12},{12,8},{16,20},{20,16},{24,28},{28,24},{1,5},{5... | collective-permute-start | bytes 110600 | tf_op jit(solution)/shard_map/ppermute | solution.py:623
  21.0 1.2 %reshape.38.own_ref = f32[20,32,20]{2,1,0:T(8,128)S(1)} reshape(f32[20,640]{1,0:T(8,128)} %coarse_hbm.1) | data formatting | bytes 102400 | tf_op jit(solution)/shard_map/reshape | solution.py:681
  22.2 0.3 reshape.39.near_ref
  22.5 0.3 reshape.40.far_ref
  22.8 3.9 %shard_map.69.dest_hbm.refs_14_.refs_21_ = f32[52,64,128]{2,1,0:T(8,128)} custom-call(s32[1]{0:T(128)} %bitcast.6.pair_ref, f32[20,32,20]{2,1,0:T(8,128)S(1)} %reshape.38.own_ref, f32[16,32,20]{2,1,0:T(8,128)S(1)} %reshape.39.near_ref, f32[16,32,20]{2,1,0:T(8,128)S(1)} %reshape.40.far_ref), custom_call_target="tpu_custom_call" | custom-call | tf_op jit(solution)/shard_map/pallas_call | solution.py:603
  26.6 0.0 collective-permute-done.5.k1_in
  26.6 0.0 collective-permute-done.4.k0_in
  26.7 10.5 %shard_map.70 = (f32[2,32,512]{2,1,0:T(8,128)S(1)}, f32[2,32,512]{2,1,0:T(8,128)S(1)}, f32[2,8,512]{2,1,0:T(8,128)S(1)}, f32[2,8,512]{2,1,0:T(8,128)S(1)}, f32[6...) custom-call(s32[9]{0:T(128)S(1)} %stack.60.edge_ref.refs_0_, ...), custom_call_target="tpu_custom_call" | custom-call | tf_op jit(solution)/shard_map/pallas_call | solution.py:603
  37.2 0.6 collective-permute-start.8
  37.8 4.6 %collective-permute-start.9 = (f32[2,32,512]{2,1,0:T(8,128)S(1)}, f32[2,32,512]{2,1,0:T(8,128)S(1)}, u32[]{:S(2)}, u32[]{:S(2)}) collective-permute-start(f32[2,32,512]{2,1,0:T(8,128)S(1)} %get-tuple-element.48), channel_id=1, source_target_pairs={{4,8},{8,4},{12,16},{16,12},{20,24},{24,20},{28,0},{0,28},{5,9},{9... | collective-permute-start | bytes 393224 | tf_op jit(solution)/shard_map/ppermute | solution.py:623
  42.3 2.6 %all-to-all-start = ((f32[32,2,128]{2,1,0:T(2,128)}), f32[32,2,128]{2,1,0:T(2,128)S(1)}, u32[]{:S(2)}, u32[]{:S(2)}) async-start(f32[32,2,128]{2,1,0:T(2,128)} %bitcast.10), calls=%async_computation | async-start | bytes 65536 | tf_op jit(solution)/shard_map/all_to_all | solution.py:721
  44.9 0.2 collective-permute-start.10
  45.1 1.6 %collective-permute-start.11 = (f32[2,8,512]{2,1,0:T(8,128)S(1)}, f32[2,8,512]{2,1,0:T(8,128)S(1)}, u32[]{:S(2)}, u32[]{:S(2)}) collective-permute-start(f32[2,8,512]{2,1,0:T(8,128)S(1)} %get-tuple-element.50), channel_id=1, source_target_pairs={{1,2},{2,1},{3,0},{0,3},{5,6},{6,5},{7,4},{4,7},{9,10},{10,9},{11,... | collective-permute-start | bytes 98312 | tf_op jit(solution)/shard_map/ppermute | solution.py:623
  46.7 0.0 collective-permute-done.10.refs_4_.refs_5_.refs_6_
  46.7 1.7 %collective-permute-done.11.refs_5_.refs_6_.refs_7_ = f32[2,8,512]{2,1,0:T(8,128)S(1)} collective-permute-done((f32[2,8,512]{2,1,0:T(8,128)S(1)}, f32[2,8,512]{2,1,0:T(8,128)S(1)}, u32[]{:S(2)}, u32[]{:S(2)}) %collective-permute-start.11) | collective-permute-done | bytes 32800 | tf_op jit(solution)/shard_map/ppermute | solution.py:623
  48.5 3.7 %all-to-all-done = f32[32,2,128]{2,1,0:T(2,128)S(1)} async-done(((f32[32,2,128]{2,1,0:T(2,128)}), f32[32,2,128]{2,1,0:T(2,128)S(1)}, u32[]{:S(2)}, u32[]{:S(2)}) %all-to-all-start) | async-done | bytes 32800 | tf_op jit(solution)/shard_map/all_to_all | solution.py:721
  52.2 0.0 collective-permute-done.8.refs_2_.refs_3_.refs_4_
  52.2 0.0 collective-permute-done.9.refs_3_.refs_4_.refs_5_
  52.2 7.3 %shard_map.71 = (f32[32,512]{1,0:T(8,128)S(1)}, f32[32,512]{1,0:T(8,128)S(1)}, f32[8,512]{1,0:T(8,128)S(1)}, f32[8,512]{1,0:T(8,128)S(1)}, f32[64,128]{1,0:T(8,1...) custom-call(s32[9]{0:T(128)S(1)} %stack.60.edge_ref.refs_0_, f32[64,128]{1,0:T(8,128)S(1)} %bitcast.20, ...), custom_call_target="tpu_custom_call" | custom-call | tf_op jit(solution)/shard_map/pallas_call | solution.py:603
  59.5 0.6 collective-permute-start.12
  60.1 1.4 %collective-permute-start.13 = (f32[32,512]{1,0:T(8,128)S(1)}, f32[32,512]{1,0:T(8,128)S(1)}, u32[]{:S(2)}, u32[]{:S(2)}) collective-permute-start(f32[32,512]{1,0:T(8,128)S(1)} %get-tuple-element.61), channel_id=1, source_target_pairs={{4,8},{8,4},{12,16},{16,12},{20,24},{24,20},{28,0},{0,28},{5,9},{9... | collective-permute-start | bytes 196616 | tf_op jit(solution)/shard_map/ppermute | solution.py:623
  61.5 3.7 %all-to-all-start.1 = ((f32[32,2,128]{2,1,0:T(2,128)}), f32[32,2,128]{2,1,0:T(2,128)S(1)}, u32[]{:S(2)}, u32[]{:S(2)}) async-start(f32[32,2,128]{2,1,0:T(2,128)} %bitcast.12), calls=%async_computation.1 | async-start | bytes 65536 | tf_op jit(solution)/shard_map/all_to_all | solution.py:721
  65.3 0.3 collective-permute-start.14
  65.6 1.6 %collective-permute-start.15 = (f32[8,512]{1,0:T(8,128)S(1)}, f32[8,512]{1,0:T(8,128)S(1)}, u32[]{:S(2)}, u32[]{:S(2)}) collective-permute-start(f32[8,512]{1,0:T(8,128)S(1)} %get-tuple-element.63), channel_id=1, source_target_pairs={{1,2},{2,1},{3,0},{0,3},{5,6},{6,5},{7,4},{4,7},{9,10},{10,9},{11,... | collective-permute-start | bytes 49160 | tf_op jit(solution)/shard_map/ppermute | solution.py:623
  67.2 0.0 collective-permute-done.14.refs_9_.refs_10_
  67.2 1.6 %collective-permute-done.15.refs_10_.refs_11_ = f32[8,512]{1,0:T(8,128)S(1)} collective-permute-done((f32[8,512]{1,0:T(8,128)S(1)}, f32[8,512]{1,0:T(8,128)S(1)}, u32[]{:S(2)}, u32[]{:S(2)}) %collective-permute-start.15) | collective-permute-done | bytes 16416 | tf_op jit(solution)/shard_map/ppermute | solution.py:623
  68.8 3.7 %all-to-all-done.1 = f32[32,2,128]{2,1,0:T(2,128)S(1)} async-done(((f32[32,2,128]{2,1,0:T(2,128)}), f32[32,2,128]{2,1,0:T(2,128)S(1)}, u32[]{:S(2)}, u32[]{:S(2)}) %all-to-all-start.1) | async-done | bytes 32800 | tf_op jit(solution)/shard_map/all_to_all | solution.py:721
  72.5 7.9 %shard_map.72 = (f32[32,512]{1,0:T(8,128)S(1)}, f32[32,512]{1,0:T(8,128)S(1)}, f32[8,512]{1,0:T(8,128)S(1)}, f32[8,512]{1,0:T(8,128)S(1)}, f32[64,128]{1,0:T(8,1...) custom-call(s32[9]{0:T(128)S(1)} %stack.60.edge_ref.refs_0_, f32[64,128]{1,0:T(8,128)S(1)} %bitcast.21, ...), custom_call_target="tpu_custom_call" | custom-call | tf_op jit(solution)/shard_map/pallas_call | solution.py:603
  80.4 0.6 collective-permute-start.16
  81.1 1.5 %collective-permute-start.17 = (f32[32,512]{1,0:T(8,128)S(1)}, f32[32,512]{1,0:T(8,128)S(1)}, u32[]{:S(2)}, u32[]{:S(2)}) collective-permute-start(f32[32,512]{1,0:T(8,128)S(1)} %get-tuple-element.68), channel_id=1, source_target_pairs={{4,8},{8,4},{12,16},{16,12},{20,24},{24,20},{28,0},{0,28},{5,9},{9... | collective-permute-start | bytes 196616 | tf_op jit(solution)/shard_map/ppermute | solution.py:623
  82.6 3.7 %all-to-all-start.2 = ((f32[32,2,128]{2,1,0:T(2,128)}), f32[32,2,128]{2,1,0:T(2,128)S(1)}, u32[]{:S(2)}, u32[]{:S(2)}) async-start(f32[32,2,128]{2,1,0:T(2,128)} %bitcast.14), calls=%async_computation.2 | async-start | bytes 65536 | tf_op jit(solution)/shard_map/all_to_all | solution.py:721
  86.2 0.3 collective-permute-start.18
  86.6 1.6 %collective-permute-start.19 = (f32[8,512]{1,0:T(8,128)S(1)}, f32[8,512]{1,0:T(8,128)S(1)}, u32[]{:S(2)}, u32[]{:S(2)}) collective-permute-start(f32[8,512]{1,0:T(8,128)S(1)} %get-tuple-element.70), channel_id=1, source_target_pairs={{1,2},{2,1},{3,0},{0,3},{5,6},{6,5},{7,4},{4,7},{9,10},{10,9},{11,... | collective-permute-start | bytes 49160 | tf_op jit(solution)/shard_map/ppermute | solution.py:623
  88.2 1.6 %collective-permute-done.19.refs_15_ = f32[8,512]{1,0:T(8,128)S(1)} collective-permute-done((f32[8,512]{1,0:T(8,128)S(1)}, f32[8,512]{1,0:T(8,128)S(1)}, u32[]{:S(2)}, u32[]{:S(2)}) %collective-permute-start.19) | collective-permute-done | bytes 16416 | tf_op jit(solution)/shard_map/ppermute | solution.py:623
  89.8 3.7 %all-to-all-done.2 = f32[32,2,128]{2,1,0:T(2,128)S(1)} async-done(((f32[32,2,128]{2,1,0:T(2,128)}), f32[32,2,128]{2,1,0:T(2,128)S(1)}, u32[]{:S(2)}, u32[]{:S(2)}) %all-to-all-start.2) | async-done | bytes 32800 | tf_op jit(solution)/shard_map/all_to_all | solution.py:721
  93.5 5.5 %shard_map.73 = (f32[32,128]{1,0:T(8,128)S(1)}, f32[8,32,512]{2,1,0:T(8,128)}, f32[8,32,512]{2,1,0:T(8,128)}, f32[8,32,512]{2,1,0:T(8,128)}, f32[8,32,512]{2,1,0:T(8,128)}, /*index=5*/f32[8,32,512]{2,1,0:T(8,128)}) custom-call(s32[9]{0:T(128)S(1)} %stack.60.edge_ref.refs_0_, f32[64,128]{1,0:T(8,128)S(1)} %bitcast.22, f32[64,128]{1,0:T(8,128)S(1)} %bitcast.24, ...), custom_call_target="tpu_custom_call" | custom-call | tf_op jit(solution)/shard_map/pallas_call | solution.py:603
  99.0 9.0 %all_to_all.20 = f32[32,1,128]{2,1,0:T(1,128)S(1)} all-to-all(f32[32,1,128]{2,1,0:T(1,128)S(1)} %bitcast.31), channel_id=1, replica_groups=mesh['gz'=8,'gy'=4] {'gz','gy'}, dimensions={0} | all-to-all | bytes 32768 | tf_op jit(solution)/shard_map/all_to_all | solution.py:721
  108.0 2.8 %shard_map.74 = (f32[8,32,512]{2,1,0:T(8,128)}, f32[8,32,512]{2,1,0:T(8,128)}) custom-call(f32[64,128]{1,0:T(8,128)S(1)} %bitcast.25, f32[64,128]{1,0:T(8,128)S(1)} %bitcast.27, f32[32,128]{1,0:T(8,128)S(1)} %bitcast.30, f32[8,32,512]{2,1,0:T(8,128)} %get-tuple-element.75.r_hbm, f32[8,32,512]{2,1,0:T(8,128)} %get-tuple-element.76.w_hbm, ...), custom_call_target="tpu_custom_call" | custom-call | tf_op jit(solution)/shard_map/pallas_call | solution.py:603
  (11 shorter events, 0.1 us)
Async XLA Ops:
  2.4 9.4 %collective-permute-start.2 = (f32[8,3,512]{2,1,0:T(4,128)S(1)}, f32[8,3,512]{2,1,0:T(4,128)S(1)}, u32[]{:S(2)}, u32[]{:S(2)}) collective-permute-start(f32[8,3,512]{2,1,0:T(4,128)S(1)} %get-tuple-element.43), channel_id=1, source_target_pairs={{0,1},{1,0},{2,3},{3,2},{4,5},{5,4},{6,7},{7,6},{8,9},{9,8},{10,11... | collective-permute-start | bytes 147464 | tf_op jit(solution)/shard_map/ppermute | solution.py:623
  3.0 8.8 %collective-permute-start.3 = (f32[8,3,512]{2,1,0:T(4,128)S(1)}, f32[8,3,512]{2,1,0:T(4,128)S(1)}, u32[]{:S(2)}, u32[]{:S(2)}) collective-permute-start(f32[8,3,512]{2,1,0:T(4,128)S(1)} %get-tuple-element.44), channel_id=1, source_target_pairs={{1,2},{2,1},{3,0},{0,3},{5,6},{6,5},{7,4},{4,7},{9,10},{10,9},{11,... | collective-permute-start | bytes 147464 | tf_op jit(solution)/shard_map/ppermute | solution.py:623
  5.6 21.1 %collective-permute-start = (f32[3,32,512]{2,1,0:T(8,128)S(1)}, f32[3,32,512]{2,1,0:T(8,128)S(1)}, u32[]{:S(2)}, u32[]{:S(2)}) collective-permute-start(f32[3,32,512]{2,1,0:T(8,128)S(1)} %get-tuple-element.41), channel_id=1, source_target_pairs={{0,4},{4,0},{8,12},{12,8},{16,20},{20,16},{24,28},{28,24},{1,5},{5... | collective-permute-start | bytes 589832 | tf_op jit(solution)/shard_map/ppermute | solution.py:623
  7.1 19.6 %collective-permute-start.1 = (f32[3,32,512]{2,1,0:T(8,128)S(1)}, f32[3,32,512]{2,1,0:T(8,128)S(1)}, u32[]{:S(2)}, u32[]{:S(2)}) collective-permute-start(f32[3,32,512]{2,1,0:T(8,128)S(1)} %get-tuple-element.42), channel_id=1, source_target_pairs={{4,8},{8,4},{12,16},{16,12},{20,24},{24,20},{28,0},{0,28},{5,9},{9... | collective-permute-start | bytes 589832 | tf_op jit(solution)/shard_map/ppermute | solution.py:623
  10.6 11.8 %collective-permute-start.7 = (f32[16,640]{1,0:T(8,128)S(1)}, f32[16,640]{1,0:T(8,128)S(1)}, u32[]{:S(2)}, u32[]{:S(2)}) collective-permute-start(f32[16,640]{1,0:T(8,128)S(1)} %get-tuple-element.45), channel_id=1, source_target_pairs={{4,8},{8,4},{12,16},{16,12},{20,24},{24,20},{28,0},{0,28},{5,9},{9... | collective-permute-start | bytes 122888 | tf_op jit(solution)/shard_map/ppermute | solution.py:623
  11.8 7.7 %collective-permute-start.6 = (f32[16,640]{1,0:T(8,128)S(1)}, f32[16,640]{1,0:T(8,128)S(1)}, u32[]{:S(2)}, u32[]{:S(2)}) collective-permute-start(f32[16,640]{1,0:T(8,128)S(1)} %get-tuple-element.45), channel_id=1, source_target_pairs={{0,4},{4,0},{8,12},{12,8},{16,20},{20,16},{24,28},{28,24},{1,5},{5... | collective-permute-start | bytes 122888 | tf_op jit(solution)/shard_map/ppermute | solution.py:623
  11.9 14.8 %collective-permute-start.5 = (f32[2,3,3,512]{3,2,1,0:T(4,128)S(1)}, f32[2,3,3,512]{3,2,1,0:T(4,128)S(1)}, u32[]{:S(2)}, u32[]{:S(2)}) collective-permute-start(f32[2,3,3,512]{3,2,1,0:T(4,128)S(1)} %get-tuple-element.80), channel_id=1, source_target_pairs={{4,8},{8,4},{12,16},{16,12},{20,24},{24,20},{28,0},{0,28},{5,9},{9... | collective-permute-start | bytes 110600 | tf_op jit(solution)/shard_map/ppermute | solution.py:623
  19.5 7.2 %collective-permute-start.4 = (f32[2,3,3,512]{3,2,1,0:T(4,128)S(1)}, f32[2,3,3,512]{3,2,1,0:T(4,128)S(1)}, u32[]{:S(2)}, u32[]{:S(2)}) collective-permute-start(f32[2,3,3,512]{3,2,1,0:T(4,128)S(1)} %get-tuple-element.81), channel_id=1, source_target_pairs={{0,4},{4,0},{8,12},{12,8},{16,20},{20,16},{24,28},{28,24},{1,5},{5... | collective-permute-start | bytes 110600 | tf_op jit(solution)/shard_map/ppermute | solution.py:623
  37.2 15.0 %collective-permute-start.8 = (f32[2,32,512]{2,1,0:T(8,128)S(1)}, f32[2,32,512]{2,1,0:T(8,128)S(1)}, u32[]{:S(2)}, u32[]{:S(2)}) collective-permute-start(f32[2,32,512]{2,1,0:T(8,128)S(1)} %get-tuple-element.47), channel_id=1, source_target_pairs={{0,4},{4,0},{8,12},{12,8},{16,20},{20,16},{24,28},{28,24},{1,5},{5... | collective-permute-start | bytes 393224 | tf_op jit(solution)/shard_map/ppermute | solution.py:623
  37.8 14.4 %collective-permute-start.9 = (f32[2,32,512]{2,1,0:T(8,128)S(1)}, f32[2,32,512]{2,1,0:T(8,128)S(1)}, u32[]{:S(2)}, u32[]{:S(2)}) collective-permute-start(f32[2,32,512]{2,1,0:T(8,128)S(1)} %get-tuple-element.48), channel_id=1, source_target_pairs={{4,8},{8,4},{12,16},{16,12},{20,24},{24,20},{28,0},{0,28},{5,9},{9... | collective-permute-start | bytes 393224 | tf_op jit(solution)/shard_map/ppermute | solution.py:623
  42.3 9.8 %all-to-all-start = ((f32[32,2,128]{2,1,0:T(2,128)}), f32[32,2,128]{2,1,0:T(2,128)S(1)}, u32[]{:S(2)}, u32[]{:S(2)}) async-start(f32[32,2,128]{2,1,0:T(2,128)} %bitcast.10), calls=%async_computation | async-start | bytes 65536 | tf_op jit(solution)/shard_map/all_to_all | solution.py:721
  44.9 1.8 %collective-permute-start.10 = (f32[2,8,512]{2,1,0:T(8,128)S(1)}, f32[2,8,512]{2,1,0:T(8,128)S(1)}, u32[]{:S(2)}, u32[]{:S(2)}) collective-permute-start(f32[2,8,512]{2,1,0:T(8,128)S(1)} %get-tuple-element.49), channel_id=1, source_target_pairs={{0,1},{1,0},{2,3},{3,2},{4,5},{5,4},{6,7},{7,6},{8,9},{9,8},{10,11... | collective-permute-start | bytes 98312 | tf_op jit(solution)/shard_map/ppermute | solution.py:623
  45.1 3.4 %collective-permute-start.11 = (f32[2,8,512]{2,1,0:T(8,128)S(1)}, f32[2,8,512]{2,1,0:T(8,128)S(1)}, u32[]{:S(2)}, u32[]{:S(2)}) collective-permute-start(f32[2,8,512]{2,1,0:T(8,128)S(1)} %get-tuple-element.50), channel_id=1, source_target_pairs={{1,2},{2,1},{3,0},{0,3},{5,6},{6,5},{7,4},{4,7},{9,10},{10,9},{11,... | collective-permute-start | bytes 98312 | tf_op jit(solution)/shard_map/ppermute | solution.py:623
  59.5 13.1 %collective-permute-start.12 = (f32[32,512]{1,0:T(8,128)S(1)}, f32[32,512]{1,0:T(8,128)S(1)}, u32[]{:S(2)}, u32[]{:S(2)}) collective-permute-start(f32[32,512]{1,0:T(8,128)S(1)} %get-tuple-element.60), channel_id=1, source_target_pairs={{0,4},{4,0},{8,12},{12,8},{16,20},{20,16},{24,28},{28,24},{1,5},{5... | collective-permute-start | bytes 196616 | tf_op jit(solution)/shard_map/ppermute | solution.py:623
  60.1 12.4 %collective-permute-start.13 = (f32[32,512]{1,0:T(8,128)S(1)}, f32[32,512]{1,0:T(8,128)S(1)}, u32[]{:S(2)}, u32[]{:S(2)}) collective-permute-start(f32[32,512]{1,0:T(8,128)S(1)} %get-tuple-element.61), channel_id=1, source_target_pairs={{4,8},{8,4},{12,16},{16,12},{20,24},{24,20},{28,0},{0,28},{5,9},{9... | collective-permute-start | bytes 196616 | tf_op jit(solution)/shard_map/ppermute | solution.py:623
  61.5 11.0 %all-to-all-start.1 = ((f32[32,2,128]{2,1,0:T(2,128)}), f32[32,2,128]{2,1,0:T(2,128)S(1)}, u32[]{:S(2)}, u32[]{:S(2)}) async-start(f32[32,2,128]{2,1,0:T(2,128)} %bitcast.12), calls=%async_computation.1 | async-start | bytes 65536 | tf_op jit(solution)/shard_map/all_to_all | solution.py:721
  65.3 2.0 %collective-permute-start.14 = (f32[8,512]{1,0:T(8,128)S(1)}, f32[8,512]{1,0:T(8,128)S(1)}, u32[]{:S(2)}, u32[]{:S(2)}) collective-permute-start(f32[8,512]{1,0:T(8,128)S(1)} %get-tuple-element.62), channel_id=1, source_target_pairs={{0,1},{1,0},{2,3},{3,2},{4,5},{5,4},{6,7},{7,6},{8,9},{9,8},{10,11... | collective-permute-start | bytes 49160 | tf_op jit(solution)/shard_map/ppermute | solution.py:623
  65.6 3.2 %collective-permute-start.15 = (f32[8,512]{1,0:T(8,128)S(1)}, f32[8,512]{1,0:T(8,128)S(1)}, u32[]{:S(2)}, u32[]{:S(2)}) collective-permute-start(f32[8,512]{1,0:T(8,128)S(1)} %get-tuple-element.63), channel_id=1, source_target_pairs={{1,2},{2,1},{3,0},{0,3},{5,6},{6,5},{7,4},{4,7},{9,10},{10,9},{11,... | collective-permute-start | bytes 49160 | tf_op jit(solution)/shard_map/ppermute | solution.py:623
  80.4 13.1 %collective-permute-start.16 = (f32[32,512]{1,0:T(8,128)S(1)}, f32[32,512]{1,0:T(8,128)S(1)}, u32[]{:S(2)}, u32[]{:S(2)}) collective-permute-start(f32[32,512]{1,0:T(8,128)S(1)} %get-tuple-element.67), channel_id=1, source_target_pairs={{0,4},{4,0},{8,12},{12,8},{16,20},{20,16},{24,28},{28,24},{1,5},{5... | collective-permute-start | bytes 196616 | tf_op jit(solution)/shard_map/ppermute | solution.py:623
  81.1 12.4 %collective-permute-start.17 = (f32[32,512]{1,0:T(8,128)S(1)}, f32[32,512]{1,0:T(8,128)S(1)}, u32[]{:S(2)}, u32[]{:S(2)}) collective-permute-start(f32[32,512]{1,0:T(8,128)S(1)} %get-tuple-element.68), channel_id=1, source_target_pairs={{4,8},{8,4},{12,16},{16,12},{20,24},{24,20},{28,0},{0,28},{5,9},{9... | collective-permute-start | bytes 196616 | tf_op jit(solution)/shard_map/ppermute | solution.py:623
  82.6 10.9 %all-to-all-start.2 = ((f32[32,2,128]{2,1,0:T(2,128)}), f32[32,2,128]{2,1,0:T(2,128)S(1)}, u32[]{:S(2)}, u32[]{:S(2)}) async-start(f32[32,2,128]{2,1,0:T(2,128)} %bitcast.14), calls=%async_computation.2 | async-start | bytes 65536 | tf_op jit(solution)/shard_map/all_to_all | solution.py:721
  86.2 2.0 %collective-permute-start.18 = (f32[8,512]{1,0:T(8,128)S(1)}, f32[8,512]{1,0:T(8,128)S(1)}, u32[]{:S(2)}, u32[]{:S(2)}) collective-permute-start(f32[8,512]{1,0:T(8,128)S(1)} %get-tuple-element.69), channel_id=1, source_target_pairs={{0,1},{1,0},{2,3},{3,2},{4,5},{5,4},{6,7},{7,6},{8,9},{9,8},{10,11... | collective-permute-start | bytes 49160 | tf_op jit(solution)/shard_map/ppermute | solution.py:623
  86.6 3.2 %collective-permute-start.19 = (f32[8,512]{1,0:T(8,128)S(1)}, f32[8,512]{1,0:T(8,128)S(1)}, u32[]{:S(2)}, u32[]{:S(2)}) collective-permute-start(f32[8,512]{1,0:T(8,128)S(1)} %get-tuple-element.70), channel_id=1, source_target_pairs={{1,2},{2,1},{3,0},{0,3},{5,6},{6,5},{7,4},{4,7},{9,10},{10,9},{11,... | collective-permute-start | bytes 49160 | tf_op jit(solution)/shard_map/ppermute | solution.py:623

commit v4 on v3

--- a/solution.py
+++ b/solution.py
@@ -59,14 +59,26 @@
     return jnp.sum(folded.reshape(rows // 8, 8, LANES), axis=0)
 
 
+def digits(code):
+    forms = []
+    rest = code.astype(f32).astype(bf16)
+    bits = []
+    for power in (32, 16, 8, 4, 2, 1):
+        bit = rest if power == 1 else jnp.clip(rest - (power - 1), 0, 1)
+        bits.append(bit)
+        rest = rest - power * bit
+    for high, low in zip(bits[::2], bits[1::2]):
+        no_high, no_low = 1 - high, 1 - low
+        forms.append([no_high * no_low, no_high * low, high * no_low, high * low])
+    return forms
+
+
 def piece_sums(values, code):
-    group = (code // B_DEV).astype(f32).astype(bf16)
-    inner = (code % B_DEV).astype(f32).astype(bf16)
+    groups, outer, inner = digits(code)
     high = values.astype(bf16)
     low = (values - high.astype(f32)).astype(bf16)
-    zero, one = jnp.zeros_like(high), jnp.ones_like(high)
-    left = [jnp.where(group == g, part, zero) for part in (high, low) for g in range(GROUPS)]
-    right = [jnp.where(inner == i, one, zero) for i in range(B_DEV)]
+    left = [group * part for part in (high, low) for group in groups]
+    right = [first * second for first in outer for second in inner]
     return lax.dot_general(
         jnp.concatenate(left, axis=0),
         jnp.concatenate(right, axis=0),
@@ -123,9 +135,22 @@
     )
 
 
+class Place:
+    def __init__(self):
+        slab, column = lax.axis_index("gz"), lax.axis_index("gy")
+        slabs, columns = lax.axis_size("gz"), lax.axis_size("gy")
+        here = slab * columns + column
+        self.first_z, self.last_z = slab == 0, slab == slabs - 1
+        self.first_y, self.last_y = column == 0, column == columns - 1
+        self.base, self.stride, self.sub_base = here * B_DEV, columns * B_DEV, here * S_DEV
+        self.even_z, self.even_y = slab % 2 == 0, column % 2 == 0
+
+
 def start_all(copies):
-    for copy in copies:
-        copy.start()
+    @pl.when(lax.axis_index("gz") >= 0)
+    def _():
+        for copy in copies:
+            copy.start()
 
 
 def wait_all(copies):
@@ -141,12 +166,13 @@
         factor = jnp.take_along_axis(wide, jnp.full((8, LANES), lane, i32), axis=1)[0:1, :]
         return acc + factor * dest_ref[region]
 
-    return lax.fori_loop(0, REGIONS, step, jnp.zeros(dest_ref.shape[1:], f32), unroll=4)
-
-
-def destinations_kernel(columns, pair_ref, own_ref, near_ref, far_ref, dest_hbm, wide_ref, dest_ref, sems):
+    small = dest_ref.shape[1] <= 64
+    return lax.fori_loop(0, REGIONS, step, jnp.zeros(dest_ref.shape[1:], f32), unroll=REGIONS if small else 4)
+
+
+def destinations_kernel(columns, own_ref, near_ref, far_ref, dest_hbm, wide_ref, dest_ref, sems):
     devices = own_ref.shape[1]
-    even_z = pair_ref[0] == 0
+    even_z = Place().even_z
     wide_ref[...] = jnp.zeros(wide_ref.shape, f32)
     low_start = pl.multiple_of(jnp.where(even_z, 2 * B_DEV, 0), B_DEV) + S_DEV
     high_start = pl.multiple_of(jnp.where(even_z, 0, 2 * B_DEV), B_DEV) + S_DEV
@@ -198,14 +224,15 @@
         y_refs[1][plane : plane + 1, :] = jnp.where(even_y, first, last)
 
 
-def slices_kernel(edge_ref, frac_hbm, coarse_hbm, z0_ref, z1_ref, y0_ref, y1_ref, bubble_ref, frac_ref, coarse_ref, sems):
+def slices_kernel(frac_hbm, coarse_hbm, z0_ref, z1_ref, y0_ref, y1_ref, bubble_ref, frac_ref, coarse_ref, sems):
     planes, rows, _ = frac_ref.shape
     copies = [
         pltpu.make_async_copy(frac_hbm, frac_ref, sems.at[0]),
         pltpu.make_async_copy(coarse_hbm, coarse_ref, sems.at[1]),
     ]
     start_all(copies)
-    even_z, even_y = edge_ref[7] == 0, edge_ref[8] == 0
+    place = Place()
+    even_z, even_y = place.even_z, place.even_y
     wait_all(copies)
     bubble_ref[...] = coarse_ref[S_DEV:SPAN, :]
     z0_ref[...] = frac_ref[pl.ds(jnp.where(even_z, planes - DEPTH, 0), DEPTH)]
@@ -216,7 +243,7 @@
 
 
 def setup_kernel(
-    edge_ref, z0_in, z1_in, y0_in, y1_in, k0_in, k1_in, frac_hbm, source_hbm, label_hbm, sub_hbm, dest_hbm,
+    z0_in, z1_in, y0_in, y1_in, k0_in, k1_in, frac_hbm, source_hbm, label_hbm, sub_hbm, dest_hbm,
     ez0_ref, ez1_ref, ey0_ref, ey1_ref, send_ref,
     code_ref, cz_ref, cy_ref, cx_ref, inv_ref, south_ref, r_hbm, diag_hbm,
     frac_ref, source_ref, label_ref, sub_ref, dest_ref, r_ref, diag_ref, b_ref,
@@ -224,9 +251,10 @@
 ):
     planes, rows, width = frac_ref.shape
     tall = rows + 8
-    first_z, last_z, first_y, last_y = (edge_ref[i] == 1 for i in range(4))
-    base, stride, sub_base = edge_ref[4], edge_ref[5], edge_ref[6]
-    even_z, even_y = edge_ref[7] == 0, edge_ref[8] == 0
+    place = Place()
+    first_z, last_z, first_y, last_y = place.first_z, place.last_z, place.first_y, place.last_y
+    base, stride, sub_base = place.base, place.stride, place.sub_base
+    even_z, even_y = place.even_z, place.even_y
     pairs = [(frac_hbm, frac_ref), (label_hbm, label_ref), (sub_hbm, sub_ref), (source_hbm, source_ref), (dest_hbm, dest_ref)]
     reads = [pltpu.make_async_copy(a, b, in_sems.at[i]) for i, (a, b) in enumerate(pairs)]
     start_all(reads)
@@ -239,63 +267,61 @@
     last_plane = jnp.where(last_z, planes, 2 * planes)
 
     def right_of(field):
-        return jnp.where(lane[: field.shape[0]] == width - 1, 0.0, next_x(field))
+        moved = next_x(field)
+        tile = lane[: field.shape[0], :LANES]
+        ended = jnp.where(tile == LANES - 1, 0.0, moved[:, width - LANES :])
+        return jnp.concatenate([moved[:, : width - LANES], ended], axis=1)
 
     def left_of(field):
-        return jnp.where(lane[: field.shape[0]] == 0, 0.0, prev_x(field))
+        moved = prev_x(field)
+        tile = lane[: field.shape[0], :LANES]
+        return jnp.concatenate([jnp.where(tile == 0, 0.0, moved[:, :LANES]), moved[:, LANES:]], axis=1)
 
     deep_ref[:, rows:tall, :] = jnp.zeros((planes + 2 * DEPTH, 8, width), f32)
     near_z = jnp.where(even_z, planes + DEPTH, 0)
     far_z = jnp.where(even_z, 0, planes + DEPTH)
-    deep_ref[pl.ds(near_z, DEPTH), 0:rows, :] = z0_in[...]
-    deep_ref[pl.ds(far_z, DEPTH), 0:rows, :] = z1_in[...]
+    out_near, out_far = jnp.where(even_z, last_z, first_z), jnp.where(even_z, first_z, last_z)
+    deep_ref[pl.ds(near_z, DEPTH), 0:rows, :] = jnp.where(out_near, 0.0, z0_in[...])
+    deep_ref[pl.ds(far_z, DEPTH), 0:rows, :] = jnp.where(out_far, 0.0, z1_in[...])
     high, low = slice(rows, rows + DEPTH), slice(tall - DEPTH, tall)
 
-    def fill_rows(first, second):
-        deep_ref[DEPTH : planes + DEPTH, first, :] = y0_in[...]
-        deep_ref[DEPTH : planes + DEPTH, second, :] = y1_in[...]
-        deep_ref[pl.ds(near_z, DEPTH), first, :] = k0_in[0]
-        deep_ref[pl.ds(near_z, DEPTH), second, :] = k0_in[1]
-        deep_ref[pl.ds(far_z, DEPTH), first, :] = k1_in[0]
-        deep_ref[pl.ds(far_z, DEPTH), second, :] = k1_in[1]
+    def fill_rows(first, second, out_first, out_second):
+        deep_ref[DEPTH : planes + DEPTH, first, :] = jnp.where(out_first, 0.0, y0_in[...])
+        deep_ref[DEPTH : planes + DEPTH, second, :] = jnp.where(out_second, 0.0, y1_in[...])
+        for start, corner, out in ((near_z, k0_in, out_near), (far_z, k1_in, out_far)):
+            deep_ref[pl.ds(start, DEPTH), first, :] = jnp.where(out | out_first, 0.0, corner[0])
+            deep_ref[pl.ds(start, DEPTH), second, :] = jnp.where(out | out_second, 0.0, corner[1])
 
     @pl.when(even_y)
     def _():
-        fill_rows(high, low)
+        fill_rows(high, low, last_y, first_y)
 
     @pl.when(jnp.logical_not(even_y))
     def _():
-        fill_rows(low, high)
+        fill_rows(low, high, first_y, last_y)
 
     reads[0].wait()
     deep_ref[DEPTH : planes + DEPTH, 0:rows, :] = frac_ref[...]
-
-    def mask_plane(index, carry):
-        keep = (index - DEPTH >= first_plane) & (index - DEPTH < last_plane)
-        deep_ref[index] = jnp.where(inside_y & keep, deep_ref[index], 0.0)
-        return carry
-
-    lax.fori_loop(0, planes + 2 * DEPTH, mask_plane, 0)
 
     def normal_plane(index, carry):
         keep = (index - 2 >= first_plane) & (index - 2 < last_plane)
         here = deep_ref[index + 1]
-        gz = 0.5 * (deep_ref[index + 2] - deep_ref[index])
-        gy = 0.5 * (up_rows(here) - down_rows(here))
-        gx = 0.5 * (right_of(here) - left_of(here))
-        scale = jnp.minimum(lax.rsqrt(gz * gz + gy * gy + gx * gx), 1.0 / norm_floor)
+        gz = deep_ref[index + 2] - deep_ref[index]
+        gy = up_rows(here) - down_rows(here)
+        gx = right_of(here) - left_of(here)
+        scale = jnp.minimum(lax.rsqrt(gz * gz + gy * gy + gx * gx), 0.5 / norm_floor)
         scale = jnp.where(inside_y & keep, scale, 0.0)
         ny = gy * scale
         nx = gx * scale
         nz_ref[index] = gz * scale
-        flat_ref[index] = 0.5 * (up_rows(ny) - down_rows(ny)) + 0.5 * (right_of(nx) - left_of(nx))
+        flat_ref[index] = (up_rows(ny) - down_rows(ny)) + (right_of(nx) - left_of(nx))
         return carry
 
     lax.fori_loop(0, planes + 4, normal_plane, 0)
 
     def kappa_plane(index, carry):
         keep = (index - 1 >= first_plane) & (index - 1 < last_plane)
-        value = -(0.5 * (nz_ref[index + 2] - nz_ref[index]) + flat_ref[index + 1])
+        value = -0.5 * ((nz_ref[index + 2] - nz_ref[index]) + flat_ref[index + 1])
         kap_ref[index] = jnp.where(inside_y & keep, value, 0.0)
         return carry
 
@@ -305,7 +331,7 @@
     def z_face(index, carry):
         f_low = deep_ref[index + 2, mid, :]
         f_high = deep_ref[index + 3, mid, :]
-        coef = 2.0 / ((1.0 - gas_drop * f_low) + (1.0 - gas_drop * f_high))
+        coef = 2.0 * pl.reciprocal((1.0 - gas_drop * f_low) + (1.0 - gas_drop * f_high))
         cz_ref[index] = coef
         mean = 0.5 * (kap_ref[index, mid, :] + kap_ref[index + 1, mid, :])
         fz_ref[index] = coef * mean * (f_high - f_low)
@@ -322,13 +348,13 @@
         k = kap_ref[plane + 1]
         d = 1.0 - gas_drop * f
         f_up = up_rows(f)
-        cy = 2.0 / (d + (1.0 - gas_drop * f_up))
+        cy = 2.0 * pl.reciprocal(d + (1.0 - gas_drop * f_up))
         fy = cy * (0.5 * (k + up_rows(k))) * (f_up - f)
         cyp, cym = cy[:rows], down_rows(cy)[:rows]
         sum_y = fy[:rows] - down_rows(fy)[:rows]
         f, k, d = f[:rows], k[:rows], d[:rows]
         f_right = right_of(f)
-        cxp = 2.0 / (d + (1.0 - gas_drop * f_right))
+        cxp = 2.0 * pl.reciprocal(d + (1.0 - gas_drop * f_right))
         fx = cxp * (0.5 * (k + right_of(k))) * (f_right - f)
         outer = jnp.concatenate([2.0 / (d[:, :LANES] + 1.0), jnp.zeros((rows, width - LANES), f32)], axis=1)
         cxm = jnp.where(lane_mid == 0, outer, prev_x(cxp))
@@ -338,7 +364,7 @@
         down = cz_ref[plane]
         diagonal = shift_term + (cz_ref[plane + 1] + down + cyp + cym + cxp + cxm)
         mult = down * inv_before
-        inv = 1.0 / (diagonal - mult * down)
+        inv = pl.reciprocal(diagonal - mult * down)
         g = rhs + mult * g_before
         r_ref[plane] = rhs
         diag_ref[plane] = diagonal
@@ -419,7 +445,6 @@
         del refs[:count]
         return out
 
-    (edge_ref,) = take(1)
     parts = take(stage + 1)
     halos = [take(4) for _ in range(stage + 1)]
     code_ref, cz_ref, cy_ref, cx_ref, inv_ref, south_ref = take(6)
@@ -430,21 +455,28 @@
     if not last:
         edges_z, edges_y = take(2), take(2)
     (send_ref,) = take(1)
-    sinks = dict(zip(out_names, take(len(out_names))))
-    held = dict(zip(names, take(len(names))))
-    pad_ref, side_ref, work_ref, w_ref = take(4)
-    made = {"z": pad_ref.at[pl.ds(1, pad_ref.shape[0] - 2)], "w": w_ref}
-    for name in out_names[:-2]:
-        (made[name],) = take(1)
-    if not last:
-        (u_ref,) = take(1)
-    in_sems, out_sems = take(2)
+    if last:
+        pad_ref, w_ref, *others = take(6)
+        made = dict(zip(("rn", "s", "p", "x"), others))
+        out_names = ()
+        held = dict(zip(names, take(len(names))))
+        side_ref, work_ref, in_sems = take(3)
+        out_sems = None
+    else:
+        sinks = dict(zip(out_names, take(len(out_names))))
+        held = dict(zip(names, take(len(names))))
+        pad_ref, side_ref, work_ref, w_ref = take(4)
+        made = {"z": pad_ref.at[pl.ds(1, pad_ref.shape[0] - 2)], "w": w_ref}
+        for name in out_names[:-2]:
+            (made[name],) = take(1)
+        u_ref, in_sems, out_sems = take(3)
 
     reads = {name: pltpu.make_async_copy(sources[name], held[name], in_sems.at[i]) for i, name in enumerate(names)}
     start_all(reads.values())
     writes = {name: pltpu.make_async_copy(made[name], sinks[name], out_sems.at[i]) for i, name in enumerate(out_names)}
     planes, rows, width = code_ref.shape
-    even_z, even_y = edge_ref[7] == 0, edge_ref[8] == 0
+    place = Place()
+    even_z, even_y = place.even_z, place.even_y
 
     sums = [table_rows(part[...]) for part in parts]
     alphas, betas = scalars_of([row[0:1] for row in sums[1:]])
@@ -493,7 +525,9 @@
         if stage == 2:
             image = held["w1"][plane] + betas[1] * held["w0"][plane]
             made["s"][plane] = image
-            made["p"][plane] = held["z1"][plane] + betas[1] * held["z0"][plane]
+            along = held["z1"][plane] + betas[1] * held["z0"][plane]
+            made["p"][plane] = along
+            made["x"][plane] = alphas[0] * held["z0"][plane] + alphas[1] * along
             value = value - alphas[1] * image
             made["rn"][plane] = value
         value = value + cz_ref[plane] * before
@@ -501,8 +535,7 @@
         return value * inv_ref[plane]
 
     lax.fori_loop(0, planes, residual, empty)
-    for name in out_names[:-2]:
-        writes[name].start()
+    start_all([writes[name] for name in out_names[:-2]])
 
     def direction(step, after):
         plane = planes - 1 - step
@@ -511,7 +544,8 @@
         return value
 
     lax.fori_loop(0, planes, direction, empty)
-    writes["z"].start()
+    if not last:
+        writes["z"].start()
     reads["diag"].wait()
     row = iota((rows, width), 0)
 
@@ -545,7 +579,8 @@
     dots, _ = lax.fori_loop(
         0, planes, image_plane, ((blank,) * (3 if stage else 2), blank if last else empty)
     )
-    writes["w"].start()
+    if not last:
+        writes["w"].start()
     row = scalar_row([jnp.sum(value) for value in dots])
     if last:
         send_ref[...] = jnp.broadcast_to(row, send_ref.shape)
@@ -566,26 +601,23 @@
 
 
 def final_kernel(
-    d0_ref, d1_ref, d2_ref, r_hbm, w_hbm, s_hbm, z0_hbm, p_hbm, z_hbm, x_out, r_out,
-    r_ref, w_ref, s_ref, z0_ref, p_ref, z_ref, x_ref, in_sems, out_sems,
+    d0_ref, d1_ref, d2_ref, z_ref, w_ref, r_ref, s_ref, p_ref, part_ref, x_out, r_out, x_new, r_new, sems
 ):
-    pairs = [(z0_hbm, z0_ref), (p_hbm, p_ref), (z_hbm, z_ref), (r_hbm, r_ref), (w_hbm, w_ref), (s_hbm, s_ref)]
-    reads = [pltpu.make_async_copy(a, b, in_sems.at[i]) for i, (a, b) in enumerate(pairs)]
-    start_all(reads)
     sums = [table_rows(d0_ref[...])[0:1], table_rows(d1_ref[...])[0:1], jnp.sum(d2_ref[...], axis=0, keepdims=True)]
     alphas, betas = scalars_of(sums)
     mixed = alphas[2] * betas[2]
-    along = alphas[1] + mixed
-    wait_all(reads[:3])
-    x_ref[...] = alphas[0] * z0_ref[...] + along * p_ref[...] + alphas[2] * z_ref[...]
-    x_write = pltpu.make_async_copy(x_ref, x_out, out_sems.at[0])
-    x_write.start()
-    wait_all(reads[3:])
-    r_ref[...] = r_ref[...] - (alphas[2] * w_ref[...] + mixed * s_ref[...])
-    r_write = pltpu.make_async_copy(r_ref, r_out, out_sems.at[1])
-    r_write.start()
-    x_write.wait()
-    r_write.wait()
+    planes = r_ref.shape[0]
+    writes = []
+    for half in range(2):
+        low, high = half * planes // 2, (half + 1) * planes // 2
+        x_new[low:high] = part_ref[low:high] + alphas[2] * z_ref[low + 1 : high + 1] + mixed * p_ref[low:high]
+        r_new[low:high] = r_ref[low:high] - alphas[2] * w_ref[low:high] - mixed * s_ref[low:high]
+        piece = pl.ds(low, high - low)
+        pairs = [(x_new.at[piece], x_out.at[piece]), (r_new.at[piece], r_out.at[piece])]
+        copies = [pltpu.make_async_copy(a, b, sems.at[2 * half + i]) for i, (a, b) in enumerate(pairs)]
+        start_all(copies)
+        writes += copies
+    wait_all(writes)
 
 
 def call(kernel, outs, scratch, args):
@@ -629,8 +661,6 @@
     columns = lax.axis_size("gy")
     devices = slabs * columns
     slab = lax.axis_index("gz")
-    column = lax.axis_index("gy")
-    here = slab * columns + column
     even_z = slab % 2 == 0
     field = jax.ShapeDtypeStruct((planes, rows, width), f32)
 
@@ -648,26 +678,12 @@
 
     def tag(space, items):
         return [(space, item) for item in items]
-
-    edge = jnp.stack(
-        [
-            (slab == 0).astype(i32),
-            (slab == slabs - 1).astype(i32),
-            (column == 0).astype(i32),
-            (column == columns - 1).astype(i32),
-            here * B_DEV,
-            jnp.int32(columns * B_DEV),
-            here * S_DEV,
-            slab % 2,
-            column % 2,
-        ]
-    )
 
     top, bottom, *sides, bubbles = call(
         slices_kernel,
         tag("vmem", [shape(DEPTH, rows, width)] * 2 + [shape(planes, DEPTH, width)] * 2 + [shape(B_DEV, devices * SPAN)]),
         [vmem(planes, rows, width), vmem(SPAN, devices * SPAN), semaphores(2)],
-        tag("smem", [edge]) + tag("hbm", [fraction, coarse_inverse]),
+        tag("hbm", [fraction, coarse_inverse]),
     )
     coarse_in = [swap(bubbles, "gz", 0), swap(bubbles, "gz", 1)]
     y_in = [swap(sides[0], "gy", 0), swap(sides[1], "gy", 1)]
@@ -686,7 +702,7 @@
         partial(destinations_kernel, columns),
         tag("hbm", [dest_shape]),
         [vmem(REGIONS, devices, LANES)] + like([dest_shape]) + [semaphores(1)],
-        tag("smem", [(slab % 2).reshape(1)]) + tag("vmem", spread_in),
+        tag("vmem", spread_in),
     )
     codes = shape(planes, rows, width, dtype=i8)
     faces = shape(planes + 1, rows, width)
@@ -712,7 +728,7 @@
             semaphores(len(inputs)),
             semaphores(2),
         ],
-        tag("smem", [edge]) + tag("vmem", z_in + y_in + corner_in) + tag("hbm", inputs),
+        tag("vmem", z_in + y_in + corner_in) + tag("hbm", inputs),
     )
     matrix = [code, cz, cy, cx, inv, south]
 
@@ -731,19 +747,25 @@
     def step(stage, parts, edges, state):
         last = stage == 2
         operands = state + ([diag] if last else [diag, dest])
-        outs = [field] * (2, 3, 5)[stage]
-        ends = [] if last else later_edges
-        scratch = like(operands) + [vmem(planes + 2, rows, width), vmem(2, planes, width)] + like([field] * len(outs))
-        if not last:
-            scratch += like([field])
-        scratch += [semaphores(len(operands)), semaphores(len(outs))]
+        tall_field = shape(planes + 2, rows, width)
+        sides = vmem(2, planes, width)
+        if last:
+            outs = tag("vmem", [shape(devices, LANES)]) + tag("kept", [tall_field] + [field] * 5)
+            scratch = like(operands) + [sides] + like([field]) + [semaphores(len(operands))]
+            count = 0
+        else:
+            fields = [field] * (2 + stage)
+            outs = tag("vmem", later_edges + [wide]) + tag("hbm", fields)
+            scratch = like(operands) + like([tall_field]) + [sides] + like([field] * (len(fields) + 1))
+            scratch += [semaphores(len(operands)), semaphores(len(fields))]
+            count = len(later_edges)
         results = call(
             partial(step_kernel, stage),
-            tag("vmem", ends + [shape(devices, LANES) if last else wide]) + tag("hbm", outs),
+            outs,
             scratch,
-            tag("smem", [edge]) + tag("vmem", parts + edges) + tag("kept", matrix) + tag("hbm", operands),
+            tag("vmem", parts + edges) + tag("kept", matrix) + tag("hbm", operands),
         )
-        return results[: len(ends)], results[len(ends)], results[len(ends) + 1 :]
+        return results[:count], results[count], results[count + 1 :]
 
     edges, parts = share(sent, send)
     sent, send, (z0, w0) = step(0, parts, edges, [r0])
@@ -752,14 +774,14 @@
     sent, send, (r1, z1, w1) = step(1, parts, edges, [r0, w0, z0])
     more_edges, more_parts = share(sent, send)
     edges, parts = edges + more_edges, parts + more_parts
-    _, send, (r2, s1, p1, z2, w2) = step(2, parts, edges, [r1, w1, w0, z1, z0])
+    _, send, kept = step(2, parts, edges, [r1, w1, w0, z1, z0])
     parts = parts + [exchange(send)]
     return tuple(
         call(
             final_kernel,
             tag("hbm", [field, field]),
-            like([field] * 7) + [semaphores(6), semaphores(2)],
-            tag("vmem", parts[1:]) + tag("hbm", [r2, w2, s1, z0, p1, z2]),
+            like([field, field]) + [semaphores(4)],
+            tag("vmem", parts[1:]) + tag("kept", kept),
         )
     )
 

time: 111 us -> 104 us (0.937)
  Pallas kernels: 39.6 us -> 32.1 us
    pallas_call x7, Pallas kernels: 39.6 us -> 32.1 us  [call(): pl.pallas_call(kernel, out_shape=made, in_specs=specs(args), out_specs=sp...]
  transfers between devices with their start and end apart: 23 -> 23, of which waited for: 7 -> 7; matrix products, arithmetic and copies ran while one was open for 2% -> 2% of each run, Pallas kernels for 3% -> 4%
where the time goes in v4:
time: 104 us; the launch traced here: 103 us
  starting transfers between devices  39.5 us (38%)
  Pallas kernels  32.1 us (31%)
  waiting for transfers between devices  20.1 us (19%)
  blocking collectives  8.94 us (9%)
  local copies, waits for them, and re-layouts  1.73 us (2%)
    pallas_call x7, Pallas kernels, call(): pl.pallas_call(kernel, out_shape=made, in_specs=specs(args), out_specs=sp...  32.1 us
    ppermute x20, starting transfers between devices, swap(): return lax.ppermute(block, axis, swaps(axis, first))  29.6 us
    all_to_all x3, waiting for transfers between devices, exchange(): return lax.all_to_all(blocks, ('gz', 'gy'), 0, 0).reshape(parts.shape)  11.2 us
    all_to_all x3, starting transfers between devices, exchange(): return lax.all_to_all(blocks, ('gz', 'gy'), 0, 0).reshape(parts.shape)  9.96 us
    all_to_all x1, blocking collectives, exchange(): return lax.all_to_all(blocks, ('gz', 'gy'), 0, 0).reshape(parts.shape)  8.94 us
    ppermute x20, waiting for transfers between devices, swap(): return lax.ppermute(block, axis, swaps(axis, first))  8.93 us
  transfers between devices with their start and end apart: 23, of which 7 were waited for; matrix products, arithmetic and copies ran while one was open for 2% of the time, Pallas kernels for 4%

profile of v4, /device:TPU:0, one launch (start us, length us, event | category | flops | bytes accessed | tf_op | source)
XLA Modules:
  0.0 103.2 jit_solution(16890869130269087784)
XLA Ops:
  0.6 1.1 %shard_map.68 = (f32[3,32,512]{2,1,0:T(8,128)S(1)}, f32[3,32,512]{2,1,0:T(8,128)S(1)}, f32[8,3,512]{2,1,0:T(4,128)S(1)}, f32[8,3,512]{2,1,0:T(4,128)S(1)}, f32[16,640]{1,0:T(8,128)S(1)}) custom-call(f32[8,32,512]{2,1,0:T(8,128)} %frac_hbm.3, f32[20,640]{1,0:T(8,128)} %coarse_hbm.1), custom_call_target="tpu_custom_call" | custom-call | tf_op jit(solution)/shard_map/pallas_call | solution.py:635
  1.8 0.6 collective-permute-start.2
  2.3 2.6 %collective-permute-start.3 = (f32[8,3,512]{2,1,0:T(4,128)S(1)}, f32[8,3,512]{2,1,0:T(4,128)S(1)}, u32[]{:S(2)}, u32[]{:S(2)}) collective-permute-start(f32[8,3,512]{2,1,0:T(4,128)S(1)} %get-tuple-element.45), channel_id=1, source_target_pairs={{1,2},{2,1},{3,0},{0,3},{5,6},{6,5},{7,4},{4,7},{9,10},{10,9},{11,... | collective-permute-start | bytes 147464 | tf_op jit(solution)/shard_map/ppermute | solution.py:655
  4.9 1.5 %collective-permute-start = (f32[3,32,512]{2,1,0:T(8,128)S(1)}, f32[3,32,512]{2,1,0:T(8,128)S(1)}, u32[]{:S(2)}, u32[]{:S(2)}) collective-permute-start(f32[3,32,512]{2,1,0:T(8,128)S(1)} %get-tuple-element.42), channel_id=1, source_target_pairs={{0,4},{4,0},{8,12},{12,8},{16,20},{20,16},{24,28},{28,24},{1,5},{5... | collective-permute-start | bytes 589832 | tf_op jit(solution)/shard_map/ppermute | solution.py:655
  6.4 3.5 %collective-permute-start.1 = (f32[3,32,512]{2,1,0:T(8,128)S(1)}, f32[3,32,512]{2,1,0:T(8,128)S(1)}, u32[]{:S(2)}, u32[]{:S(2)}) collective-permute-start(f32[3,32,512]{2,1,0:T(8,128)S(1)} %get-tuple-element.43), channel_id=1, source_target_pairs={{4,8},{8,4},{12,16},{16,12},{20,24},{24,20},{28,0},{0,28},{5,9},{9... | collective-permute-start | bytes 589832 | tf_op jit(solution)/shard_map/ppermute | solution.py:655
  10.0 1.2 %collective-permute-start.7 = (f32[16,640]{1,0:T(8,128)S(1)}, f32[16,640]{1,0:T(8,128)S(1)}, u32[]{:S(2)}, u32[]{:S(2)}) collective-permute-start(f32[16,640]{1,0:T(8,128)S(1)} %get-tuple-element.46), channel_id=1, source_target_pairs={{4,8},{8,4},{12,16},{16,12},{20,24},{24,20},{28,0},{0,28},{5,9},{9... | collective-permute-start | bytes 122888 | tf_op jit(solution)/shard_map/ppermute | solution.py:655
  11.2 0.0 collective-permute-done.2.y0_in
  11.2 0.0 collective-permute-start.6
  11.2 0.0 collective-permute-done.3.y1_in
  11.2 3.6 %collective-permute-start.5 = (f32[2,3,3,512]{3,2,1,0:T(4,128)S(1)}, f32[2,3,3,512]{3,2,1,0:T(4,128)S(1)}, u32[]{:S(2)}, u32[]{:S(2)}) collective-permute-start(f32[2,3,3,512]{3,2,1,0:T(4,128)S(1)} %get-tuple-element.82), channel_id=1, source_target_pairs={{4,8},{8,4},{12,16},{16,12},{20,24},{24,20},{28,0},{0,28},{5,9},{9... | collective-permute-start | bytes 110600 | tf_op jit(solution)/shard_map/ppermute | solution.py:655
  14.8 4.0 %collective-permute-done.6 = f32[16,640]{1,0:T(8,128)S(1)} collective-permute-done((f32[16,640]{1,0:T(8,128)S(1)}, f32[16,640]{1,0:T(8,128)S(1)}, u32[]{:S(2)}, u32[]{:S(2)}) %collective-permute-start.6) | collective-permute-done | bytes 40992 | tf_op jit(solution)/shard_map/ppermute | solution.py:655
  18.8 1.5 %collective-permute-start.4 = (f32[2,3,3,512]{3,2,1,0:T(4,128)S(1)}, f32[2,3,3,512]{3,2,1,0:T(4,128)S(1)}, u32[]{:S(2)}, u32[]{:S(2)}) collective-permute-start(f32[2,3,3,512]{3,2,1,0:T(4,128)S(1)} %get-tuple-element.83), channel_id=1, source_target_pairs={{0,4},{4,0},{8,12},{12,8},{16,20},{20,16},{24,28},{28,24},{1,5},{5... | collective-permute-start | bytes 110600 | tf_op jit(solution)/shard_map/ppermute | solution.py:655
  20.3 1.2 %reshape.37.own_ref = f32[20,32,20]{2,1,0:T(8,128)S(1)} reshape(f32[20,640]{1,0:T(8,128)} %coarse_hbm.1) | data formatting | bytes 102400 | tf_op jit(solution)/shard_map/reshape | solution.py:697
  21.5 0.3 reshape.38.near_ref
  21.8 0.0 collective-permute-done.7
  21.8 0.3 reshape.39.far_ref
  22.1 3.9 %shard_map.69.dest_hbm.refs_13_.refs_20_ = f32[52,64,128]{2,1,0:T(8,128)} custom-call(f32[20,32,20]{2,1,0:T(8,128)S(1)} %reshape.37.own_ref, f32[16,32,20]{2,1,0:T(8,128)S(1)} %reshape.38.near_ref, f32[16,32,20]{2,1,0:T(8,128)S(1)} %reshape.39.far_ref), custom_call_target="tpu_custom_call" | custom-call | tf_op jit(solution)/shard_map/pallas_call | solution.py:635
  26.0 0.0 collective-permute-done.5.k1_in
  26.0 0.0 collective-permute-done.1.z1_in
  26.0 8.9 %shard_map.70 = (f32[2,32,512]{2,1,0:T(8,128)S(1)}, f32[2,32,512]{2,1,0:T(8,128)S(1)}, f32[2,8,512]{2,1,0:T(8,128)S(1)}, f32[2,8,512]{2,1,0:T(8,128)S(1)}, f32[6...) custom-call(f32[3,32,512]{2,1,0:T(8,128)S(1)} %collective-permute-do, ...), custom_call_target="tpu_custom_call" | custom-call | tf_op jit(solution)/shard_map/pallas_call | solution.py:635
  34.9 0.6 collective-permute-start.8
  35.5 4.6 %collective-permute-start.9 = (f32[2,32,512]{2,1,0:T(8,128)S(1)}, f32[2,32,512]{2,1,0:T(8,128)S(1)}, u32[]{:S(2)}, u32[]{:S(2)}) collective-permute-start(f32[2,32,512]{2,1,0:T(8,128)S(1)} %get-tuple-element.49), channel_id=1, source_target_pairs={{4,8},{8,4},{12,16},{16,12},{20,24},{24,20},{28,0},{0,28},{5,9},{9... | collective-permute-start | bytes 393224 | tf_op jit(solution)/shard_map/ppermute | solution.py:655
  40.0 2.6 %all-to-all-start = ((f32[32,2,128]{2,1,0:T(2,128)}), f32[32,2,128]{2,1,0:T(2,128)S(1)}, u32[]{:S(2)}, u32[]{:S(2)}) async-start(f32[32,2,128]{2,1,0:T(2,128)} %bitcast.2), calls=%async_computation | async-start | bytes 65536 | tf_op jit(solution)/shard_map/all_to_all | solution.py:737
  42.6 0.2 collective-permute-start.10
  42.8 1.6 %collective-permute-start.11 = (f32[2,8,512]{2,1,0:T(8,128)S(1)}, f32[2,8,512]{2,1,0:T(8,128)S(1)}, u32[]{:S(2)}, u32[]{:S(2)}) collective-permute-start(f32[2,8,512]{2,1,0:T(8,128)S(1)} %get-tuple-element.51), channel_id=1, source_target_pairs={{1,2},{2,1},{3,0},{0,3},{5,6},{6,5},{7,4},{4,7},{9,10},{10,9},{11,... | collective-permute-start | bytes 98312 | tf_op jit(solution)/shard_map/ppermute | solution.py:655
  44.4 0.0 collective-permute-done.10.refs_3_.refs_4_.refs_5_
  44.4 1.7 %collective-permute-done.11.refs_4_.refs_5_.refs_6_ = f32[2,8,512]{2,1,0:T(8,128)S(1)} collective-permute-done((f32[2,8,512]{2,1,0:T(8,128)S(1)}, f32[2,8,512]{2,1,0:T(8,128)S(1)}, u32[]{:S(2)}, u32[]{:S(2)}) %collective-permute-start.11) | collective-permute-done | bytes 32800 | tf_op jit(solution)/shard_map/ppermute | solution.py:655
  46.2 3.7 %all-to-all-done = f32[32,2,128]{2,1,0:T(2,128)S(1)} async-done(((f32[32,2,128]{2,1,0:T(2,128)}), f32[32,2,128]{2,1,0:T(2,128)S(1)}, u32[]{:S(2)}, u32[]{:S(2)}) %all-to-all-start) | async-done | bytes 32800 | tf_op jit(solution)/shard_map/all_to_all | solution.py:737
  49.9 0.0 collective-permute-done.9.refs_2_.refs_3_.refs_4_
  49.9 5.9 %shard_map.71 = (f32[32,512]{1,0:T(8,128)S(1)}, f32[32,512]{1,0:T(8,128)S(1)}, f32[8,512]{1,0:T(8,128)S(1)}, f32[8,512]{1,0:T(8,128)S(1)}, f32[64,128]{1,0:T(8,1...) custom-call(f32[64,128]{1,0:T(8,128)S(1)} %bitcast.12, ...), custom_call_target="tpu_custom_call" | custom-call | tf_op jit(solution)/shard_map/pallas_call | solution.py:635
  55.8 0.6 collective-permute-start.12
  56.4 1.4 %collective-permute-start.13 = (f32[32,512]{1,0:T(8,128)S(1)}, f32[32,512]{1,0:T(8,128)S(1)}, u32[]{:S(2)}, u32[]{:S(2)}) collective-permute-start(f32[32,512]{1,0:T(8,128)S(1)} %get-tuple-element.62), channel_id=1, source_target_pairs={{4,8},{8,4},{12,16},{16,12},{20,24},{24,20},{28,0},{0,28},{5,9},{9... | collective-permute-start | bytes 196616 | tf_op jit(solution)/shard_map/ppermute | solution.py:655
  57.9 3.7 %all-to-all-start.1 = ((f32[32,2,128]{2,1,0:T(2,128)}), f32[32,2,128]{2,1,0:T(2,128)S(1)}, u32[]{:S(2)}, u32[]{:S(2)}) async-start(f32[32,2,128]{2,1,0:T(2,128)} %bitcast.4), calls=%async_computation.1 | async-start | bytes 65536 | tf_op jit(solution)/shard_map/all_to_all | solution.py:737
  61.6 0.3 collective-permute-start.14
  61.9 1.6 %collective-permute-start.15 = (f32[8,512]{1,0:T(8,128)S(1)}, f32[8,512]{1,0:T(8,128)S(1)}, u32[]{:S(2)}, u32[]{:S(2)}) collective-permute-start(f32[8,512]{1,0:T(8,128)S(1)} %get-tuple-element.64), channel_id=1, source_target_pairs={{1,2},{2,1},{3,0},{0,3},{5,6},{6,5},{7,4},{4,7},{9,10},{10,9},{11,... | collective-permute-start | bytes 49160 | tf_op jit(solution)/shard_map/ppermute | solution.py:655
  63.5 1.6 %collective-permute-done.15.refs_9_.refs_10_ = f32[8,512]{1,0:T(8,128)S(1)} collective-permute-done((f32[8,512]{1,0:T(8,128)S(1)}, f32[8,512]{1,0:T(8,128)S(1)}, u32[]{:S(2)}, u32[]{:S(2)}) %collective-permute-start.15) | collective-permute-done | bytes 16416 | tf_op jit(solution)/shard_map/ppermute | solution.py:655
  65.1 3.7 %all-to-all-done.1 = f32[32,2,128]{2,1,0:T(2,128)S(1)} async-done(((f32[32,2,128]{2,1,0:T(2,128)}), f32[32,2,128]{2,1,0:T(2,128)S(1)}, u32[]{:S(2)}, u32[]{:S(2)}) %all-to-all-start.1) | async-done | bytes 32800 | tf_op jit(solution)/shard_map/all_to_all | solution.py:737
  68.8 6.6 %shard_map.72 = (f32[32,512]{1,0:T(8,128)S(1)}, f32[32,512]{1,0:T(8,128)S(1)}, f32[8,512]{1,0:T(8,128)S(1)}, f32[8,512]{1,0:T(8,128)S(1)}, f32[64,128]{1,0:T(8,1...) custom-call(f32[64,128]{1,0:T(8,128)S(1)} %bitcast.13, f32[64,128]{1,0:T(8,128)S(1)} %bitcast.15, ...), custom_call_target="tpu_custom_call" | custom-call | tf_op jit(solution)/shard_map/pallas_call | solution.py:635
  75.5 0.6 collective-permute-start.16
  76.1 1.5 %collective-permute-start.17 = (f32[32,512]{1,0:T(8,128)S(1)}, f32[32,512]{1,0:T(8,128)S(1)}, u32[]{:S(2)}, u32[]{:S(2)}) collective-permute-start(f32[32,512]{1,0:T(8,128)S(1)} %get-tuple-element.69), channel_id=1, source_target_pairs={{4,8},{8,4},{12,16},{16,12},{20,24},{24,20},{28,0},{0,28},{5,9},{9... | collective-permute-start | bytes 196616 | tf_op jit(solution)/shard_map/ppermute | solution.py:655
  77.6 3.7 %all-to-all-start.2 = ((f32[32,2,128]{2,1,0:T(2,128)}), f32[32,2,128]{2,1,0:T(2,128)S(1)}, u32[]{:S(2)}, u32[]{:S(2)}) async-start(f32[32,2,128]{2,1,0:T(2,128)} %bitcast.6), calls=%async_computation.2 | async-start | bytes 65536 | tf_op jit(solution)/shard_map/all_to_all | solution.py:737
  81.3 0.3 collective-permute-start.18
  81.6 1.6 %collective-permute-start.19 = (f32[8,512]{1,0:T(8,128)S(1)}, f32[8,512]{1,0:T(8,128)S(1)}, u32[]{:S(2)}, u32[]{:S(2)}) collective-permute-start(f32[8,512]{1,0:T(8,128)S(1)} %get-tuple-element.71), channel_id=1, source_target_pairs={{1,2},{2,1},{3,0},{0,3},{5,6},{6,5},{7,4},{4,7},{9,10},{10,9},{11,... | collective-permute-start | bytes 49160 | tf_op jit(solution)/shard_map/ppermute | solution.py:655
  83.2 1.6 %collective-permute-done.19.refs_14_ = f32[8,512]{1,0:T(8,128)S(1)} collective-permute-done((f32[8,512]{1,0:T(8,128)S(1)}, f32[8,512]{1,0:T(8,128)S(1)}, u32[]{:S(2)}, u32[]{:S(2)}) %collective-permute-start.19) | collective-permute-done | bytes 16416 | tf_op jit(solution)/shard_map/ppermute | solution.py:655
  84.8 3.7 %all-to-all-done.2 = f32[32,2,128]{2,1,0:T(2,128)S(1)} async-done(((f32[32,2,128]{2,1,0:T(2,128)}), f32[32,2,128]{2,1,0:T(2,128)S(1)}, u32[]{:S(2)}, u32[]{:S(2)}) %all-to-all-start.2) | async-done | bytes 32800 | tf_op jit(solution)/shard_map/all_to_all | solution.py:737
  88.5 4.4 %shard_map.73 = (f32[32,128]{1,0:T(8,128)S(1)}, f32[10,32,512]{2,1,0:T(8,128)S(1)}, f32[8,32,512]{2,1,0:T(8,128)S(1)}, f32[8,32,512]{2,1,0:T(8,128)S(1)}, f32[8,...) custom-call(f32[64,128]{1,0:T(8,128)S(1)} %bitcast.14, f32[64,128]{1,0:T(8,128)S(1)} %bitcast.16, ...), custom_call_target="tpu_custom_call" | custom-call | tf_op jit(solution)/shard_map/pallas_call | solution.py:635
  92.9 8.9 %all_to_all.20 = f32[32,1,128]{2,1,0:T(1,128)S(1)} all-to-all(f32[32,1,128]{2,1,0:T(1,128)S(1)} %bitcast.23), channel_id=1, replica_groups=mesh['gz'=8,'gy'=4] {'gz','gy'}, dimensions={0} | all-to-all | bytes 32768 | tf_op jit(solution)/shard_map/all_to_all | solution.py:737
  101.8 1.4 %shard_map.74 = (f32[8,32,512]{2,1,0:T(8,128)}, f32[8,32,512]{2,1,0:T(8,128)}) custom-call(f32[64,128]{1,0:T(8,128)S(1)} %bitcast.17, f32[64,128]{1,0:T(8,128)S(1)} %bitcast.19, f32[32,128]{1,0:T(8,128)S(1)} %bitcast.22, f32[10,32,512]{2,1,0:T(8,128)S(1)} %get-tuple-element.76.z_ref, f32[8,32,512]{2,1,0:T(8,128)S(1)} %get-tuple-element.77.w_ref, ...), custom_call_target="tpu_custom_call" | custom-call | tf_op jit(solution)/shard_map/pallas_call | solution.py:635
  (10 shorter events, 0.0 us)
Async XLA Ops:
  1.8 9.4 %collective-permute-start.2 = (f32[8,3,512]{2,1,0:T(4,128)S(1)}, f32[8,3,512]{2,1,0:T(4,128)S(1)}, u32[]{:S(2)}, u32[]{:S(2)}) collective-permute-start(f32[8,3,512]{2,1,0:T(4,128)S(1)} %get-tuple-element.44), channel_id=1, source_target_pairs={{0,1},{1,0},{2,3},{3,2},{4,5},{5,4},{6,7},{7,6},{8,9},{9,8},{10,11... | collective-permute-start | bytes 147464 | tf_op jit(solution)/shard_map/ppermute | solution.py:655
  2.3 8.8 %collective-permute-start.3 = (f32[8,3,512]{2,1,0:T(4,128)S(1)}, f32[8,3,512]{2,1,0:T(4,128)S(1)}, u32[]{:S(2)}, u32[]{:S(2)}) collective-permute-start(f32[8,3,512]{2,1,0:T(4,128)S(1)} %get-tuple-element.45), channel_id=1, source_target_pairs={{1,2},{2,1},{3,0},{0,3},{5,6},{6,5},{7,4},{4,7},{9,10},{10,9},{11,... | collective-permute-start | bytes 147464 | tf_op jit(solution)/shard_map/ppermute | solution.py:655
  4.9 21.1 %collective-permute-start = (f32[3,32,512]{2,1,0:T(8,128)S(1)}, f32[3,32,512]{2,1,0:T(8,128)S(1)}, u32[]{:S(2)}, u32[]{:S(2)}) collective-permute-start(f32[3,32,512]{2,1,0:T(8,128)S(1)} %get-tuple-element.42), channel_id=1, source_target_pairs={{0,4},{4,0},{8,12},{12,8},{16,20},{20,16},{24,28},{28,24},{1,5},{5... | collective-permute-start | bytes 589832 | tf_op jit(solution)/shard_map/ppermute | solution.py:655
  6.4 19.6 %collective-permute-start.1 = (f32[3,32,512]{2,1,0:T(8,128)S(1)}, f32[3,32,512]{2,1,0:T(8,128)S(1)}, u32[]{:S(2)}, u32[]{:S(2)}) collective-permute-start(f32[3,32,512]{2,1,0:T(8,128)S(1)} %get-tuple-element.43), channel_id=1, source_target_pairs={{4,8},{8,4},{12,16},{16,12},{20,24},{24,20},{28,0},{0,28},{5,9},{9... | collective-permute-start | bytes 589832 | tf_op jit(solution)/shard_map/ppermute | solution.py:655
  10.0 11.8 %collective-permute-start.7 = (f32[16,640]{1,0:T(8,128)S(1)}, f32[16,640]{1,0:T(8,128)S(1)}, u32[]{:S(2)}, u32[]{:S(2)}) collective-permute-start(f32[16,640]{1,0:T(8,128)S(1)} %get-tuple-element.46), channel_id=1, source_target_pairs={{4,8},{8,4},{12,16},{16,12},{20,24},{24,20},{28,0},{0,28},{5,9},{9... | collective-permute-start | bytes 122888 | tf_op jit(solution)/shard_map/ppermute | solution.py:655
  11.2 7.7 %collective-permute-start.6 = (f32[16,640]{1,0:T(8,128)S(1)}, f32[16,640]{1,0:T(8,128)S(1)}, u32[]{:S(2)}, u32[]{:S(2)}) collective-permute-start(f32[16,640]{1,0:T(8,128)S(1)} %get-tuple-element.46), channel_id=1, source_target_pairs={{0,4},{4,0},{8,12},{12,8},{16,20},{20,16},{24,28},{28,24},{1,5},{5... | collective-permute-start | bytes 122888 | tf_op jit(solution)/shard_map/ppermute | solution.py:655
  11.2 14.8 %collective-permute-start.5 = (f32[2,3,3,512]{3,2,1,0:T(4,128)S(1)}, f32[2,3,3,512]{3,2,1,0:T(4,128)S(1)}, u32[]{:S(2)}, u32[]{:S(2)}) collective-permute-start(f32[2,3,3,512]{3,2,1,0:T(4,128)S(1)} %get-tuple-element.82), channel_id=1, source_target_pairs={{4,8},{8,4},{12,16},{16,12},{20,24},{24,20},{28,0},{0,28},{5,9},{9... | collective-permute-start | bytes 110600 | tf_op jit(solution)/shard_map/ppermute | solution.py:655
  18.8 7.2 %collective-permute-start.4 = (f32[2,3,3,512]{3,2,1,0:T(4,128)S(1)}, f32[2,3,3,512]{3,2,1,0:T(4,128)S(1)}, u32[]{:S(2)}, u32[]{:S(2)}) collective-permute-start(f32[2,3,3,512]{3,2,1,0:T(4,128)S(1)} %get-tuple-element.83), channel_id=1, source_target_pairs={{0,4},{4,0},{8,12},{12,8},{16,20},{20,16},{24,28},{28,24},{1,5},{5... | collective-permute-start | bytes 110600 | tf_op jit(solution)/shard_map/ppermute | solution.py:655
  34.9 15.0 %collective-permute-start.8 = (f32[2,32,512]{2,1,0:T(8,128)S(1)}, f32[2,32,512]{2,1,0:T(8,128)S(1)}, u32[]{:S(2)}, u32[]{:S(2)}) collective-permute-start(f32[2,32,512]{2,1,0:T(8,128)S(1)} %get-tuple-element.48), channel_id=1, source_target_pairs={{0,4},{4,0},{8,12},{12,8},{16,20},{20,16},{24,28},{28,24},{1,5},{5... | collective-permute-start | bytes 393224 | tf_op jit(solution)/shard_map/ppermute | solution.py:655
  35.5 14.4 %collective-permute-start.9 = (f32[2,32,512]{2,1,0:T(8,128)S(1)}, f32[2,32,512]{2,1,0:T(8,128)S(1)}, u32[]{:S(2)}, u32[]{:S(2)}) collective-permute-start(f32[2,32,512]{2,1,0:T(8,128)S(1)} %get-tuple-element.49), channel_id=1, source_target_pairs={{4,8},{8,4},{12,16},{16,12},{20,24},{24,20},{28,0},{0,28},{5,9},{9... | collective-permute-start | bytes 393224 | tf_op jit(solution)/shard_map/ppermute | solution.py:655
  40.0 9.8 %all-to-all-start = ((f32[32,2,128]{2,1,0:T(2,128)}), f32[32,2,128]{2,1,0:T(2,128)S(1)}, u32[]{:S(2)}, u32[]{:S(2)}) async-start(f32[32,2,128]{2,1,0:T(2,128)} %bitcast.2), calls=%async_computation | async-start | bytes 65536 | tf_op jit(solution)/shard_map/all_to_all | solution.py:737
  42.6 1.8 %collective-permute-start.10 = (f32[2,8,512]{2,1,0:T(8,128)S(1)}, f32[2,8,512]{2,1,0:T(8,128)S(1)}, u32[]{:S(2)}, u32[]{:S(2)}) collective-permute-start(f32[2,8,512]{2,1,0:T(8,128)S(1)} %get-tuple-element.50), channel_id=1, source_target_pairs={{0,1},{1,0},{2,3},{3,2},{4,5},{5,4},{6,7},{7,6},{8,9},{9,8},{10,11... | collective-permute-start | bytes 98312 | tf_op jit(solution)/shard_map/ppermute | solution.py:655
  42.8 3.4 %collective-permute-start.11 = (f32[2,8,512]{2,1,0:T(8,128)S(1)}, f32[2,8,512]{2,1,0:T(8,128)S(1)}, u32[]{:S(2)}, u32[]{:S(2)}) collective-permute-start(f32[2,8,512]{2,1,0:T(8,128)S(1)} %get-tuple-element.51), channel_id=1, source_target_pairs={{1,2},{2,1},{3,0},{0,3},{5,6},{6,5},{7,4},{4,7},{9,10},{10,9},{11,... | collective-permute-start | bytes 98312 | tf_op jit(solution)/shard_map/ppermute | solution.py:655
  55.8 13.1 %collective-permute-start.12 = (f32[32,512]{1,0:T(8,128)S(1)}, f32[32,512]{1,0:T(8,128)S(1)}, u32[]{:S(2)}, u32[]{:S(2)}) collective-permute-start(f32[32,512]{1,0:T(8,128)S(1)} %get-tuple-element.61), channel_id=1, source_target_pairs={{0,4},{4,0},{8,12},{12,8},{16,20},{20,16},{24,28},{28,24},{1,5},{5... | collective-permute-start | bytes 196616 | tf_op jit(solution)/shard_map/ppermute | solution.py:655
  56.4 12.4 %collective-permute-start.13 = (f32[32,512]{1,0:T(8,128)S(1)}, f32[32,512]{1,0:T(8,128)S(1)}, u32[]{:S(2)}, u32[]{:S(2)}) collective-permute-start(f32[32,512]{1,0:T(8,128)S(1)} %get-tuple-element.62), channel_id=1, source_target_pairs={{4,8},{8,4},{12,16},{16,12},{20,24},{24,20},{28,0},{0,28},{5,9},{9... | collective-permute-start | bytes 196616 | tf_op jit(solution)/shard_map/ppermute | solution.py:655
  57.9 11.0 %all-to-all-start.1 = ((f32[32,2,128]{2,1,0:T(2,128)}), f32[32,2,128]{2,1,0:T(2,128)S(1)}, u32[]{:S(2)}, u32[]{:S(2)}) async-start(f32[32,2,128]{2,1,0:T(2,128)} %bitcast.4), calls=%async_computation.1 | async-start | bytes 65536 | tf_op jit(solution)/shard_map/all_to_all | solution.py:737
  61.6 2.0 %collective-permute-start.14 = (f32[8,512]{1,0:T(8,128)S(1)}, f32[8,512]{1,0:T(8,128)S(1)}, u32[]{:S(2)}, u32[]{:S(2)}) collective-permute-start(f32[8,512]{1,0:T(8,128)S(1)} %get-tuple-element.63), channel_id=1, source_target_pairs={{0,1},{1,0},{2,3},{3,2},{4,5},{5,4},{6,7},{7,6},{8,9},{9,8},{10,11... | collective-permute-start | bytes 49160 | tf_op jit(solution)/shard_map/ppermute | solution.py:655
  61.9 3.2 %collective-permute-start.15 = (f32[8,512]{1,0:T(8,128)S(1)}, f32[8,512]{1,0:T(8,128)S(1)}, u32[]{:S(2)}, u32[]{:S(2)}) collective-permute-start(f32[8,512]{1,0:T(8,128)S(1)} %get-tuple-element.64), channel_id=1, source_target_pairs={{1,2},{2,1},{3,0},{0,3},{5,6},{6,5},{7,4},{4,7},{9,10},{10,9},{11,... | collective-permute-start | bytes 49160 | tf_op jit(solution)/shard_map/ppermute | solution.py:655
  75.5 13.1 %collective-permute-start.16 = (f32[32,512]{1,0:T(8,128)S(1)}, f32[32,512]{1,0:T(8,128)S(1)}, u32[]{:S(2)}, u32[]{:S(2)}) collective-permute-start(f32[32,512]{1,0:T(8,128)S(1)} %get-tuple-element.68), channel_id=1, source_target_pairs={{0,4},{4,0},{8,12},{12,8},{16,20},{20,16},{24,28},{28,24},{1,5},{5... | collective-permute-start | bytes 196616 | tf_op jit(solution)/shard_map/ppermute | solution.py:655
  76.1 12.4 %collective-permute-start.17 = (f32[32,512]{1,0:T(8,128)S(1)}, f32[32,512]{1,0:T(8,128)S(1)}, u32[]{:S(2)}, u32[]{:S(2)}) collective-permute-start(f32[32,512]{1,0:T(8,128)S(1)} %get-tuple-element.69), channel_id=1, source_target_pairs={{4,8},{8,4},{12,16},{16,12},{20,24},{24,20},{28,0},{0,28},{5,9},{9... | collective-permute-start | bytes 196616 | tf_op jit(solution)/shard_map/ppermute | solution.py:655
  77.6 10.9 %all-to-all-start.2 = ((f32[32,2,128]{2,1,0:T(2,128)}), f32[32,2,128]{2,1,0:T(2,128)S(1)}, u32[]{:S(2)}, u32[]{:S(2)}) async-start(f32[32,2,128]{2,1,0:T(2,128)} %bitcast.6), calls=%async_computation.2 | async-start | bytes 65536 | tf_op jit(solution)/shard_map/all_to_all | solution.py:737
  81.3 2.0 %collective-permute-start.18 = (f32[8,512]{1,0:T(8,128)S(1)}, f32[8,512]{1,0:T(8,128)S(1)}, u32[]{:S(2)}, u32[]{:S(2)}) collective-permute-start(f32[8,512]{1,0:T(8,128)S(1)} %get-tuple-element.70), channel_id=1, source_target_pairs={{0,1},{1,0},{2,3},{3,2},{4,5},{5,4},{6,7},{7,6},{8,9},{9,8},{10,11... | collective-permute-start | bytes 49160 | tf_op jit(solution)/shard_map/ppermute | solution.py:655
  81.6 3.2 %collective-permute-start.19 = (f32[8,512]{1,0:T(8,128)S(1)}, f32[8,512]{1,0:T(8,128)S(1)}, u32[]{:S(2)}, u32[]{:S(2)}) collective-permute-start(f32[8,512]{1,0:T(8,128)S(1)} %get-tuple-element.71), channel_id=1, source_target_pairs={{1,2},{2,1},{3,0},{0,3},{5,6},{6,5},{7,4},{4,7},{9,10},{10,9},{11,... | collective-permute-start | bytes 49160 | tf_op jit(solution)/shard_map/ppermute | solution.py:655

commit v5 on v4

--- a/solution.py
+++ b/solution.py
@@ -317,7 +317,7 @@
         flat_ref[index] = (up_rows(ny) - down_rows(ny)) + (right_of(nx) - left_of(nx))
         return carry
 
-    lax.fori_loop(0, planes + 4, normal_plane, 0)
+    lax.fori_loop(0, planes + 4, normal_plane, 0, unroll=2)
 
     def kappa_plane(index, carry):
         keep = (index - 1 >= first_plane) & (index - 1 < last_plane)
@@ -512,9 +512,9 @@
         )
         side_ref[jnp.where(upper, 1, 0)] = block + found
 
-    for name in names:
-        if name not in ("diag", "dest"):
-            reads[name].wait()
+    early = tuple(name for name in names if name[0] in "rw")
+    for name in early:
+        reads[name].wait()
     empty = jnp.zeros((rows, width), f32)
 
     def residual(plane, before):
@@ -525,9 +525,6 @@
         if stage == 2:
             image = held["w1"][plane] + betas[1] * held["w0"][plane]
             made["s"][plane] = image
-            along = held["z1"][plane] + betas[1] * held["z0"][plane]
-            made["p"][plane] = along
-            made["x"][plane] = alphas[0] * held["z0"][plane] + alphas[1] * along
             value = value - alphas[1] * image
             made["rn"][plane] = value
         value = value + cz_ref[plane] * before
@@ -546,7 +543,9 @@
     lax.fori_loop(0, planes, direction, empty)
     if not last:
         writes["z"].start()
-    reads["diag"].wait()
+    for name in names:
+        if name not in early and name != "dest":
+            reads[name].wait()
     row = iota((rows, width), 0)
 
     def image_plane(plane, carry):
@@ -568,7 +567,10 @@
         if stage == 1:
             found.append(total(here * held["w0"][plane] + held["z0"][plane] * image))
         if stage == 2:
-            found.append(total(here * made["s"][plane] + made["p"][plane] * image))
+            along = held["z1"][plane] + betas[1] * held["z0"][plane]
+            made["p"][plane] = along
+            made["x"][plane] = alphas[0] * held["z0"][plane] + alphas[1] * along
+            found.append(total(here * made["s"][plane] + along * image))
         if not last:
             before = image + cz_ref[plane] * before
             work_ref[plane] = before
@@ -577,7 +579,7 @@
 
     blank = jnp.zeros((8, LANES), f32)
     dots, _ = lax.fori_loop(
-        0, planes, image_plane, ((blank,) * (3 if stage else 2), blank if last else empty)
+        0, planes, image_plane, ((blank,) * (3 if stage else 2), blank if last else empty), unroll=2
     )
     if not last:
         writes["w"].start()
@@ -736,11 +738,9 @@
         blocks = parts.reshape(devices, -1, LANES)
         return lax.all_to_all(blocks, ("gz", "gy"), 0, 0).reshape(parts.shape)
 
-    def halos(sent):
-        return [swap(sent[0], "gz", 0), swap(sent[1], "gz", 1), swap(sent[2], "gy", 0), swap(sent[3], "gy", 1)]
-
     def share(sent, send):
-        edges = halos(sent)
+        edges = [swap(sent[0], "gz", 0), swap(sent[1], "gz", 1)]
+        edges += [swap(sent[2], "gy", 0), swap(sent[3], "gy", 1)]
         parts = [exchange(send)]
         return edges, parts
 

time: 104 us -> 102 us (0.981)
  Pallas kernels: 32.1 us -> 30.3 us
    pallas_call x7, Pallas kernels: 32.1 us -> 30.3 us  [call(): pl.pallas_call(kernel, out_shape=made, in_specs=specs(args), out_specs=sp...]
where the time goes in v5:
time: 102 us; the launch traced here: 101 us
  starting transfers between devices  39.5 us (39%)
  Pallas kernels  30.3 us (30%)
  waiting for transfers between devices  20.1 us (20%)
  blocking collectives  8.94 us (9%)
  local copies, waits for them, and re-layouts  1.73 us (2%)
    pallas_call x7, Pallas kernels, call(): pl.pallas_call(kernel, out_shape=made, in_specs=specs(args), out_specs=sp...  30.3 us
    ppermute x20, starting transfers between devices, swap(): return lax.ppermute(block, axis, swaps(axis, first))  29.5 us
    all_to_all x3, waiting for transfers between devices, exchange(): return lax.all_to_all(blocks, ('gz', 'gy'), 0, 0).reshape(parts.shape)  11.2 us
    all_to_all x3, starting transfers between devices, exchange(): return lax.all_to_all(blocks, ('gz', 'gy'), 0, 0).reshape(parts.shape)  9.97 us
    all_to_all x1, blocking collectives, exchange(): return lax.all_to_all(blocks, ('gz', 'gy'), 0, 0).reshape(parts.shape)  8.94 us
    ppermute x20, waiting for transfers between devices, swap(): return lax.ppermute(block, axis, swaps(axis, first))  8.93 us
  transfers between devices with their start and end apart: 23, of which 7 were waited for; matrix products, arithmetic and copies ran while one was open for 2% of the time, Pallas kernels for 4%

profile of v5, /device:TPU:0, one launch (start us, length us, event | category | flops | bytes accessed | tf_op | source)
XLA Modules:
  0.0 101.4 jit_solution(17896228073593588466)
XLA Ops:
  0.6 1.1 %shard_map.68 = (f32[3,32,512]{2,1,0:T(8,128)S(1)}, f32[3,32,512]{2,1,0:T(8,128)S(1)}, f32[8,3,512]{2,1,0:T(4,128)S(1)}, f32[8,3,512]{2,1,0:T(4,128)S(1)}, f32[16,640]{1,0:T(8,128)S(1)}) custom-call(f32[8,32,512]{2,1,0:T(8,128)} %frac_hbm.3, f32[20,640]{1,0:T(8,128)} %coarse_hbm.1), custom_call_target="tpu_custom_call" | custom-call | tf_op jit(solution)/shard_map/pallas_call | solution.py:637
  1.8 0.6 collective-permute-start.2
  2.3 2.6 %collective-permute-start.3 = (f32[8,3,512]{2,1,0:T(4,128)S(1)}, f32[8,3,512]{2,1,0:T(4,128)S(1)}, u32[]{:S(2)}, u32[]{:S(2)}) collective-permute-start(f32[8,3,512]{2,1,0:T(4,128)S(1)} %get-tuple-element.45), channel_id=1, source_target_pairs={{1,2},{2,1},{3,0},{0,3},{5,6},{6,5},{7,4},{4,7},{9,10},{10,9},{11,... | collective-permute-start | bytes 147464 | tf_op jit(solution)/shard_map/ppermute | solution.py:657
  4.9 1.5 %collective-permute-start = (f32[3,32,512]{2,1,0:T(8,128)S(1)}, f32[3,32,512]{2,1,0:T(8,128)S(1)}, u32[]{:S(2)}, u32[]{:S(2)}) collective-permute-start(f32[3,32,512]{2,1,0:T(8,128)S(1)} %get-tuple-element.42), channel_id=1, source_target_pairs={{0,4},{4,0},{8,12},{12,8},{16,20},{20,16},{24,28},{28,24},{1,5},{5... | collective-permute-start | bytes 589832 | tf_op jit(solution)/shard_map/ppermute | solution.py:657
  6.4 3.5 %collective-permute-start.1 = (f32[3,32,512]{2,1,0:T(8,128)S(1)}, f32[3,32,512]{2,1,0:T(8,128)S(1)}, u32[]{:S(2)}, u32[]{:S(2)}) collective-permute-start(f32[3,32,512]{2,1,0:T(8,128)S(1)} %get-tuple-element.43), channel_id=1, source_target_pairs={{4,8},{8,4},{12,16},{16,12},{20,24},{24,20},{28,0},{0,28},{5,9},{9... | collective-permute-start | bytes 589832 | tf_op jit(solution)/shard_map/ppermute | solution.py:657
  10.0 1.2 %collective-permute-start.7 = (f32[16,640]{1,0:T(8,128)S(1)}, f32[16,640]{1,0:T(8,128)S(1)}, u32[]{:S(2)}, u32[]{:S(2)}) collective-permute-start(f32[16,640]{1,0:T(8,128)S(1)} %get-tuple-element.46), channel_id=1, source_target_pairs={{4,8},{8,4},{12,16},{16,12},{20,24},{24,20},{28,0},{0,28},{5,9},{9... | collective-permute-start | bytes 122888 | tf_op jit(solution)/shard_map/ppermute | solution.py:657
  11.2 0.0 collective-permute-done.2.y0_in
  11.2 0.0 collective-permute-start.6
  11.2 0.0 collective-permute-done.3.y1_in
  11.2 3.6 %collective-permute-start.5 = (f32[2,3,3,512]{3,2,1,0:T(4,128)S(1)}, f32[2,3,3,512]{3,2,1,0:T(4,128)S(1)}, u32[]{:S(2)}, u32[]{:S(2)}) collective-permute-start(f32[2,3,3,512]{3,2,1,0:T(4,128)S(1)} %get-tuple-element.82), channel_id=1, source_target_pairs={{4,8},{8,4},{12,16},{16,12},{20,24},{24,20},{28,0},{0,28},{5,9},{9... | collective-permute-start | bytes 110600 | tf_op jit(solution)/shard_map/ppermute | solution.py:657
  14.8 4.0 %collective-permute-done.6 = f32[16,640]{1,0:T(8,128)S(1)} collective-permute-done((f32[16,640]{1,0:T(8,128)S(1)}, f32[16,640]{1,0:T(8,128)S(1)}, u32[]{:S(2)}, u32[]{:S(2)}) %collective-permute-start.6) | collective-permute-done | bytes 40992 | tf_op jit(solution)/shard_map/ppermute | solution.py:657
  18.8 1.5 %collective-permute-start.4 = (f32[2,3,3,512]{3,2,1,0:T(4,128)S(1)}, f32[2,3,3,512]{3,2,1,0:T(4,128)S(1)}, u32[]{:S(2)}, u32[]{:S(2)}) collective-permute-start(f32[2,3,3,512]{3,2,1,0:T(4,128)S(1)} %get-tuple-element.83), channel_id=1, source_target_pairs={{0,4},{4,0},{8,12},{12,8},{16,20},{20,16},{24,28},{28,24},{1,5},{5... | collective-permute-start | bytes 110600 | tf_op jit(solution)/shard_map/ppermute | solution.py:657
  20.3 1.2 %reshape.37.own_ref = f32[20,32,20]{2,1,0:T(8,128)S(1)} reshape(f32[20,640]{1,0:T(8,128)} %coarse_hbm.1) | data formatting | bytes 102400 | tf_op jit(solution)/shard_map/reshape | solution.py:699
  21.5 0.3 reshape.38.near_ref
  21.8 0.0 collective-permute-done.7
  21.8 0.3 reshape.39.far_ref
  22.1 3.9 %shard_map.69.dest_hbm.refs_13_.refs_20_ = f32[52,64,128]{2,1,0:T(8,128)} custom-call(f32[20,32,20]{2,1,0:T(8,128)S(1)} %reshape.37.own_ref, f32[16,32,20]{2,1,0:T(8,128)S(1)} %reshape.38.near_ref, f32[16,32,20]{2,1,0:T(8,128)S(1)} %reshape.39.far_ref), custom_call_target="tpu_custom_call" | custom-call | tf_op jit(solution)/shard_map/pallas_call | solution.py:637
  26.0 0.0 collective-permute-done.5.k1_in
  26.0 0.0 collective-permute-done.1.z1_in
  26.0 8.4 %shard_map.70 = (f32[2,32,512]{2,1,0:T(8,128)S(1)}, f32[2,32,512]{2,1,0:T(8,128)S(1)}, f32[2,8,512]{2,1,0:T(8,128)S(1)}, f32[2,8,512]{2,1,0:T(8,128)S(1)}, f32[6...) custom-call(f32[3,32,512]{2,1,0:T(8,128)S(1)} %collective-permute-do, ...), custom_call_target="tpu_custom_call" | custom-call | tf_op jit(solution)/shard_map/pallas_call | solution.py:637
  34.4 0.6 collective-permute-start.8
  35.0 4.6 %collective-permute-start.9 = (f32[2,32,512]{2,1,0:T(8,128)S(1)}, f32[2,32,512]{2,1,0:T(8,128)S(1)}, u32[]{:S(2)}, u32[]{:S(2)}) collective-permute-start(f32[2,32,512]{2,1,0:T(8,128)S(1)} %get-tuple-element.49), channel_id=1, source_target_pairs={{4,8},{8,4},{12,16},{16,12},{20,24},{24,20},{28,0},{0,28},{5,9},{9... | collective-permute-start | bytes 393224 | tf_op jit(solution)/shard_map/ppermute | solution.py:657
  39.5 2.6 %all-to-all-start = ((f32[32,2,128]{2,1,0:T(2,128)}), f32[32,2,128]{2,1,0:T(2,128)S(1)}, u32[]{:S(2)}, u32[]{:S(2)}) async-start(f32[32,2,128]{2,1,0:T(2,128)} %bitcast.2), calls=%async_computation | async-start | bytes 65536 | tf_op jit(solution)/shard_map/all_to_all | solution.py:739
  42.1 0.2 collective-permute-start.10
  42.3 1.6 %collective-permute-start.11 = (f32[2,8,512]{2,1,0:T(8,128)S(1)}, f32[2,8,512]{2,1,0:T(8,128)S(1)}, u32[]{:S(2)}, u32[]{:S(2)}) collective-permute-start(f32[2,8,512]{2,1,0:T(8,128)S(1)} %get-tuple-element.51), channel_id=1, source_target_pairs={{1,2},{2,1},{3,0},{0,3},{5,6},{6,5},{7,4},{4,7},{9,10},{10,9},{11,... | collective-permute-start | bytes 98312 | tf_op jit(solution)/shard_map/ppermute | solution.py:657
  43.9 0.0 collective-permute-done.10.refs_3_.refs_4_.refs_5_
  43.9 1.7 %collective-permute-done.11.refs_4_.refs_5_.refs_6_ = f32[2,8,512]{2,1,0:T(8,128)S(1)} collective-permute-done((f32[2,8,512]{2,1,0:T(8,128)S(1)}, f32[2,8,512]{2,1,0:T(8,128)S(1)}, u32[]{:S(2)}, u32[]{:S(2)}) %collective-permute-start.11) | collective-permute-done | bytes 32800 | tf_op jit(solution)/shard_map/ppermute | solution.py:657
  45.7 3.7 %all-to-all-done = f32[32,2,128]{2,1,0:T(2,128)S(1)} async-done(((f32[32,2,128]{2,1,0:T(2,128)}), f32[32,2,128]{2,1,0:T(2,128)S(1)}, u32[]{:S(2)}, u32[]{:S(2)}) %all-to-all-start) | async-done | bytes 32800 | tf_op jit(solution)/shard_map/all_to_all | solution.py:739
  49.4 0.0 collective-permute-done.9.refs_2_.refs_3_.refs_4_
  49.4 5.6 %shard_map.71 = (f32[32,512]{1,0:T(8,128)S(1)}, f32[32,512]{1,0:T(8,128)S(1)}, f32[8,512]{1,0:T(8,128)S(1)}, f32[8,512]{1,0:T(8,128)S(1)}, f32[64,128]{1,0:T(8,1...) custom-call(f32[64,128]{1,0:T(8,128)S(1)} %bitcast.12, ...), custom_call_target="tpu_custom_call" | custom-call | tf_op jit(solution)/shard_map/pallas_call | solution.py:637
  55.0 0.6 collective-permute-start.12
  55.6 1.4 %collective-permute-start.13 = (f32[32,512]{1,0:T(8,128)S(1)}, f32[32,512]{1,0:T(8,128)S(1)}, u32[]{:S(2)}, u32[]{:S(2)}) collective-permute-start(f32[32,512]{1,0:T(8,128)S(1)} %get-tuple-element.62), channel_id=1, source_target_pairs={{4,8},{8,4},{12,16},{16,12},{20,24},{24,20},{28,0},{0,28},{5,9},{9... | collective-permute-start | bytes 196616 | tf_op jit(solution)/shard_map/ppermute | solution.py:657
  57.1 3.7 %all-to-all-start.1 = ((f32[32,2,128]{2,1,0:T(2,128)}), f32[32,2,128]{2,1,0:T(2,128)S(1)}, u32[]{:S(2)}, u32[]{:S(2)}) async-start(f32[32,2,128]{2,1,0:T(2,128)} %bitcast.4), calls=%async_computation.1 | async-start | bytes 65536 | tf_op jit(solution)/shard_map/all_to_all | solution.py:739
  60.8 0.3 collective-permute-start.14
  61.1 1.6 %collective-permute-start.15 = (f32[8,512]{1,0:T(8,128)S(1)}, f32[8,512]{1,0:T(8,128)S(1)}, u32[]{:S(2)}, u32[]{:S(2)}) collective-permute-start(f32[8,512]{1,0:T(8,128)S(1)} %get-tuple-element.64), channel_id=1, source_target_pairs={{1,2},{2,1},{3,0},{0,3},{5,6},{6,5},{7,4},{4,7},{9,10},{10,9},{11,... | collective-permute-start | bytes 49160 | tf_op jit(solution)/shard_map/ppermute | solution.py:657
  62.7 1.6 %collective-permute-done.15.refs_9_.refs_10_ = f32[8,512]{1,0:T(8,128)S(1)} collective-permute-done((f32[8,512]{1,0:T(8,128)S(1)}, f32[8,512]{1,0:T(8,128)S(1)}, u32[]{:S(2)}, u32[]{:S(2)}) %collective-permute-start.15) | collective-permute-done | bytes 16416 | tf_op jit(solution)/shard_map/ppermute | solution.py:657
  64.3 3.7 %all-to-all-done.1 = f32[32,2,128]{2,1,0:T(2,128)S(1)} async-done(((f32[32,2,128]{2,1,0:T(2,128)}), f32[32,2,128]{2,1,0:T(2,128)S(1)}, u32[]{:S(2)}, u32[]{:S(2)}) %all-to-all-start.1) | async-done | bytes 32800 | tf_op jit(solution)/shard_map/all_to_all | solution.py:739
  68.1 6.2 %shard_map.72 = (f32[32,512]{1,0:T(8,128)S(1)}, f32[32,512]{1,0:T(8,128)S(1)}, f32[8,512]{1,0:T(8,128)S(1)}, f32[8,512]{1,0:T(8,128)S(1)}, f32[64,128]{1,0:T(8,1...) custom-call(f32[64,128]{1,0:T(8,128)S(1)} %bitcast.13, f32[64,128]{1,0:T(8,128)S(1)} %bitcast.15, ...), custom_call_target="tpu_custom_call" | custom-call | tf_op jit(solution)/shard_map/pallas_call | solution.py:637
  74.2 0.6 collective-permute-start.16
  74.9 1.5 %collective-permute-start.17 = (f32[32,512]{1,0:T(8,128)S(1)}, f32[32,512]{1,0:T(8,128)S(1)}, u32[]{:S(2)}, u32[]{:S(2)}) collective-permute-start(f32[32,512]{1,0:T(8,128)S(1)} %get-tuple-element.69), channel_id=1, source_target_pairs={{4,8},{8,4},{12,16},{16,12},{20,24},{24,20},{28,0},{0,28},{5,9},{9... | collective-permute-start | bytes 196616 | tf_op jit(solution)/shard_map/ppermute | solution.py:657
  76.4 3.7 %all-to-all-start.2 = ((f32[32,2,128]{2,1,0:T(2,128)}), f32[32,2,128]{2,1,0:T(2,128)S(1)}, u32[]{:S(2)}, u32[]{:S(2)}) async-start(f32[32,2,128]{2,1,0:T(2,128)} %bitcast.6), calls=%async_computation.2 | async-start | bytes 65536 | tf_op jit(solution)/shard_map/all_to_all | solution.py:739
  80.0 0.3 collective-permute-start.18
  80.4 1.6 %collective-permute-start.19 = (f32[8,512]{1,0:T(8,128)S(1)}, f32[8,512]{1,0:T(8,128)S(1)}, u32[]{:S(2)}, u32[]{:S(2)}) collective-permute-start(f32[8,512]{1,0:T(8,128)S(1)} %get-tuple-element.71), channel_id=1, source_target_pairs={{1,2},{2,1},{3,0},{0,3},{5,6},{6,5},{7,4},{4,7},{9,10},{10,9},{11,... | collective-permute-start | bytes 49160 | tf_op jit(solution)/shard_map/ppermute | solution.py:657
  82.0 1.6 %collective-permute-done.19.refs_14_ = f32[8,512]{1,0:T(8,128)S(1)} collective-permute-done((f32[8,512]{1,0:T(8,128)S(1)}, f32[8,512]{1,0:T(8,128)S(1)}, u32[]{:S(2)}, u32[]{:S(2)}) %collective-permute-start.19) | collective-permute-done | bytes 16416 | tf_op jit(solution)/shard_map/ppermute | solution.py:657
  83.6 3.7 %all-to-all-done.2 = f32[32,2,128]{2,1,0:T(2,128)S(1)} async-done(((f32[32,2,128]{2,1,0:T(2,128)}), f32[32,2,128]{2,1,0:T(2,128)S(1)}, u32[]{:S(2)}, u32[]{:S(2)}) %all-to-all-start.2) | async-done | bytes 32800 | tf_op jit(solution)/shard_map/all_to_all | solution.py:739
  87.3 3.8 %shard_map.73 = (f32[32,128]{1,0:T(8,128)S(1)}, f32[10,32,512]{2,1,0:T(8,128)S(1)}, f32[8,32,512]{2,1,0:T(8,128)S(1)}, f32[8,32,512]{2,1,0:T(8,128)S(1)}, f32[8,...) custom-call(f32[64,128]{1,0:T(8,128)S(1)} %bitcast.14, f32[64,128]{1,0:T(8,128)S(1)} %bitcast.16, ...), custom_call_target="tpu_custom_call" | custom-call | tf_op jit(solution)/shard_map/pallas_call | solution.py:637
  91.1 8.9 %all_to_all.20 = f32[32,1,128]{2,1,0:T(1,128)S(1)} all-to-all(f32[32,1,128]{2,1,0:T(1,128)S(1)} %bitcast.23), channel_id=1, replica_groups=mesh['gz'=8,'gy'=4] {'gz','gy'}, dimensions={0} | all-to-all | bytes 32768 | tf_op jit(solution)/shard_map/all_to_all | solution.py:739
  100.0 1.4 %shard_map.74 = (f32[8,32,512]{2,1,0:T(8,128)}, f32[8,32,512]{2,1,0:T(8,128)}) custom-call(f32[64,128]{1,0:T(8,128)S(1)} %bitcast.17, f32[64,128]{1,0:T(8,128)S(1)} %bitcast.19, f32[32,128]{1,0:T(8,128)S(1)} %bitcast.22, f32[10,32,512]{2,1,0:T(8,128)S(1)} %get-tuple-element.76.z_ref, f32[8,32,512]{2,1,0:T(8,128)S(1)} %get-tuple-element.77.w_ref, ...), custom_call_target="tpu_custom_call" | custom-call | tf_op jit(solution)/shard_map/pallas_call | solution.py:637
  (10 shorter events, 0.0 us)
Async XLA Ops:
  1.8 9.4 %collective-permute-start.2 = (f32[8,3,512]{2,1,0:T(4,128)S(1)}, f32[8,3,512]{2,1,0:T(4,128)S(1)}, u32[]{:S(2)}, u32[]{:S(2)}) collective-permute-start(f32[8,3,512]{2,1,0:T(4,128)S(1)} %get-tuple-element.44), channel_id=1, source_target_pairs={{0,1},{1,0},{2,3},{3,2},{4,5},{5,4},{6,7},{7,6},{8,9},{9,8},{10,11... | collective-permute-start | bytes 147464 | tf_op jit(solution)/shard_map/ppermute | solution.py:657
  2.3 8.8 %collective-permute-start.3 = (f32[8,3,512]{2,1,0:T(4,128)S(1)}, f32[8,3,512]{2,1,0:T(4,128)S(1)}, u32[]{:S(2)}, u32[]{:S(2)}) collective-permute-start(f32[8,3,512]{2,1,0:T(4,128)S(1)} %get-tuple-element.45), channel_id=1, source_target_pairs={{1,2},{2,1},{3,0},{0,3},{5,6},{6,5},{7,4},{4,7},{9,10},{10,9},{11,... | collective-permute-start | bytes 147464 | tf_op jit(solution)/shard_map/ppermute | solution.py:657
  4.9 21.1 %collective-permute-start = (f32[3,32,512]{2,1,0:T(8,128)S(1)}, f32[3,32,512]{2,1,0:T(8,128)S(1)}, u32[]{:S(2)}, u32[]{:S(2)}) collective-permute-start(f32[3,32,512]{2,1,0:T(8,128)S(1)} %get-tuple-element.42), channel_id=1, source_target_pairs={{0,4},{4,0},{8,12},{12,8},{16,20},{20,16},{24,28},{28,24},{1,5},{5... | collective-permute-start | bytes 589832 | tf_op jit(solution)/shard_map/ppermute | solution.py:657
  6.4 19.6 %collective-permute-start.1 = (f32[3,32,512]{2,1,0:T(8,128)S(1)}, f32[3,32,512]{2,1,0:T(8,128)S(1)}, u32[]{:S(2)}, u32[]{:S(2)}) collective-permute-start(f32[3,32,512]{2,1,0:T(8,128)S(1)} %get-tuple-element.43), channel_id=1, source_target_pairs={{4,8},{8,4},{12,16},{16,12},{20,24},{24,20},{28,0},{0,28},{5,9},{9... | collective-permute-start | bytes 589832 | tf_op jit(solution)/shard_map/ppermute | solution.py:657
  10.0 11.8 %collective-permute-start.7 = (f32[16,640]{1,0:T(8,128)S(1)}, f32[16,640]{1,0:T(8,128)S(1)}, u32[]{:S(2)}, u32[]{:S(2)}) collective-permute-start(f32[16,640]{1,0:T(8,128)S(1)} %get-tuple-element.46), channel_id=1, source_target_pairs={{4,8},{8,4},{12,16},{16,12},{20,24},{24,20},{28,0},{0,28},{5,9},{9... | collective-permute-start | bytes 122888 | tf_op jit(solution)/shard_map/ppermute | solution.py:657
  11.2 7.7 %collective-permute-start.6 = (f32[16,640]{1,0:T(8,128)S(1)}, f32[16,640]{1,0:T(8,128)S(1)}, u32[]{:S(2)}, u32[]{:S(2)}) collective-permute-start(f32[16,640]{1,0:T(8,128)S(1)} %get-tuple-element.46), channel_id=1, source_target_pairs={{0,4},{4,0},{8,12},{12,8},{16,20},{20,16},{24,28},{28,24},{1,5},{5... | collective-permute-start | bytes 122888 | tf_op jit(solution)/shard_map/ppermute | solution.py:657
  11.2 14.8 %collective-permute-start.5 = (f32[2,3,3,512]{3,2,1,0:T(4,128)S(1)}, f32[2,3,3,512]{3,2,1,0:T(4,128)S(1)}, u32[]{:S(2)}, u32[]{:S(2)}) collective-permute-start(f32[2,3,3,512]{3,2,1,0:T(4,128)S(1)} %get-tuple-element.82), channel_id=1, source_target_pairs={{4,8},{8,4},{12,16},{16,12},{20,24},{24,20},{28,0},{0,28},{5,9},{9... | collective-permute-start | bytes 110600 | tf_op jit(solution)/shard_map/ppermute | solution.py:657
  18.8 7.2 %collective-permute-start.4 = (f32[2,3,3,512]{3,2,1,0:T(4,128)S(1)}, f32[2,3,3,512]{3,2,1,0:T(4,128)S(1)}, u32[]{:S(2)}, u32[]{:S(2)}) collective-permute-start(f32[2,3,3,512]{3,2,1,0:T(4,128)S(1)} %get-tuple-element.83), channel_id=1, source_target_pairs={{0,4},{4,0},{8,12},{12,8},{16,20},{20,16},{24,28},{28,24},{1,5},{5... | collective-permute-start | bytes 110600 | tf_op jit(solution)/shard_map/ppermute | solution.py:657
  34.4 15.0 %collective-permute-start.8 = (f32[2,32,512]{2,1,0:T(8,128)S(1)}, f32[2,32,512]{2,1,0:T(8,128)S(1)}, u32[]{:S(2)}, u32[]{:S(2)}) collective-permute-start(f32[2,32,512]{2,1,0:T(8,128)S(1)} %get-tuple-element.48), channel_id=1, source_target_pairs={{0,4},{4,0},{8,12},{12,8},{16,20},{20,16},{24,28},{28,24},{1,5},{5... | collective-permute-start | bytes 393224 | tf_op jit(solution)/shard_map/ppermute | solution.py:657
  35.0 14.4 %collective-permute-start.9 = (f32[2,32,512]{2,1,0:T(8,128)S(1)}, f32[2,32,512]{2,1,0:T(8,128)S(1)}, u32[]{:S(2)}, u32[]{:S(2)}) collective-permute-start(f32[2,32,512]{2,1,0:T(8,128)S(1)} %get-tuple-element.49), channel_id=1, source_target_pairs={{4,8},{8,4},{12,16},{16,12},{20,24},{24,20},{28,0},{0,28},{5,9},{9... | collective-permute-start | bytes 393224 | tf_op jit(solution)/shard_map/ppermute | solution.py:657
  39.5 9.8 %all-to-all-start = ((f32[32,2,128]{2,1,0:T(2,128)}), f32[32,2,128]{2,1,0:T(2,128)S(1)}, u32[]{:S(2)}, u32[]{:S(2)}) async-start(f32[32,2,128]{2,1,0:T(2,128)} %bitcast.2), calls=%async_computation | async-start | bytes 65536 | tf_op jit(solution)/shard_map/all_to_all | solution.py:739
  42.1 1.8 %collective-permute-start.10 = (f32[2,8,512]{2,1,0:T(8,128)S(1)}, f32[2,8,512]{2,1,0:T(8,128)S(1)}, u32[]{:S(2)}, u32[]{:S(2)}) collective-permute-start(f32[2,8,512]{2,1,0:T(8,128)S(1)} %get-tuple-element.50), channel_id=1, source_target_pairs={{0,1},{1,0},{2,3},{3,2},{4,5},{5,4},{6,7},{7,6},{8,9},{9,8},{10,11... | collective-permute-start | bytes 98312 | tf_op jit(solution)/shard_map/ppermute | solution.py:657
  42.3 3.4 %collective-permute-start.11 = (f32[2,8,512]{2,1,0:T(8,128)S(1)}, f32[2,8,512]{2,1,0:T(8,128)S(1)}, u32[]{:S(2)}, u32[]{:S(2)}) collective-permute-start(f32[2,8,512]{2,1,0:T(8,128)S(1)} %get-tuple-element.51), channel_id=1, source_target_pairs={{1,2},{2,1},{3,0},{0,3},{5,6},{6,5},{7,4},{4,7},{9,10},{10,9},{11,... | collective-permute-start | bytes 98312 | tf_op jit(solution)/shard_map/ppermute | solution.py:657
  55.0 13.1 %collective-permute-start.12 = (f32[32,512]{1,0:T(8,128)S(1)}, f32[32,512]{1,0:T(8,128)S(1)}, u32[]{:S(2)}, u32[]{:S(2)}) collective-permute-start(f32[32,512]{1,0:T(8,128)S(1)} %get-tuple-element.61), channel_id=1, source_target_pairs={{0,4},{4,0},{8,12},{12,8},{16,20},{20,16},{24,28},{28,24},{1,5},{5... | collective-permute-start | bytes 196616 | tf_op jit(solution)/shard_map/ppermute | solution.py:657
  55.6 12.4 %collective-permute-start.13 = (f32[32,512]{1,0:T(8,128)S(1)}, f32[32,512]{1,0:T(8,128)S(1)}, u32[]{:S(2)}, u32[]{:S(2)}) collective-permute-start(f32[32,512]{1,0:T(8,128)S(1)} %get-tuple-element.62), channel_id=1, source_target_pairs={{4,8},{8,4},{12,16},{16,12},{20,24},{24,20},{28,0},{0,28},{5,9},{9... | collective-permute-start | bytes 196616 | tf_op jit(solution)/shard_map/ppermute | solution.py:657
  57.1 11.0 %all-to-all-start.1 = ((f32[32,2,128]{2,1,0:T(2,128)}), f32[32,2,128]{2,1,0:T(2,128)S(1)}, u32[]{:S(2)}, u32[]{:S(2)}) async-start(f32[32,2,128]{2,1,0:T(2,128)} %bitcast.4), calls=%async_computation.1 | async-start | bytes 65536 | tf_op jit(solution)/shard_map/all_to_all | solution.py:739
  60.8 2.0 %collective-permute-start.14 = (f32[8,512]{1,0:T(8,128)S(1)}, f32[8,512]{1,0:T(8,128)S(1)}, u32[]{:S(2)}, u32[]{:S(2)}) collective-permute-start(f32[8,512]{1,0:T(8,128)S(1)} %get-tuple-element.63), channel_id=1, source_target_pairs={{0,1},{1,0},{2,3},{3,2},{4,5},{5,4},{6,7},{7,6},{8,9},{9,8},{10,11... | collective-permute-start | bytes 49160 | tf_op jit(solution)/shard_map/ppermute | solution.py:657
  61.1 3.2 %collective-permute-start.15 = (f32[8,512]{1,0:T(8,128)S(1)}, f32[8,512]{1,0:T(8,128)S(1)}, u32[]{:S(2)}, u32[]{:S(2)}) collective-permute-start(f32[8,512]{1,0:T(8,128)S(1)} %get-tuple-element.64), channel_id=1, source_target_pairs={{1,2},{2,1},{3,0},{0,3},{5,6},{6,5},{7,4},{4,7},{9,10},{10,9},{11,... | collective-permute-start | bytes 49160 | tf_op jit(solution)/shard_map/ppermute | solution.py:657
  74.2 13.1 %collective-permute-start.16 = (f32[32,512]{1,0:T(8,128)S(1)}, f32[32,512]{1,0:T(8,128)S(1)}, u32[]{:S(2)}, u32[]{:S(2)}) collective-permute-start(f32[32,512]{1,0:T(8,128)S(1)} %get-tuple-element.68), channel_id=1, source_target_pairs={{0,4},{4,0},{8,12},{12,8},{16,20},{20,16},{24,28},{28,24},{1,5},{5... | collective-permute-start | bytes 196616 | tf_op jit(solution)/shard_map/ppermute | solution.py:657
  74.9 12.4 %collective-permute-start.17 = (f32[32,512]{1,0:T(8,128)S(1)}, f32[32,512]{1,0:T(8,128)S(1)}, u32[]{:S(2)}, u32[]{:S(2)}) collective-permute-start(f32[32,512]{1,0:T(8,128)S(1)} %get-tuple-element.69), channel_id=1, source_target_pairs={{4,8},{8,4},{12,16},{16,12},{20,24},{24,20},{28,0},{0,28},{5,9},{9... | collective-permute-start | bytes 196616 | tf_op jit(solution)/shard_map/ppermute | solution.py:657
  76.4 10.9 %all-to-all-start.2 = ((f32[32,2,128]{2,1,0:T(2,128)}), f32[32,2,128]{2,1,0:T(2,128)S(1)}, u32[]{:S(2)}, u32[]{:S(2)}) async-start(f32[32,2,128]{2,1,0:T(2,128)} %bitcast.6), calls=%async_computation.2 | async-start | bytes 65536 | tf_op jit(solution)/shard_map/all_to_all | solution.py:739
  80.0 2.0 %collective-permute-start.18 = (f32[8,512]{1,0:T(8,128)S(1)}, f32[8,512]{1,0:T(8,128)S(1)}, u32[]{:S(2)}, u32[]{:S(2)}) collective-permute-start(f32[8,512]{1,0:T(8,128)S(1)} %get-tuple-element.70), channel_id=1, source_target_pairs={{0,1},{1,0},{2,3},{3,2},{4,5},{5,4},{6,7},{7,6},{8,9},{9,8},{10,11... | collective-permute-start | bytes 49160 | tf_op jit(solution)/shard_map/ppermute | solution.py:657
  80.4 3.2 %collective-permute-start.19 = (f32[8,512]{1,0:T(8,128)S(1)}, f32[8,512]{1,0:T(8,128)S(1)}, u32[]{:S(2)}, u32[]{:S(2)}) collective-permute-start(f32[8,512]{1,0:T(8,128)S(1)} %get-tuple-element.71), channel_id=1, source_target_pairs={{1,2},{2,1},{3,0},{0,3},{5,6},{6,5},{7,4},{4,7},{9,10},{10,9},{11,... | collective-permute-start | bytes 49160 | tf_op jit(solution)/shard_map/ppermute | solution.py:657

commit v6 on v5

--- a/solution.py
+++ b/solution.py
@@ -654,7 +654,22 @@
 
 
 def swap(block, axis, first):
+    if axis == "gz" and first == 1:
+        return lax.ppermute(block, ("gz", "gy"), inner_swaps())
     return lax.ppermute(block, axis, swaps(axis, first))
+
+
+def inner_swaps():
+    slabs, columns = lax.axis_size("gz"), lax.axis_size("gy")
+    pairs = []
+    for slab in range(slabs):
+        for column in range(columns):
+            if slab in (0, slabs - 1):
+                target = slab * columns + (column ^ 1)
+            else:
+                target = (slab + 1 if slab % 2 else slab - 1) * columns + column
+            pairs.append((slab * columns + column, target))
+    return pairs
 
 
 def solve(fraction, source, bubble_label, subdomain, coarse_inverse):

time: 102 us -> 96.7 us (0.948)
  starting transfers between devices: 39.5 us -> 30.7 us
  waiting for transfers between devices: 20.1 us -> 23.8 us
    ppermute x20 -> x14, starting transfers between devices: 29.5 us -> 17.2 us  [swap(): return lax.ppermute(block, axis, swaps(axis, first))]
    ppermute x20 -> x14, waiting for transfers between devices: 8.93 us -> 12.8 us  [swap(): return lax.ppermute(block, axis, swaps(axis, first))]
    all_to_all x3, starting transfers between devices: 9.97 us -> 12.8 us  [exchange(): return lax.all_to_all(blocks, ('gz', 'gy'), 0, 0).reshape(parts.shape)]
where the time goes in v6:
time: 96.7 us; the launch traced here: 96.3 us
  starting transfers between devices  30.7 us (32%)
  Pallas kernels  30.3 us (31%)
  waiting for transfers between devices  23.8 us (25%)
  blocking collectives  8.94 us (9%)
  local copies, waits for them, and re-layouts  1.73 us (2%)
    pallas_call x7, Pallas kernels, call(): pl.pallas_call(kernel, out_shape=made, in_specs=specs(args), out_specs=sp...  30.3 us
    ppermute x14, starting transfers between devices, swap(): return lax.ppermute(block, axis, swaps(axis, first))  17.2 us
    all_to_all x3, starting transfers between devices, exchange(): return lax.all_to_all(blocks, ('gz', 'gy'), 0, 0).reshape(parts.shape)  12.8 us
    ppermute x14, waiting for transfers between devices, swap(): return lax.ppermute(block, axis, swaps(axis, first))  12.8 us
    all_to_all x3, waiting for transfers between devices, exchange(): return lax.all_to_all(blocks, ('gz', 'gy'), 0, 0).reshape(parts.shape)  11 us
    all_to_all x1, blocking collectives, exchange(): return lax.all_to_all(blocks, ('gz', 'gy'), 0, 0).reshape(parts.shape)  8.94 us
  transfers between devices with their start and end apart: 23, of which 7 were waited for; matrix products, arithmetic and copies ran while one was open for 2% of the time, Pallas kernels for 4%

profile of v6, /device:TPU:0, one launch (start us, length us, event | category | flops | bytes accessed | tf_op | source)
XLA Modules:
  0.0 96.3 jit_solution(10689433054156761881)
XLA Ops:
  0.6 1.1 %shard_map.68 = (f32[3,32,512]{2,1,0:T(8,128)S(1)}, f32[3,32,512]{2,1,0:T(8,128)S(1)}, f32[8,3,512]{2,1,0:T(4,128)S(1)}, f32[8,3,512]{2,1,0:T(4,128)S(1)}, f32[16,640]{1,0:T(8,128)S(1)}) custom-call(f32[8,32,512]{2,1,0:T(8,128)} %frac_hbm.3, f32[20,640]{1,0:T(8,128)} %coarse_hbm.1), custom_call_target="tpu_custom_call" | custom-call | tf_op jit(solution)/shard_map/pallas_call | solution.py:637
  1.8 0.6 collective-permute-start.2
  2.3 2.6 %collective-permute-start.3 = (f32[8,3,512]{2,1,0:T(4,128)S(1)}, f32[8,3,512]{2,1,0:T(4,128)S(1)}, u32[]{:S(2)}, u32[]{:S(2)}) collective-permute-start(f32[8,3,512]{2,1,0:T(4,128)S(1)} %get-tuple-element.45), channel_id=1, source_target_pairs={{1,2},{2,1},{3,0},{0,3},{5,6},{6,5},{7,4},{4,7},{9,10},{10,9},{11,... | collective-permute-start | bytes 147464 | tf_op jit(solution)/shard_map/ppermute | solution.py:659
  4.9 1.5 %collective-permute-start = (f32[3,32,512]{2,1,0:T(8,128)S(1)}, f32[3,32,512]{2,1,0:T(8,128)S(1)}, u32[]{:S(2)}, u32[]{:S(2)}) collective-permute-start(f32[3,32,512]{2,1,0:T(8,128)S(1)} %get-tuple-element.42), channel_id=1, source_target_pairs={{0,4},{4,0},{8,12},{12,8},{16,20},{20,16},{24,28},{28,24},{1,5},{5... | collective-permute-start | bytes 589832 | tf_op jit(solution)/shard_map/ppermute | solution.py:659
  6.4 0.0 collective-permute-start.1
  6.4 0.5 collective-permute-start.7
  6.9 0.0 collective-permute-done.2.y0_in
  6.9 2.9 %collective-permute-start.6 = (f32[16,640]{1,0:T(8,128)S(1)}, f32[16,640]{1,0:T(8,128)S(1)}, u32[]{:S(2)}, u32[]{:S(2)}) collective-permute-start(f32[16,640]{1,0:T(8,128)S(1)} %get-tuple-element.46), channel_id=1, source_target_pairs={{0,4},{4,0},{8,12},{12,8},{16,20},{20,16},{24,28},{28,24},{1,5},{5... | collective-permute-start | bytes 122888 | tf_op jit(solution)/shard_map/ppermute | solution.py:659
  9.9 0.0 collective-permute-done.3.y1_in
  9.9 0.1 collective-permute-start.5
  10.0 7.9 %collective-permute-done.6 = f32[16,640]{1,0:T(8,128)S(1)} collective-permute-done((f32[16,640]{1,0:T(8,128)S(1)}, f32[16,640]{1,0:T(8,128)S(1)}, u32[]{:S(2)}, u32[]{:S(2)}) %collective-permute-start.6) | collective-permute-done | bytes 40992 | tf_op jit(solution)/shard_map/ppermute | solution.py:659
  17.9 2.5 %collective-permute-start.4 = (f32[2,3,3,512]{3,2,1,0:T(4,128)S(1)}, f32[2,3,3,512]{3,2,1,0:T(4,128)S(1)}, u32[]{:S(2)}, u32[]{:S(2)}) collective-permute-start(f32[2,3,3,512]{3,2,1,0:T(4,128)S(1)} %get-tuple-element.83), channel_id=1, source_target_pairs={{0,4},{4,0},{8,12},{12,8},{16,20},{20,16},{24,28},{28,24},{1,5},{5... | collective-permute-start | bytes 110600 | tf_op jit(solution)/shard_map/ppermute | solution.py:659
  20.3 1.2 %reshape.37.own_ref = f32[20,32,20]{2,1,0:T(8,128)S(1)} reshape(f32[20,640]{1,0:T(8,128)} %coarse_hbm.1) | data formatting | bytes 102400 | tf_op jit(solution)/shard_map/reshape | solution.py:714
  21.5 0.3 reshape.38.near_ref
  21.8 0.0 collective-permute-done.7
  21.8 0.3 reshape.39.far_ref
  22.1 3.9 %shard_map.69.dest_hbm.refs_13_.refs_20_ = f32[52,64,128]{2,1,0:T(8,128)} custom-call(f32[20,32,20]{2,1,0:T(8,128)S(1)} %reshape.37.own_ref, f32[16,32,20]{2,1,0:T(8,128)S(1)} %reshape.38.near_ref, f32[16,32,20]{2,1,0:T(8,128)S(1)} %reshape.39.far_ref), custom_call_target="tpu_custom_call" | custom-call | tf_op jit(solution)/shard_map/pallas_call | solution.py:637
  26.0 0.0 collective-permute-done.5.k1_in
  26.0 0.0 collective-permute-done.1.z1_in
  26.0 8.4 %shard_map.70 = (f32[2,32,512]{2,1,0:T(8,128)S(1)}, f32[2,32,512]{2,1,0:T(8,128)S(1)}, f32[2,8,512]{2,1,0:T(8,128)S(1)}, f32[2,8,512]{2,1,0:T(8,128)S(1)}, f32[6...) custom-call(f32[3,32,512]{2,1,0:T(8,128)S(1)} %collective-permute-do, ...), custom_call_target="tpu_custom_call" | custom-call | tf_op jit(solution)/shard_map/pallas_call | solution.py:637
  34.4 0.1 collective-permute-start.8
  34.5 0.1 collective-permute-start.9
  34.6 5.8 %all-to-all-start = ((f32[32,2,128]{2,1,0:T(2,128)}), f32[32,2,128]{2,1,0:T(2,128)S(1)}, u32[]{:S(2)}, u32[]{:S(2)}) async-start(f32[32,2,128]{2,1,0:T(2,128)} %bitcast.2), calls=%async_computation | async-start | bytes 65536 | tf_op jit(solution)/shard_map/all_to_all | solution.py:754
  40.4 0.3 collective-permute-start.10
  40.7 1.6 %collective-permute-start.11 = (f32[2,8,512]{2,1,0:T(8,128)S(1)}, f32[2,8,512]{2,1,0:T(8,128)S(1)}, u32[]{:S(2)}, u32[]{:S(2)}) collective-permute-start(f32[2,8,512]{2,1,0:T(8,128)S(1)} %get-tuple-element.51), channel_id=1, source_target_pairs={{1,2},{2,1},{3,0},{0,3},{5,6},{6,5},{7,4},{4,7},{9,10},{10,9},{11,... | collective-permute-start | bytes 98312 | tf_op jit(solution)/shard_map/ppermute | solution.py:659
  42.4 1.7 %collective-permute-done.11.refs_4_.refs_5_.refs_6_ = f32[2,8,512]{2,1,0:T(8,128)S(1)} collective-permute-done((f32[2,8,512]{2,1,0:T(8,128)S(1)}, f32[2,8,512]{2,1,0:T(8,128)S(1)}, u32[]{:S(2)}, u32[]{:S(2)}) %collective-permute-start.11) | collective-permute-done | bytes 32800 | tf_op jit(solution)/shard_map/ppermute | solution.py:659
  44.1 3.6 %all-to-all-done = f32[32,2,128]{2,1,0:T(2,128)S(1)} async-done(((f32[32,2,128]{2,1,0:T(2,128)}), f32[32,2,128]{2,1,0:T(2,128)S(1)}, u32[]{:S(2)}, u32[]{:S(2)}) %all-to-all-start) | async-done | bytes 32800 | tf_op jit(solution)/shard_map/all_to_all | solution.py:754
  47.7 0.0 collective-permute-done.8.refs_1_.refs_2_.refs_3_
  47.7 5.6 %shard_map.71 = (f32[32,512]{1,0:T(8,128)S(1)}, f32[32,512]{1,0:T(8,128)S(1)}, f32[8,512]{1,0:T(8,128)S(1)}, f32[8,512]{1,0:T(8,128)S(1)}, f32[64,128]{1,0:T(8,1...) custom-call(f32[64,128]{1,0:T(8,128)S(1)} %bitcast.12, ...), custom_call_target="tpu_custom_call" | custom-call | tf_op jit(solution)/shard_map/pallas_call | solution.py:637
  53.3 0.6 collective-permute-start.12
  53.9 3.6 %all-to-all-start.1 = ((f32[32,2,128]{2,1,0:T(2,128)}), f32[32,2,128]{2,1,0:T(2,128)S(1)}, u32[]{:S(2)}, u32[]{:S(2)}) async-start(f32[32,2,128]{2,1,0:T(2,128)} %bitcast.4), calls=%async_computation.1 | async-start | bytes 65536 | tf_op jit(solution)/shard_map/all_to_all | solution.py:754
  57.5 0.3 collective-permute-start.14
  57.8 1.6 %collective-permute-start.15 = (f32[8,512]{1,0:T(8,128)S(1)}, f32[8,512]{1,0:T(8,128)S(1)}, u32[]{:S(2)}, u32[]{:S(2)}) collective-permute-start(f32[8,512]{1,0:T(8,128)S(1)} %get-tuple-element.64), channel_id=1, source_target_pairs={{1,2},{2,1},{3,0},{0,3},{5,6},{6,5},{7,4},{4,7},{9,10},{10,9},{11,... | collective-permute-start | bytes 49160 | tf_op jit(solution)/shard_map/ppermute | solution.py:659
  59.5 1.6 %collective-permute-done.15.refs_9_.refs_10_ = f32[8,512]{1,0:T(8,128)S(1)} collective-permute-done((f32[8,512]{1,0:T(8,128)S(1)}, f32[8,512]{1,0:T(8,128)S(1)}, u32[]{:S(2)}, u32[]{:S(2)}) %collective-permute-start.15) | collective-permute-done | bytes 16416 | tf_op jit(solution)/shard_map/ppermute | solution.py:659
  61.0 3.7 %all-to-all-done.1 = f32[32,2,128]{2,1,0:T(2,128)S(1)} async-done(((f32[32,2,128]{2,1,0:T(2,128)}), f32[32,2,128]{2,1,0:T(2,128)S(1)}, u32[]{:S(2)}, u32[]{:S(2)}) %all-to-all-start.1) | async-done | bytes 32800 | tf_op jit(solution)/shard_map/all_to_all | solution.py:754
  64.8 0.0 collective-permute-done.12.refs_6_.refs_7_
  64.8 6.2 %shard_map.72 = (f32[32,512]{1,0:T(8,128)S(1)}, f32[32,512]{1,0:T(8,128)S(1)}, f32[8,512]{1,0:T(8,128)S(1)}, f32[8,512]{1,0:T(8,128)S(1)}, f32[64,128]{1,0:T(8,1...) custom-call(f32[64,128]{1,0:T(8,128)S(1)} %bitcast.13, f32[64,128]{1,0:T(8,128)S(1)} %bitcast.15, ...), custom_call_target="tpu_custom_call" | custom-call | tf_op jit(solution)/shard_map/pallas_call | solution.py:637
  71.0 0.6 collective-permute-start.16
  71.6 3.4 %all-to-all-start.2 = ((f32[32,2,128]{2,1,0:T(2,128)}), f32[32,2,128]{2,1,0:T(2,128)S(1)}, u32[]{:S(2)}, u32[]{:S(2)}) async-start(f32[32,2,128]{2,1,0:T(2,128)} %bitcast.6), calls=%async_computation.2 | async-start | bytes 65536 | tf_op jit(solution)/shard_map/all_to_all | solution.py:754
  75.0 0.3 collective-permute-start.18
  75.3 1.6 %collective-permute-start.19 = (f32[8,512]{1,0:T(8,128)S(1)}, f32[8,512]{1,0:T(8,128)S(1)}, u32[]{:S(2)}, u32[]{:S(2)}) collective-permute-start(f32[8,512]{1,0:T(8,128)S(1)} %get-tuple-element.71), channel_id=1, source_target_pairs={{1,2},{2,1},{3,0},{0,3},{5,6},{6,5},{7,4},{4,7},{9,10},{10,9},{11,... | collective-permute-start | bytes 49160 | tf_op jit(solution)/shard_map/ppermute | solution.py:659
  77.0 0.0 collective-permute-done.18.refs_13_
  77.0 1.6 %collective-permute-done.19.refs_14_ = f32[8,512]{1,0:T(8,128)S(1)} collective-permute-done((f32[8,512]{1,0:T(8,128)S(1)}, f32[8,512]{1,0:T(8,128)S(1)}, u32[]{:S(2)}, u32[]{:S(2)}) %collective-permute-start.19) | collective-permute-done | bytes 16416 | tf_op jit(solution)/shard_map/ppermute | solution.py:659
  78.5 3.7 %all-to-all-done.2 = f32[32,2,128]{2,1,0:T(2,128)S(1)} async-done(((f32[32,2,128]{2,1,0:T(2,128)}), f32[32,2,128]{2,1,0:T(2,128)S(1)}, u32[]{:S(2)}, u32[]{:S(2)}) %all-to-all-start.2) | async-done | bytes 32800 | tf_op jit(solution)/shard_map/all_to_all | solution.py:754
  82.3 0.0 collective-permute-done.17.refs_12_
  82.3 3.8 %shard_map.73 = (f32[32,128]{1,0:T(8,128)S(1)}, f32[10,32,512]{2,1,0:T(8,128)S(1)}, f32[8,32,512]{2,1,0:T(8,128)S(1)}, f32[8,32,512]{2,1,0:T(8,128)S(1)}, f32[8,...) custom-call(f32[64,128]{1,0:T(8,128)S(1)} %bitcast.14, f32[64,128]{1,0:T(8,128)S(1)} %bitcast.16, ...), custom_call_target="tpu_custom_call" | custom-call | tf_op jit(solution)/shard_map/pallas_call | solution.py:637
  86.1 8.9 %all_to_all.20 = f32[32,1,128]{2,1,0:T(1,128)S(1)} all-to-all(f32[32,1,128]{2,1,0:T(1,128)S(1)} %bitcast.23), channel_id=1, replica_groups=mesh['gz'=8,'gy'=4] {'gz','gy'}, dimensions={0} | all-to-all | bytes 32768 | tf_op jit(solution)/shard_map/all_to_all | solution.py:754
  95.0 1.4 %shard_map.74 = (f32[8,32,512]{2,1,0:T(8,128)}, f32[8,32,512]{2,1,0:T(8,128)}) custom-call(f32[64,128]{1,0:T(8,128)S(1)} %bitcast.17, f32[64,128]{1,0:T(8,128)S(1)} %bitcast.19, f32[32,128]{1,0:T(8,128)S(1)} %bitcast.22, f32[10,32,512]{2,1,0:T(8,128)S(1)} %get-tuple-element.76.z_ref, f32[8,32,512]{2,1,0:T(8,128)S(1)} %get-tuple-element.77.w_ref, ...), custom_call_target="tpu_custom_call" | custom-call | tf_op jit(solution)/shard_map/pallas_call | solution.py:637
  (10 shorter events, 0.0 us)
Async XLA Ops:
  1.8 5.2 %collective-permute-start.2 = (f32[8,3,512]{2,1,0:T(4,128)S(1)}, f32[8,3,512]{2,1,0:T(4,128)S(1)}, u32[]{:S(2)}, u32[]{:S(2)}) collective-permute-start(f32[8,3,512]{2,1,0:T(4,128)S(1)} %get-tuple-element.44), channel_id=1, source_target_pairs={{0,1},{1,0},{2,3},{3,2},{4,5},{5,4},{6,7},{7,6},{8,9},{9,8},{10,11... | collective-permute-start | bytes 147464 | tf_op jit(solution)/shard_map/ppermute | solution.py:659
  2.3 7.5 %collective-permute-start.3 = (f32[8,3,512]{2,1,0:T(4,128)S(1)}, f32[8,3,512]{2,1,0:T(4,128)S(1)}, u32[]{:S(2)}, u32[]{:S(2)}) collective-permute-start(f32[8,3,512]{2,1,0:T(4,128)S(1)} %get-tuple-element.45), channel_id=1, source_target_pairs={{1,2},{2,1},{3,0},{0,3},{5,6},{6,5},{7,4},{4,7},{9,10},{10,9},{11,... | collective-permute-start | bytes 147464 | tf_op jit(solution)/shard_map/ppermute | solution.py:659
  4.9 21.1 %collective-permute-start = (f32[3,32,512]{2,1,0:T(8,128)S(1)}, f32[3,32,512]{2,1,0:T(8,128)S(1)}, u32[]{:S(2)}, u32[]{:S(2)}) collective-permute-start(f32[3,32,512]{2,1,0:T(8,128)S(1)} %get-tuple-element.42), channel_id=1, source_target_pairs={{0,4},{4,0},{8,12},{12,8},{16,20},{20,16},{24,28},{28,24},{1,5},{5... | collective-permute-start | bytes 589832 | tf_op jit(solution)/shard_map/ppermute | solution.py:659
  6.4 19.6 %collective-permute-start.1 = (f32[3,32,512]{2,1,0:T(8,128)S(1)}, f32[3,32,512]{2,1,0:T(8,128)S(1)}, u32[]{:S(2)}, u32[]{:S(2)}) collective-permute-start(f32[3,32,512]{2,1,0:T(8,128)S(1)} %get-tuple-element.43), channel_id=1, source_target_pairs={{0,1},{1,0},{2,3},{3,2},{4,8},{5,9},{6,10},{7,11},{8,4},{9,5},{10,... | collective-permute-start | bytes 589832 | tf_op jit(solution)/shard_map/ppermute | solution.py:658
  6.4 15.4 %collective-permute-start.7 = (f32[16,640]{1,0:T(8,128)S(1)}, f32[16,640]{1,0:T(8,128)S(1)}, u32[]{:S(2)}, u32[]{:S(2)}) collective-permute-start(f32[16,640]{1,0:T(8,128)S(1)} %get-tuple-element.46), channel_id=1, source_target_pairs={{0,1},{1,0},{2,3},{3,2},{4,8},{5,9},{6,10},{7,11},{8,4},{9,5},{10,... | collective-permute-start | bytes 122888 | tf_op jit(solution)/shard_map/ppermute | solution.py:658
  6.9 10.9 %collective-permute-start.6 = (f32[16,640]{1,0:T(8,128)S(1)}, f32[16,640]{1,0:T(8,128)S(1)}, u32[]{:S(2)}, u32[]{:S(2)}) collective-permute-start(f32[16,640]{1,0:T(8,128)S(1)} %get-tuple-element.46), channel_id=1, source_target_pairs={{0,4},{4,0},{8,12},{12,8},{16,20},{20,16},{24,28},{28,24},{1,5},{5... | collective-permute-start | bytes 122888 | tf_op jit(solution)/shard_map/ppermute | solution.py:659
  9.9 16.1 %collective-permute-start.5 = (f32[2,3,3,512]{3,2,1,0:T(4,128)S(1)}, f32[2,3,3,512]{3,2,1,0:T(4,128)S(1)}, u32[]{:S(2)}, u32[]{:S(2)}) collective-permute-start(f32[2,3,3,512]{3,2,1,0:T(4,128)S(1)} %get-tuple-element.82), channel_id=1, source_target_pairs={{0,1},{1,0},{2,3},{3,2},{4,8},{5,9},{6,10},{7,11},{8,4},{9,5},{10,... | collective-permute-start | bytes 110600 | tf_op jit(solution)/shard_map/ppermute | solution.py:658
  17.9 8.1 %collective-permute-start.4 = (f32[2,3,3,512]{3,2,1,0:T(4,128)S(1)}, f32[2,3,3,512]{3,2,1,0:T(4,128)S(1)}, u32[]{:S(2)}, u32[]{:S(2)}) collective-permute-start(f32[2,3,3,512]{3,2,1,0:T(4,128)S(1)} %get-tuple-element.83), channel_id=1, source_target_pairs={{0,4},{4,0},{8,12},{12,8},{16,20},{20,16},{24,28},{28,24},{1,5},{5... | collective-permute-start | bytes 110600 | tf_op jit(solution)/shard_map/ppermute | solution.py:659
  34.4 13.3 %collective-permute-start.8 = (f32[2,32,512]{2,1,0:T(8,128)S(1)}, f32[2,32,512]{2,1,0:T(8,128)S(1)}, u32[]{:S(2)}, u32[]{:S(2)}) collective-permute-start(f32[2,32,512]{2,1,0:T(8,128)S(1)} %get-tuple-element.48), channel_id=1, source_target_pairs={{0,4},{4,0},{8,12},{12,8},{16,20},{20,16},{24,28},{28,24},{1,5},{5... | collective-permute-start | bytes 393224 | tf_op jit(solution)/shard_map/ppermute | solution.py:659
  34.5 13.2 %collective-permute-start.9 = (f32[2,32,512]{2,1,0:T(8,128)S(1)}, f32[2,32,512]{2,1,0:T(8,128)S(1)}, u32[]{:S(2)}, u32[]{:S(2)}) collective-permute-start(f32[2,32,512]{2,1,0:T(8,128)S(1)} %get-tuple-element.49), channel_id=1, source_target_pairs={{0,1},{1,0},{2,3},{3,2},{4,8},{5,9},{6,10},{7,11},{8,4},{9,5},{10,... | collective-permute-start | bytes 393224 | tf_op jit(solution)/shard_map/ppermute | solution.py:658
  34.6 13.1 %all-to-all-start = ((f32[32,2,128]{2,1,0:T(2,128)}), f32[32,2,128]{2,1,0:T(2,128)S(1)}, u32[]{:S(2)}, u32[]{:S(2)}) async-start(f32[32,2,128]{2,1,0:T(2,128)} %bitcast.2), calls=%async_computation | async-start | bytes 65536 | tf_op jit(solution)/shard_map/all_to_all | solution.py:754
  40.4 2.0 %collective-permute-start.10 = (f32[2,8,512]{2,1,0:T(8,128)S(1)}, f32[2,8,512]{2,1,0:T(8,128)S(1)}, u32[]{:S(2)}, u32[]{:S(2)}) collective-permute-start(f32[2,8,512]{2,1,0:T(8,128)S(1)} %get-tuple-element.50), channel_id=1, source_target_pairs={{0,1},{1,0},{2,3},{3,2},{4,5},{5,4},{6,7},{7,6},{8,9},{9,8},{10,11... | collective-permute-start | bytes 98312 | tf_op jit(solution)/shard_map/ppermute | solution.py:659
  40.7 3.4 %collective-permute-start.11 = (f32[2,8,512]{2,1,0:T(8,128)S(1)}, f32[2,8,512]{2,1,0:T(8,128)S(1)}, u32[]{:S(2)}, u32[]{:S(2)}) collective-permute-start(f32[2,8,512]{2,1,0:T(8,128)S(1)} %get-tuple-element.51), channel_id=1, source_target_pairs={{1,2},{2,1},{3,0},{0,3},{5,6},{6,5},{7,4},{4,7},{9,10},{10,9},{11,... | collective-permute-start | bytes 98312 | tf_op jit(solution)/shard_map/ppermute | solution.py:659
  53.3 11.5 %collective-permute-start.12 = (f32[32,512]{1,0:T(8,128)S(1)}, f32[32,512]{1,0:T(8,128)S(1)}, u32[]{:S(2)}, u32[]{:S(2)}) collective-permute-start(f32[32,512]{1,0:T(8,128)S(1)} %get-tuple-element.61), channel_id=1, source_target_pairs={{0,4},{4,0},{8,12},{12,8},{16,20},{20,16},{24,28},{28,24},{1,5},{5... | collective-permute-start | bytes 196616 | tf_op jit(solution)/shard_map/ppermute | solution.py:659
  53.9 10.9 %collective-permute-start.13 = (f32[32,512]{1,0:T(8,128)S(1)}, f32[32,512]{1,0:T(8,128)S(1)}, u32[]{:S(2)}, u32[]{:S(2)}) collective-permute-start(f32[32,512]{1,0:T(8,128)S(1)} %get-tuple-element.62), channel_id=1, source_target_pairs={{0,1},{1,0},{2,3},{3,2},{4,8},{5,9},{6,10},{7,11},{8,4},{9,5},{10,... | collective-permute-start | bytes 196616 | tf_op jit(solution)/shard_map/ppermute | solution.py:658
  53.9 10.8 %all-to-all-start.1 = ((f32[32,2,128]{2,1,0:T(2,128)}), f32[32,2,128]{2,1,0:T(2,128)S(1)}, u32[]{:S(2)}, u32[]{:S(2)}) async-start(f32[32,2,128]{2,1,0:T(2,128)} %bitcast.4), calls=%async_computation.1 | async-start | bytes 65536 | tf_op jit(solution)/shard_map/all_to_all | solution.py:754
  57.5 2.0 %collective-permute-start.14 = (f32[8,512]{1,0:T(8,128)S(1)}, f32[8,512]{1,0:T(8,128)S(1)}, u32[]{:S(2)}, u32[]{:S(2)}) collective-permute-start(f32[8,512]{1,0:T(8,128)S(1)} %get-tuple-element.63), channel_id=1, source_target_pairs={{0,1},{1,0},{2,3},{3,2},{4,5},{5,4},{6,7},{7,6},{8,9},{9,8},{10,11... | collective-permute-start | bytes 49160 | tf_op jit(solution)/shard_map/ppermute | solution.py:659
  57.8 3.2 %collective-permute-start.15 = (f32[8,512]{1,0:T(8,128)S(1)}, f32[8,512]{1,0:T(8,128)S(1)}, u32[]{:S(2)}, u32[]{:S(2)}) collective-permute-start(f32[8,512]{1,0:T(8,128)S(1)} %get-tuple-element.64), channel_id=1, source_target_pairs={{1,2},{2,1},{3,0},{0,3},{5,6},{6,5},{7,4},{4,7},{9,10},{10,9},{11,... | collective-permute-start | bytes 49160 | tf_op jit(solution)/shard_map/ppermute | solution.py:659
  71.0 11.3 %collective-permute-start.16 = (f32[32,512]{1,0:T(8,128)S(1)}, f32[32,512]{1,0:T(8,128)S(1)}, u32[]{:S(2)}, u32[]{:S(2)}) collective-permute-start(f32[32,512]{1,0:T(8,128)S(1)} %get-tuple-element.68), channel_id=1, source_target_pairs={{0,4},{4,0},{8,12},{12,8},{16,20},{20,16},{24,28},{28,24},{1,5},{5... | collective-permute-start | bytes 196616 | tf_op jit(solution)/shard_map/ppermute | solution.py:659
  71.6 10.7 %collective-permute-start.17 = (f32[32,512]{1,0:T(8,128)S(1)}, f32[32,512]{1,0:T(8,128)S(1)}, u32[]{:S(2)}, u32[]{:S(2)}) collective-permute-start(f32[32,512]{1,0:T(8,128)S(1)} %get-tuple-element.69), channel_id=1, source_target_pairs={{0,1},{1,0},{2,3},{3,2},{4,8},{5,9},{6,10},{7,11},{8,4},{9,5},{10,... | collective-permute-start | bytes 196616 | tf_op jit(solution)/shard_map/ppermute | solution.py:658
  71.6 10.7 %all-to-all-start.2 = ((f32[32,2,128]{2,1,0:T(2,128)}), f32[32,2,128]{2,1,0:T(2,128)S(1)}, u32[]{:S(2)}, u32[]{:S(2)}) async-start(f32[32,2,128]{2,1,0:T(2,128)} %bitcast.6), calls=%async_computation.2 | async-start | bytes 65536 | tf_op jit(solution)/shard_map/all_to_all | solution.py:754
  75.0 2.0 %collective-permute-start.18 = (f32[8,512]{1,0:T(8,128)S(1)}, f32[8,512]{1,0:T(8,128)S(1)}, u32[]{:S(2)}, u32[]{:S(2)}) collective-permute-start(f32[8,512]{1,0:T(8,128)S(1)} %get-tuple-element.70), channel_id=1, source_target_pairs={{0,1},{1,0},{2,3},{3,2},{4,5},{5,4},{6,7},{7,6},{8,9},{9,8},{10,11... | collective-permute-start | bytes 49160 | tf_op jit(solution)/shard_map/ppermute | solution.py:659
  75.3 3.2 %collective-permute-start.19 = (f32[8,512]{1,0:T(8,128)S(1)}, f32[8,512]{1,0:T(8,128)S(1)}, u32[]{:S(2)}, u32[]{:S(2)}) collective-permute-start(f32[8,512]{1,0:T(8,128)S(1)} %get-tuple-element.71), channel_id=1, source_target_pairs={{1,2},{2,1},{3,0},{0,3},{5,6},{6,5},{7,4},{4,7},{9,10},{10,9},{11,... | collective-permute-start | bytes 49160 | tf_op jit(solution)/shard_map/ppermute | solution.py:659

commit v7 on v6

--- a/solution.py
+++ b/solution.py
@@ -325,7 +325,7 @@
         kap_ref[index] = jnp.where(inside_y & keep, value, 0.0)
         return carry
 
-    lax.fori_loop(0, planes + 2, kappa_plane, 0)
+    lax.fori_loop(0, planes + 2, kappa_plane, 0, unroll=2)
     mid = pl.ds(0, rows)
 
     def z_face(index, carry):
@@ -337,7 +337,7 @@
         fz_ref[index] = coef * mean * (f_high - f_low)
         return carry
 
-    lax.fori_loop(0, planes + 1, z_face, 0)
+    lax.fori_loop(0, planes + 1, z_face, 0, unroll=3)
     row_mid = row[:rows]
     lane_mid = lane[:rows]
     wait_all(reads[1:])
@@ -384,7 +384,7 @@
         return (inv, g)
 
     blank = jnp.zeros((rows, width), f32)
-    lax.fori_loop(0, planes, assemble_plane, (blank, blank))
+    lax.fori_loop(0, planes, assemble_plane, (blank, blank), unroll=2)
 
     def backward(step, after):
         plane = planes - 1 - step
@@ -392,7 +392,7 @@
         b_ref[plane] = value
         return value
 
-    lax.fori_loop(0, planes, backward, blank)
+    lax.fori_loop(0, planes, backward, blank, unroll=4)
     cz_ref[0] = jnp.where(first_z, 0.0, cz_ref[0])
     cz_ref[planes] = jnp.where(last_z, 0.0, cz_ref[planes])
     writes = [
@@ -531,7 +531,7 @@
         work_ref[plane] = value
         return value * inv_ref[plane]
 
-    lax.fori_loop(0, planes, residual, empty)
+    lax.fori_loop(0, planes, residual, empty, unroll=4)
     start_all([writes[name] for name in out_names[:-2]])
 
     def direction(step, after):
@@ -594,7 +594,7 @@
             u_ref[plane] = value
             return value
 
-        lax.fori_loop(0, planes, backward, empty)
+        lax.fori_loop(0, planes, backward, empty, unroll=4)
         write_edges(even_z, even_y, u_ref, edges_z, edges_y)
         reads["dest"].wait()
         parts = coarse_parts(region_row(w_ref, code_ref), held["dest"])

time: 96.7 us -> 96.3 us (level)
  no operation moved by 1% of the time
where the time goes in v7:
time: 96.3 us; the launch traced here: 96 us
  starting transfers between devices  30.7 us (32%)
  Pallas kernels  29.9 us (31%)
  waiting for transfers between devices  23.8 us (25%)
  blocking collectives  8.94 us (9%)
  local copies, waits for them, and re-layouts  1.73 us (2%)
    pallas_call x7, Pallas kernels, call(): pl.pallas_call(kernel, out_shape=made, in_specs=specs(args), out_specs=sp...  29.9 us
    ppermute x14, starting transfers between devices, swap(): return lax.ppermute(block, axis, swaps(axis, first))  17.2 us
    all_to_all x3, starting transfers between devices, exchange(): return lax.all_to_all(blocks, ('gz', 'gy'), 0, 0).reshape(parts.shape)  12.8 us
    ppermute x14, waiting for transfers between devices, swap(): return lax.ppermute(block, axis, swaps(axis, first))  12.8 us
    all_to_all x3, waiting for transfers between devices, exchange(): return lax.all_to_all(blocks, ('gz', 'gy'), 0, 0).reshape(parts.shape)  11 us
    all_to_all x1, blocking collectives, exchange(): return lax.all_to_all(blocks, ('gz', 'gy'), 0, 0).reshape(parts.shape)  8.94 us
  transfers between devices with their start and end apart: 23, of which 7 were waited for; matrix products, arithmetic and copies ran while one was open for 2% of the time, Pallas kernels for 4%

profile of v7, /device:TPU:0, one launch (start us, length us, event | category | flops | bytes accessed | tf_op | source)
XLA Modules:
  0.0 96.0 jit_solution(251645171505335855)
XLA Ops:
  0.6 1.1 %shard_map.68 = (f32[3,32,512]{2,1,0:T(8,128)S(1)}, f32[3,32,512]{2,1,0:T(8,128)S(1)}, f32[8,3,512]{2,1,0:T(4,128)S(1)}, f32[8,3,512]{2,1,0:T(4,128)S(1)}, f32[16,640]{1,0:T(8,128)S(1)}) custom-call(f32[8,32,512]{2,1,0:T(8,128)} %frac_hbm.3, f32[20,640]{1,0:T(8,128)} %coarse_hbm.1), custom_call_target="tpu_custom_call" | custom-call | tf_op jit(solution)/shard_map/pallas_call | solution.py:637
  1.8 0.6 collective-permute-start.2
  2.3 2.6 %collective-permute-start.3 = (f32[8,3,512]{2,1,0:T(4,128)S(1)}, f32[8,3,512]{2,1,0:T(4,128)S(1)}, u32[]{:S(2)}, u32[]{:S(2)}) collective-permute-start(f32[8,3,512]{2,1,0:T(4,128)S(1)} %get-tuple-element.45), channel_id=1, source_target_pairs={{1,2},{2,1},{3,0},{0,3},{5,6},{6,5},{7,4},{4,7},{9,10},{10,9},{11,... | collective-permute-start | bytes 147464 | tf_op jit(solution)/shard_map/ppermute | solution.py:659
  4.9 1.5 %collective-permute-start = (f32[3,32,512]{2,1,0:T(8,128)S(1)}, f32[3,32,512]{2,1,0:T(8,128)S(1)}, u32[]{:S(2)}, u32[]{:S(2)}) collective-permute-start(f32[3,32,512]{2,1,0:T(8,128)S(1)} %get-tuple-element.42), channel_id=1, source_target_pairs={{0,4},{4,0},{8,12},{12,8},{16,20},{20,16},{24,28},{28,24},{1,5},{5... | collective-permute-start | bytes 589832 | tf_op jit(solution)/shard_map/ppermute | solution.py:659
  6.4 0.0 collective-permute-start.1
  6.4 0.5 collective-permute-start.7
  6.9 2.9 %collective-permute-start.6 = (f32[16,640]{1,0:T(8,128)S(1)}, f32[16,640]{1,0:T(8,128)S(1)}, u32[]{:S(2)}, u32[]{:S(2)}) collective-permute-start(f32[16,640]{1,0:T(8,128)S(1)} %get-tuple-element.46), channel_id=1, source_target_pairs={{0,4},{4,0},{8,12},{12,8},{16,20},{20,16},{24,28},{28,24},{1,5},{5... | collective-permute-start | bytes 122888 | tf_op jit(solution)/shard_map/ppermute | solution.py:659
  9.9 0.1 collective-permute-start.5
  10.0 7.9 %collective-permute-done.6 = f32[16,640]{1,0:T(8,128)S(1)} collective-permute-done((f32[16,640]{1,0:T(8,128)S(1)}, f32[16,640]{1,0:T(8,128)S(1)}, u32[]{:S(2)}, u32[]{:S(2)}) %collective-permute-start.6) | collective-permute-done | bytes 40992 | tf_op jit(solution)/shard_map/ppermute | solution.py:659
  17.9 2.5 %collective-permute-start.4 = (f32[2,3,3,512]{3,2,1,0:T(4,128)S(1)}, f32[2,3,3,512]{3,2,1,0:T(4,128)S(1)}, u32[]{:S(2)}, u32[]{:S(2)}) collective-permute-start(f32[2,3,3,512]{3,2,1,0:T(4,128)S(1)} %get-tuple-element.83), channel_id=1, source_target_pairs={{0,4},{4,0},{8,12},{12,8},{16,20},{20,16},{24,28},{28,24},{1,5},{5... | collective-permute-start | bytes 110600 | tf_op jit(solution)/shard_map/ppermute | solution.py:659
  20.3 1.2 %reshape.37.own_ref = f32[20,32,20]{2,1,0:T(8,128)S(1)} reshape(f32[20,640]{1,0:T(8,128)} %coarse_hbm.1) | data formatting | bytes 102400 | tf_op jit(solution)/shard_map/reshape | solution.py:714
  21.5 0.3 reshape.38.near_ref
  21.8 0.0 collective-permute-done.7
  21.8 0.3 reshape.39.far_ref
  22.1 3.9 %shard_map.69.dest_hbm.refs_13_.refs_20_ = f32[52,64,128]{2,1,0:T(8,128)} custom-call(f32[20,32,20]{2,1,0:T(8,128)S(1)} %reshape.37.own_ref, f32[16,32,20]{2,1,0:T(8,128)S(1)} %reshape.38.near_ref, f32[16,32,20]{2,1,0:T(8,128)S(1)} %reshape.39.far_ref), custom_call_target="tpu_custom_call" | custom-call | tf_op jit(solution)/shard_map/pallas_call | solution.py:637
  26.0 0.0 collective-permute-done.5.k1_in
  26.0 0.0 collective-permute-done.1.z1_in
  26.0 8.1 %shard_map.70 = (f32[2,32,512]{2,1,0:T(8,128)S(1)}, f32[2,32,512]{2,1,0:T(8,128)S(1)}, f32[2,8,512]{2,1,0:T(8,128)S(1)}, f32[2,8,512]{2,1,0:T(8,128)S(1)}, f32[6...) custom-call(f32[3,32,512]{2,1,0:T(8,128)S(1)} %collective-permute-do, ...), custom_call_target="tpu_custom_call" | custom-call | tf_op jit(solution)/shard_map/pallas_call | solution.py:637
  34.1 0.1 collective-permute-start.8
  34.2 0.1 collective-permute-start.9
  34.3 5.8 %all-to-all-start = ((f32[32,2,128]{2,1,0:T(2,128)}), f32[32,2,128]{2,1,0:T(2,128)S(1)}, u32[]{:S(2)}, u32[]{:S(2)}) async-start(f32[32,2,128]{2,1,0:T(2,128)} %bitcast.2), calls=%async_computation | async-start | bytes 65536 | tf_op jit(solution)/shard_map/all_to_all | solution.py:754
  40.1 0.3 collective-permute-start.10
  40.5 1.6 %collective-permute-start.11 = (f32[2,8,512]{2,1,0:T(8,128)S(1)}, f32[2,8,512]{2,1,0:T(8,128)S(1)}, u32[]{:S(2)}, u32[]{:S(2)}) collective-permute-start(f32[2,8,512]{2,1,0:T(8,128)S(1)} %get-tuple-element.51), channel_id=1, source_target_pairs={{1,2},{2,1},{3,0},{0,3},{5,6},{6,5},{7,4},{4,7},{9,10},{10,9},{11,... | collective-permute-start | bytes 98312 | tf_op jit(solution)/shard_map/ppermute | solution.py:659
  42.1 1.7 %collective-permute-done.11.refs_4_.refs_5_.refs_6_ = f32[2,8,512]{2,1,0:T(8,128)S(1)} collective-permute-done((f32[2,8,512]{2,1,0:T(8,128)S(1)}, f32[2,8,512]{2,1,0:T(8,128)S(1)}, u32[]{:S(2)}, u32[]{:S(2)}) %collective-permute-start.11) | collective-permute-done | bytes 32800 | tf_op jit(solution)/shard_map/ppermute | solution.py:659
  43.8 3.6 %all-to-all-done = f32[32,2,128]{2,1,0:T(2,128)S(1)} async-done(((f32[32,2,128]{2,1,0:T(2,128)}), f32[32,2,128]{2,1,0:T(2,128)S(1)}, u32[]{:S(2)}, u32[]{:S(2)}) %all-to-all-start) | async-done | bytes 32800 | tf_op jit(solution)/shard_map/all_to_all | solution.py:754
  47.4 0.0 collective-permute-done.8.refs_1_.refs_2_.refs_3_
  47.4 0.0 collective-permute-done.9.refs_2_.refs_3_.refs_4_
  47.4 5.6 %shard_map.71 = (f32[32,512]{1,0:T(8,128)S(1)}, f32[32,512]{1,0:T(8,128)S(1)}, f32[8,512]{1,0:T(8,128)S(1)}, f32[8,512]{1,0:T(8,128)S(1)}, f32[64,128]{1,0:T(8,1...) custom-call(f32[64,128]{1,0:T(8,128)S(1)} %bitcast.12, ...), custom_call_target="tpu_custom_call" | custom-call | tf_op jit(solution)/shard_map/pallas_call | solution.py:637
  53.0 0.6 collective-permute-start.12
  53.6 0.0 collective-permute-start.13
  53.6 3.6 %all-to-all-start.1 = ((f32[32,2,128]{2,1,0:T(2,128)}), f32[32,2,128]{2,1,0:T(2,128)S(1)}, u32[]{:S(2)}, u32[]{:S(2)}) async-start(f32[32,2,128]{2,1,0:T(2,128)} %bitcast.4), calls=%async_computation.1 | async-start | bytes 65536 | tf_op jit(solution)/shard_map/all_to_all | solution.py:754
  57.2 0.3 collective-permute-start.14
  57.5 1.6 %collective-permute-start.15 = (f32[8,512]{1,0:T(8,128)S(1)}, f32[8,512]{1,0:T(8,128)S(1)}, u32[]{:S(2)}, u32[]{:S(2)}) collective-permute-start(f32[8,512]{1,0:T(8,128)S(1)} %get-tuple-element.64), channel_id=1, source_target_pairs={{1,2},{2,1},{3,0},{0,3},{5,6},{6,5},{7,4},{4,7},{9,10},{10,9},{11,... | collective-permute-start | bytes 49160 | tf_op jit(solution)/shard_map/ppermute | solution.py:659
  59.2 1.6 %collective-permute-done.15.refs_9_.refs_10_ = f32[8,512]{1,0:T(8,128)S(1)} collective-permute-done((f32[8,512]{1,0:T(8,128)S(1)}, f32[8,512]{1,0:T(8,128)S(1)}, u32[]{:S(2)}, u32[]{:S(2)}) %collective-permute-start.15) | collective-permute-done | bytes 16416 | tf_op jit(solution)/shard_map/ppermute | solution.py:659
  60.7 3.7 %all-to-all-done.1 = f32[32,2,128]{2,1,0:T(2,128)S(1)} async-done(((f32[32,2,128]{2,1,0:T(2,128)}), f32[32,2,128]{2,1,0:T(2,128)S(1)}, u32[]{:S(2)}, u32[]{:S(2)}) %all-to-all-start.1) | async-done | bytes 32800 | tf_op jit(solution)/shard_map/all_to_all | solution.py:754
  64.5 0.0 collective-permute-done.12.refs_6_.refs_7_
  64.5 0.0 collective-permute-done.13.refs_7_.refs_8_
  64.5 6.1 %shard_map.72 = (f32[32,512]{1,0:T(8,128)S(1)}, f32[32,512]{1,0:T(8,128)S(1)}, f32[8,512]{1,0:T(8,128)S(1)}, f32[8,512]{1,0:T(8,128)S(1)}, f32[64,128]{1,0:T(8,1...) custom-call(f32[64,128]{1,0:T(8,128)S(1)} %bitcast.13, f32[64,128]{1,0:T(8,128)S(1)} %bitcast.15, ...), custom_call_target="tpu_custom_call" | custom-call | tf_op jit(solution)/shard_map/pallas_call | solution.py:637
  70.6 0.6 collective-permute-start.16
  71.2 0.0 collective-permute-start.17
  71.2 3.4 %all-to-all-start.2 = ((f32[32,2,128]{2,1,0:T(2,128)}), f32[32,2,128]{2,1,0:T(2,128)S(1)}, u32[]{:S(2)}, u32[]{:S(2)}) async-start(f32[32,2,128]{2,1,0:T(2,128)} %bitcast.6), calls=%async_computation.2 | async-start | bytes 65536 | tf_op jit(solution)/shard_map/all_to_all | solution.py:754
  74.6 0.3 collective-permute-start.18
  75.0 1.6 %collective-permute-start.19 = (f32[8,512]{1,0:T(8,128)S(1)}, f32[8,512]{1,0:T(8,128)S(1)}, u32[]{:S(2)}, u32[]{:S(2)}) collective-permute-start(f32[8,512]{1,0:T(8,128)S(1)} %get-tuple-element.71), channel_id=1, source_target_pairs={{1,2},{2,1},{3,0},{0,3},{5,6},{6,5},{7,4},{4,7},{9,10},{10,9},{11,... | collective-permute-start | bytes 49160 | tf_op jit(solution)/shard_map/ppermute | solution.py:659
  76.6 1.6 %collective-permute-done.19.refs_14_ = f32[8,512]{1,0:T(8,128)S(1)} collective-permute-done((f32[8,512]{1,0:T(8,128)S(1)}, f32[8,512]{1,0:T(8,128)S(1)}, u32[]{:S(2)}, u32[]{:S(2)}) %collective-permute-start.19) | collective-permute-done | bytes 16416 | tf_op jit(solution)/shard_map/ppermute | solution.py:659
  78.2 3.7 %all-to-all-done.2 = f32[32,2,128]{2,1,0:T(2,128)S(1)} async-done(((f32[32,2,128]{2,1,0:T(2,128)}), f32[32,2,128]{2,1,0:T(2,128)S(1)}, u32[]{:S(2)}, u32[]{:S(2)}) %all-to-all-start.2) | async-done | bytes 32800 | tf_op jit(solution)/shard_map/all_to_all | solution.py:754
  81.9 3.7 %shard_map.73 = (f32[32,128]{1,0:T(8,128)S(1)}, f32[10,32,512]{2,1,0:T(8,128)S(1)}, f32[8,32,512]{2,1,0:T(8,128)S(1)}, f32[8,32,512]{2,1,0:T(8,128)S(1)}, f32[8,...) custom-call(f32[64,128]{1,0:T(8,128)S(1)} %bitcast.14, f32[64,128]{1,0:T(8,128)S(1)} %bitcast.16, ...), custom_call_target="tpu_custom_call" | custom-call | tf_op jit(solution)/shard_map/pallas_call | solution.py:637
  85.7 8.9 %all_to_all.20 = f32[32,1,128]{2,1,0:T(1,128)S(1)} all-to-all(f32[32,1,128]{2,1,0:T(1,128)S(1)} %bitcast.23), channel_id=1, replica_groups=mesh['gz'=8,'gy'=4] {'gz','gy'}, dimensions={0} | all-to-all | bytes 32768 | tf_op jit(solution)/shard_map/all_to_all | solution.py:754
  94.6 1.4 %shard_map.74 = (f32[8,32,512]{2,1,0:T(8,128)}, f32[8,32,512]{2,1,0:T(8,128)}) custom-call(f32[64,128]{1,0:T(8,128)S(1)} %bitcast.17, f32[64,128]{1,0:T(8,128)S(1)} %bitcast.19, f32[32,128]{1,0:T(8,128)S(1)} %bitcast.22, f32[10,32,512]{2,1,0:T(8,128)S(1)} %get-tuple-element.76.z_ref, f32[8,32,512]{2,1,0:T(8,128)S(1)} %get-tuple-element.77.w_ref, ...), custom_call_target="tpu_custom_call" | custom-call | tf_op jit(solution)/shard_map/pallas_call | solution.py:637
  (10 shorter events, 0.0 us)
Async XLA Ops:
  1.8 5.2 %collective-permute-start.2 = (f32[8,3,512]{2,1,0:T(4,128)S(1)}, f32[8,3,512]{2,1,0:T(4,128)S(1)}, u32[]{:S(2)}, u32[]{:S(2)}) collective-permute-start(f32[8,3,512]{2,1,0:T(4,128)S(1)} %get-tuple-element.44), channel_id=1, source_target_pairs={{0,1},{1,0},{2,3},{3,2},{4,5},{5,4},{6,7},{7,6},{8,9},{9,8},{10,11... | collective-permute-start | bytes 147464 | tf_op jit(solution)/shard_map/ppermute | solution.py:659
  2.3 7.5 %collective-permute-start.3 = (f32[8,3,512]{2,1,0:T(4,128)S(1)}, f32[8,3,512]{2,1,0:T(4,128)S(1)}, u32[]{:S(2)}, u32[]{:S(2)}) collective-permute-start(f32[8,3,512]{2,1,0:T(4,128)S(1)} %get-tuple-element.45), channel_id=1, source_target_pairs={{1,2},{2,1},{3,0},{0,3},{5,6},{6,5},{7,4},{4,7},{9,10},{10,9},{11,... | collective-permute-start | bytes 147464 | tf_op jit(solution)/shard_map/ppermute | solution.py:659
  4.9 21.1 %collective-permute-start = (f32[3,32,512]{2,1,0:T(8,128)S(1)}, f32[3,32,512]{2,1,0:T(8,128)S(1)}, u32[]{:S(2)}, u32[]{:S(2)}) collective-permute-start(f32[3,32,512]{2,1,0:T(8,128)S(1)} %get-tuple-element.42), channel_id=1, source_target_pairs={{0,4},{4,0},{8,12},{12,8},{16,20},{20,16},{24,28},{28,24},{1,5},{5... | collective-permute-start | bytes 589832 | tf_op jit(solution)/shard_map/ppermute | solution.py:659
  6.4 19.6 %collective-permute-start.1 = (f32[3,32,512]{2,1,0:T(8,128)S(1)}, f32[3,32,512]{2,1,0:T(8,128)S(1)}, u32[]{:S(2)}, u32[]{:S(2)}) collective-permute-start(f32[3,32,512]{2,1,0:T(8,128)S(1)} %get-tuple-element.43), channel_id=1, source_target_pairs={{0,1},{1,0},{2,3},{3,2},{4,8},{5,9},{6,10},{7,11},{8,4},{9,5},{10,... | collective-permute-start | bytes 589832 | tf_op jit(solution)/shard_map/ppermute | solution.py:658
  6.4 15.4 %collective-permute-start.7 = (f32[16,640]{1,0:T(8,128)S(1)}, f32[16,640]{1,0:T(8,128)S(1)}, u32[]{:S(2)}, u32[]{:S(2)}) collective-permute-start(f32[16,640]{1,0:T(8,128)S(1)} %get-tuple-element.46), channel_id=1, source_target_pairs={{0,1},{1,0},{2,3},{3,2},{4,8},{5,9},{6,10},{7,11},{8,4},{9,5},{10,... | collective-permute-start | bytes 122888 | tf_op jit(solution)/shard_map/ppermute | solution.py:658
  6.9 10.9 %collective-permute-start.6 = (f32[16,640]{1,0:T(8,128)S(1)}, f32[16,640]{1,0:T(8,128)S(1)}, u32[]{:S(2)}, u32[]{:S(2)}) collective-permute-start(f32[16,640]{1,0:T(8,128)S(1)} %get-tuple-element.46), channel_id=1, source_target_pairs={{0,4},{4,0},{8,12},{12,8},{16,20},{20,16},{24,28},{28,24},{1,5},{5... | collective-permute-start | bytes 122888 | tf_op jit(solution)/shard_map/ppermute | solution.py:659
  9.9 16.1 %collective-permute-start.5 = (f32[2,3,3,512]{3,2,1,0:T(4,128)S(1)}, f32[2,3,3,512]{3,2,1,0:T(4,128)S(1)}, u32[]{:S(2)}, u32[]{:S(2)}) collective-permute-start(f32[2,3,3,512]{3,2,1,0:T(4,128)S(1)} %get-tuple-element.82), channel_id=1, source_target_pairs={{0,1},{1,0},{2,3},{3,2},{4,8},{5,9},{6,10},{7,11},{8,4},{9,5},{10,... | collective-permute-start | bytes 110600 | tf_op jit(solution)/shard_map/ppermute | solution.py:658
  17.9 8.1 %collective-permute-start.4 = (f32[2,3,3,512]{3,2,1,0:T(4,128)S(1)}, f32[2,3,3,512]{3,2,1,0:T(4,128)S(1)}, u32[]{:S(2)}, u32[]{:S(2)}) collective-permute-start(f32[2,3,3,512]{3,2,1,0:T(4,128)S(1)} %get-tuple-element.83), channel_id=1, source_target_pairs={{0,4},{4,0},{8,12},{12,8},{16,20},{20,16},{24,28},{28,24},{1,5},{5... | collective-permute-start | bytes 110600 | tf_op jit(solution)/shard_map/ppermute | solution.py:659
  34.1 13.3 %collective-permute-start.8 = (f32[2,32,512]{2,1,0:T(8,128)S(1)}, f32[2,32,512]{2,1,0:T(8,128)S(1)}, u32[]{:S(2)}, u32[]{:S(2)}) collective-permute-start(f32[2,32,512]{2,1,0:T(8,128)S(1)} %get-tuple-element.48), channel_id=1, source_target_pairs={{0,4},{4,0},{8,12},{12,8},{16,20},{20,16},{24,28},{28,24},{1,5},{5... | collective-permute-start | bytes 393224 | tf_op jit(solution)/shard_map/ppermute | solution.py:659
  34.2 13.2 %collective-permute-start.9 = (f32[2,32,512]{2,1,0:T(8,128)S(1)}, f32[2,32,512]{2,1,0:T(8,128)S(1)}, u32[]{:S(2)}, u32[]{:S(2)}) collective-permute-start(f32[2,32,512]{2,1,0:T(8,128)S(1)} %get-tuple-element.49), channel_id=1, source_target_pairs={{0,1},{1,0},{2,3},{3,2},{4,8},{5,9},{6,10},{7,11},{8,4},{9,5},{10,... | collective-permute-start | bytes 393224 | tf_op jit(solution)/shard_map/ppermute | solution.py:658
  34.3 13.1 %all-to-all-start = ((f32[32,2,128]{2,1,0:T(2,128)}), f32[32,2,128]{2,1,0:T(2,128)S(1)}, u32[]{:S(2)}, u32[]{:S(2)}) async-start(f32[32,2,128]{2,1,0:T(2,128)} %bitcast.2), calls=%async_computation | async-start | bytes 65536 | tf_op jit(solution)/shard_map/all_to_all | solution.py:754
  40.1 2.0 %collective-permute-start.10 = (f32[2,8,512]{2,1,0:T(8,128)S(1)}, f32[2,8,512]{2,1,0:T(8,128)S(1)}, u32[]{:S(2)}, u32[]{:S(2)}) collective-permute-start(f32[2,8,512]{2,1,0:T(8,128)S(1)} %get-tuple-element.50), channel_id=1, source_target_pairs={{0,1},{1,0},{2,3},{3,2},{4,5},{5,4},{6,7},{7,6},{8,9},{9,8},{10,11... | collective-permute-start | bytes 98312 | tf_op jit(solution)/shard_map/ppermute | solution.py:659
  40.5 3.4 %collective-permute-start.11 = (f32[2,8,512]{2,1,0:T(8,128)S(1)}, f32[2,8,512]{2,1,0:T(8,128)S(1)}, u32[]{:S(2)}, u32[]{:S(2)}) collective-permute-start(f32[2,8,512]{2,1,0:T(8,128)S(1)} %get-tuple-element.51), channel_id=1, source_target_pairs={{1,2},{2,1},{3,0},{0,3},{5,6},{6,5},{7,4},{4,7},{9,10},{10,9},{11,... | collective-permute-start | bytes 98312 | tf_op jit(solution)/shard_map/ppermute | solution.py:659
  53.0 11.5 %collective-permute-start.12 = (f32[32,512]{1,0:T(8,128)S(1)}, f32[32,512]{1,0:T(8,128)S(1)}, u32[]{:S(2)}, u32[]{:S(2)}) collective-permute-start(f32[32,512]{1,0:T(8,128)S(1)} %get-tuple-element.61), channel_id=1, source_target_pairs={{0,4},{4,0},{8,12},{12,8},{16,20},{20,16},{24,28},{28,24},{1,5},{5... | collective-permute-start | bytes 196616 | tf_op jit(solution)/shard_map/ppermute | solution.py:659
  53.6 10.9 %collective-permute-start.13 = (f32[32,512]{1,0:T(8,128)S(1)}, f32[32,512]{1,0:T(8,128)S(1)}, u32[]{:S(2)}, u32[]{:S(2)}) collective-permute-start(f32[32,512]{1,0:T(8,128)S(1)} %get-tuple-element.62), channel_id=1, source_target_pairs={{0,1},{1,0},{2,3},{3,2},{4,8},{5,9},{6,10},{7,11},{8,4},{9,5},{10,... | collective-permute-start | bytes 196616 | tf_op jit(solution)/shard_map/ppermute | solution.py:658
  53.6 10.8 %all-to-all-start.1 = ((f32[32,2,128]{2,1,0:T(2,128)}), f32[32,2,128]{2,1,0:T(2,128)S(1)}, u32[]{:S(2)}, u32[]{:S(2)}) async-start(f32[32,2,128]{2,1,0:T(2,128)} %bitcast.4), calls=%async_computation.1 | async-start | bytes 65536 | tf_op jit(solution)/shard_map/all_to_all | solution.py:754
  57.2 2.0 %collective-permute-start.14 = (f32[8,512]{1,0:T(8,128)S(1)}, f32[8,512]{1,0:T(8,128)S(1)}, u32[]{:S(2)}, u32[]{:S(2)}) collective-permute-start(f32[8,512]{1,0:T(8,128)S(1)} %get-tuple-element.63), channel_id=1, source_target_pairs={{0,1},{1,0},{2,3},{3,2},{4,5},{5,4},{6,7},{7,6},{8,9},{9,8},{10,11... | collective-permute-start | bytes 49160 | tf_op jit(solution)/shard_map/ppermute | solution.py:659
  57.5 3.2 %collective-permute-start.15 = (f32[8,512]{1,0:T(8,128)S(1)}, f32[8,512]{1,0:T(8,128)S(1)}, u32[]{:S(2)}, u32[]{:S(2)}) collective-permute-start(f32[8,512]{1,0:T(8,128)S(1)} %get-tuple-element.64), channel_id=1, source_target_pairs={{1,2},{2,1},{3,0},{0,3},{5,6},{6,5},{7,4},{4,7},{9,10},{10,9},{11,... | collective-permute-start | bytes 49160 | tf_op jit(solution)/shard_map/ppermute | solution.py:659
  70.6 11.3 %collective-permute-start.16 = (f32[32,512]{1,0:T(8,128)S(1)}, f32[32,512]{1,0:T(8,128)S(1)}, u32[]{:S(2)}, u32[]{:S(2)}) collective-permute-start(f32[32,512]{1,0:T(8,128)S(1)} %get-tuple-element.68), channel_id=1, source_target_pairs={{0,4},{4,0},{8,12},{12,8},{16,20},{20,16},{24,28},{28,24},{1,5},{5... | collective-permute-start | bytes 196616 | tf_op jit(solution)/shard_map/ppermute | solution.py:659
  71.2 10.7 %collective-permute-start.17 = (f32[32,512]{1,0:T(8,128)S(1)}, f32[32,512]{1,0:T(8,128)S(1)}, u32[]{:S(2)}, u32[]{:S(2)}) collective-permute-start(f32[32,512]{1,0:T(8,128)S(1)} %get-tuple-element.69), channel_id=1, source_target_pairs={{0,1},{1,0},{2,3},{3,2},{4,8},{5,9},{6,10},{7,11},{8,4},{9,5},{10,... | collective-permute-start | bytes 196616 | tf_op jit(solution)/shard_map/ppermute | solution.py:658
  71.2 10.7 %all-to-all-start.2 = ((f32[32,2,128]{2,1,0:T(2,128)}), f32[32,2,128]{2,1,0:T(2,128)S(1)}, u32[]{:S(2)}, u32[]{:S(2)}) async-start(f32[32,2,128]{2,1,0:T(2,128)} %bitcast.6), calls=%async_computation.2 | async-start | bytes 65536 | tf_op jit(solution)/shard_map/all_to_all | solution.py:754
  74.6 2.0 %collective-permute-start.18 = (f32[8,512]{1,0:T(8,128)S(1)}, f32[8,512]{1,0:T(8,128)S(1)}, u32[]{:S(2)}, u32[]{:S(2)}) collective-permute-start(f32[8,512]{1,0:T(8,128)S(1)} %get-tuple-element.70), channel_id=1, source_target_pairs={{0,1},{1,0},{2,3},{3,2},{4,5},{5,4},{6,7},{7,6},{8,9},{9,8},{10,11... | collective-permute-start | bytes 49160 | tf_op jit(solution)/shard_map/ppermute | solution.py:659
  75.0 3.2 %collective-permute-start.19 = (f32[8,512]{1,0:T(8,128)S(1)}, f32[8,512]{1,0:T(8,128)S(1)}, u32[]{:S(2)}, u32[]{:S(2)}) collective-permute-start(f32[8,512]{1,0:T(8,128)S(1)} %get-tuple-element.71), channel_id=1, source_target_pairs={{1,2},{2,1},{3,0},{0,3},{5,6},{6,5},{7,4},{4,7},{9,10},{10,9},{11,... | collective-permute-start | bytes 49160 | tf_op jit(solution)/shard_map/ppermute | solution.py:659

commit v8 on v7

--- a/solution.py
+++ b/solution.py
@@ -579,7 +579,7 @@
 
     blank = jnp.zeros((8, LANES), f32)
     dots, _ = lax.fori_loop(
-        0, planes, image_plane, ((blank,) * (3 if stage else 2), blank if last else empty), unroll=2
+        0, planes, image_plane, ((blank,) * (3 if stage else 2), blank if last else empty), unroll=4
     )
     if not last:
         writes["w"].start()
@@ -610,8 +610,8 @@
     mixed = alphas[2] * betas[2]
     planes = r_ref.shape[0]
     writes = []
-    for half in range(2):
-        low, high = half * planes // 2, (half + 1) * planes // 2
+    for half in range(4):
+        low, high = half * planes // 4, (half + 1) * planes // 4
         x_new[low:high] = part_ref[low:high] + alphas[2] * z_ref[low + 1 : high + 1] + mixed * p_ref[low:high]
         r_new[low:high] = r_ref[low:high] - alphas[2] * w_ref[low:high] - mixed * s_ref[low:high]
         piece = pl.ds(low, high - low)
@@ -795,7 +795,7 @@
         call(
             final_kernel,
             tag("hbm", [field, field]),
-            like([field, field]) + [semaphores(4)],
+            like([field, field]) + [semaphores(8)],
             tag("vmem", parts[1:]) + tag("kept", kept),
         )
     )

time: 96.3 us -> 96.2 us (level)
  no operation moved by 1% of the time
where the time goes in v8:
time: 96.2 us; the launch traced here: 95.9 us
  starting transfers between devices  30.7 us (32%)
  Pallas kernels  29.8 us (31%)
  waiting for transfers between devices  23.8 us (25%)
  blocking collectives  8.94 us (9%)
  local copies, waits for them, and re-layouts  1.73 us (2%)
    pallas_call x7, Pallas kernels, call(): pl.pallas_call(kernel, out_shape=made, in_specs=specs(args), out_specs=sp...  29.8 us
    ppermute x14, starting transfers between devices, swap(): return lax.ppermute(block, axis, swaps(axis, first))  17.2 us
    all_to_all x3, starting transfers between devices, exchange(): return lax.all_to_all(blocks, ('gz', 'gy'), 0, 0).reshape(parts.shape)  12.8 us
    ppermute x14, waiting for transfers between devices, swap(): return lax.ppermute(block, axis, swaps(axis, first))  12.8 us
    all_to_all x3, waiting for transfers between devices, exchange(): return lax.all_to_all(blocks, ('gz', 'gy'), 0, 0).reshape(parts.shape)  11 us
    all_to_all x1, blocking collectives, exchange(): return lax.all_to_all(blocks, ('gz', 'gy'), 0, 0).reshape(parts.shape)  8.94 us
  transfers between devices with their start and end apart: 23, of which 7 were waited for; matrix products, arithmetic and copies ran while one was open for 2% of the time, Pallas kernels for 4%

profile of v8, /device:TPU:0, one launch (start us, length us, event | category | flops | bytes accessed | tf_op | source)
XLA Modules:
  0.0 95.9 jit_solution(10094962896697459985)
XLA Ops:
  0.6 1.1 %shard_map.68 = (f32[3,32,512]{2,1,0:T(8,128)S(1)}, f32[3,32,512]{2,1,0:T(8,128)S(1)}, f32[8,3,512]{2,1,0:T(4,128)S(1)}, f32[8,3,512]{2,1,0:T(4,128)S(1)}, f32[16,640]{1,0:T(8,128)S(1)}) custom-call(f32[8,32,512]{2,1,0:T(8,128)} %frac_hbm.3, f32[20,640]{1,0:T(8,128)} %coarse_hbm.1), custom_call_target="tpu_custom_call" | custom-call | tf_op jit(solution)/shard_map/pallas_call | solution.py:637
  1.8 0.6 collective-permute-start.2
  2.3 2.6 %collective-permute-start.3 = (f32[8,3,512]{2,1,0:T(4,128)S(1)}, f32[8,3,512]{2,1,0:T(4,128)S(1)}, u32[]{:S(2)}, u32[]{:S(2)}) collective-permute-start(f32[8,3,512]{2,1,0:T(4,128)S(1)} %get-tuple-element.45), channel_id=1, source_target_pairs={{1,2},{2,1},{3,0},{0,3},{5,6},{6,5},{7,4},{4,7},{9,10},{10,9},{11,... | collective-permute-start | bytes 147464 | tf_op jit(solution)/shard_map/ppermute | solution.py:659
  4.9 1.5 %collective-permute-start = (f32[3,32,512]{2,1,0:T(8,128)S(1)}, f32[3,32,512]{2,1,0:T(8,128)S(1)}, u32[]{:S(2)}, u32[]{:S(2)}) collective-permute-start(f32[3,32,512]{2,1,0:T(8,128)S(1)} %get-tuple-element.42), channel_id=1, source_target_pairs={{0,4},{4,0},{8,12},{12,8},{16,20},{20,16},{24,28},{28,24},{1,5},{5... | collective-permute-start | bytes 589832 | tf_op jit(solution)/shard_map/ppermute | solution.py:659
  6.4 0.0 collective-permute-start.1
  6.4 0.5 collective-permute-start.7
  6.9 2.9 %collective-permute-start.6 = (f32[16,640]{1,0:T(8,128)S(1)}, f32[16,640]{1,0:T(8,128)S(1)}, u32[]{:S(2)}, u32[]{:S(2)}) collective-permute-start(f32[16,640]{1,0:T(8,128)S(1)} %get-tuple-element.46), channel_id=1, source_target_pairs={{0,4},{4,0},{8,12},{12,8},{16,20},{20,16},{24,28},{28,24},{1,5},{5... | collective-permute-start | bytes 122888 | tf_op jit(solution)/shard_map/ppermute | solution.py:659
  9.9 0.1 collective-permute-start.5
  10.0 7.9 %collective-permute-done.6 = f32[16,640]{1,0:T(8,128)S(1)} collective-permute-done((f32[16,640]{1,0:T(8,128)S(1)}, f32[16,640]{1,0:T(8,128)S(1)}, u32[]{:S(2)}, u32[]{:S(2)}) %collective-permute-start.6) | collective-permute-done | bytes 40992 | tf_op jit(solution)/shard_map/ppermute | solution.py:659
  17.9 2.5 %collective-permute-start.4 = (f32[2,3,3,512]{3,2,1,0:T(4,128)S(1)}, f32[2,3,3,512]{3,2,1,0:T(4,128)S(1)}, u32[]{:S(2)}, u32[]{:S(2)}) collective-permute-start(f32[2,3,3,512]{3,2,1,0:T(4,128)S(1)} %get-tuple-element.83), channel_id=1, source_target_pairs={{0,4},{4,0},{8,12},{12,8},{16,20},{20,16},{24,28},{28,24},{1,5},{5... | collective-permute-start | bytes 110600 | tf_op jit(solution)/shard_map/ppermute | solution.py:659
  20.3 1.2 %reshape.37.own_ref = f32[20,32,20]{2,1,0:T(8,128)S(1)} reshape(f32[20,640]{1,0:T(8,128)} %coarse_hbm.1) | data formatting | bytes 102400 | tf_op jit(solution)/shard_map/reshape | solution.py:714
  21.5 0.3 reshape.38.near_ref
  21.8 0.0 collective-permute-done.7
  21.8 0.3 reshape.39.far_ref
  22.1 3.9 %shard_map.69.dest_hbm.refs_13_.refs_20_ = f32[52,64,128]{2,1,0:T(8,128)} custom-call(f32[20,32,20]{2,1,0:T(8,128)S(1)} %reshape.37.own_ref, f32[16,32,20]{2,1,0:T(8,128)S(1)} %reshape.38.near_ref, f32[16,32,20]{2,1,0:T(8,128)S(1)} %reshape.39.far_ref), custom_call_target="tpu_custom_call" | custom-call | tf_op jit(solution)/shard_map/pallas_call | solution.py:637
  26.0 0.0 collective-permute-done.5.k1_in
  26.0 0.0 collective-permute-done.1.z1_in
  26.0 8.1 %shard_map.70 = (f32[2,32,512]{2,1,0:T(8,128)S(1)}, f32[2,32,512]{2,1,0:T(8,128)S(1)}, f32[2,8,512]{2,1,0:T(8,128)S(1)}, f32[2,8,512]{2,1,0:T(8,128)S(1)}, f32[6...) custom-call(f32[3,32,512]{2,1,0:T(8,128)S(1)} %collective-permute-do, ...), custom_call_target="tpu_custom_call" | custom-call | tf_op jit(solution)/shard_map/pallas_call | solution.py:637
  34.1 0.1 collective-permute-start.8
  34.2 0.1 collective-permute-start.9
  34.3 5.8 %all-to-all-start = ((f32[32,2,128]{2,1,0:T(2,128)}), f32[32,2,128]{2,1,0:T(2,128)S(1)}, u32[]{:S(2)}, u32[]{:S(2)}) async-start(f32[32,2,128]{2,1,0:T(2,128)} %bitcast.2), calls=%async_computation | async-start | bytes 65536 | tf_op jit(solution)/shard_map/all_to_all | solution.py:754
  40.1 0.3 collective-permute-start.10
  40.5 1.6 %collective-permute-start.11 = (f32[2,8,512]{2,1,0:T(8,128)S(1)}, f32[2,8,512]{2,1,0:T(8,128)S(1)}, u32[]{:S(2)}, u32[]{:S(2)}) collective-permute-start(f32[2,8,512]{2,1,0:T(8,128)S(1)} %get-tuple-element.51), channel_id=1, source_target_pairs={{1,2},{2,1},{3,0},{0,3},{5,6},{6,5},{7,4},{4,7},{9,10},{10,9},{11,... | collective-permute-start | bytes 98312 | tf_op jit(solution)/shard_map/ppermute | solution.py:659
  42.1 1.7 %collective-permute-done.11.refs_4_.refs_5_.refs_6_ = f32[2,8,512]{2,1,0:T(8,128)S(1)} collective-permute-done((f32[2,8,512]{2,1,0:T(8,128)S(1)}, f32[2,8,512]{2,1,0:T(8,128)S(1)}, u32[]{:S(2)}, u32[]{:S(2)}) %collective-permute-start.11) | collective-permute-done | bytes 32800 | tf_op jit(solution)/shard_map/ppermute | solution.py:659
  43.8 3.6 %all-to-all-done = f32[32,2,128]{2,1,0:T(2,128)S(1)} async-done(((f32[32,2,128]{2,1,0:T(2,128)}), f32[32,2,128]{2,1,0:T(2,128)S(1)}, u32[]{:S(2)}, u32[]{:S(2)}) %all-to-all-start) | async-done | bytes 32800 | tf_op jit(solution)/shard_map/all_to_all | solution.py:754
  47.4 0.0 collective-permute-done.8.refs_1_.refs_2_.refs_3_
  47.4 0.0 collective-permute-done.9.refs_2_.refs_3_.refs_4_
  47.4 5.5 %shard_map.71 = (f32[32,512]{1,0:T(8,128)S(1)}, f32[32,512]{1,0:T(8,128)S(1)}, f32[8,512]{1,0:T(8,128)S(1)}, f32[8,512]{1,0:T(8,128)S(1)}, f32[64,128]{1,0:T(8,1...) custom-call(f32[64,128]{1,0:T(8,128)S(1)} %bitcast.12, ...), custom_call_target="tpu_custom_call" | custom-call | tf_op jit(solution)/shard_map/pallas_call | solution.py:637
  53.0 0.6 collective-permute-start.12
  53.6 3.6 %all-to-all-start.1 = ((f32[32,2,128]{2,1,0:T(2,128)}), f32[32,2,128]{2,1,0:T(2,128)S(1)}, u32[]{:S(2)}, u32[]{:S(2)}) async-start(f32[32,2,128]{2,1,0:T(2,128)} %bitcast.4), calls=%async_computation.1 | async-start | bytes 65536 | tf_op jit(solution)/shard_map/all_to_all | solution.py:754
  57.2 0.3 collective-permute-start.14
  57.5 1.6 %collective-permute-start.15 = (f32[8,512]{1,0:T(8,128)S(1)}, f32[8,512]{1,0:T(8,128)S(1)}, u32[]{:S(2)}, u32[]{:S(2)}) collective-permute-start(f32[8,512]{1,0:T(8,128)S(1)} %get-tuple-element.64), channel_id=1, source_target_pairs={{1,2},{2,1},{3,0},{0,3},{5,6},{6,5},{7,4},{4,7},{9,10},{10,9},{11,... | collective-permute-start | bytes 49160 | tf_op jit(solution)/shard_map/ppermute | solution.py:659
  59.1 0.0 collective-permute-done.14.refs_8_.refs_9_
  59.1 1.6 %collective-permute-done.15.refs_9_.refs_10_ = f32[8,512]{1,0:T(8,128)S(1)} collective-permute-done((f32[8,512]{1,0:T(8,128)S(1)}, f32[8,512]{1,0:T(8,128)S(1)}, u32[]{:S(2)}, u32[]{:S(2)}) %collective-permute-start.15) | collective-permute-done | bytes 16416 | tf_op jit(solution)/shard_map/ppermute | solution.py:659
  60.7 3.7 %all-to-all-done.1 = f32[32,2,128]{2,1,0:T(2,128)S(1)} async-done(((f32[32,2,128]{2,1,0:T(2,128)}), f32[32,2,128]{2,1,0:T(2,128)S(1)}, u32[]{:S(2)}, u32[]{:S(2)}) %all-to-all-start.1) | async-done | bytes 32800 | tf_op jit(solution)/shard_map/all_to_all | solution.py:754
  64.4 6.1 %shard_map.72 = (f32[32,512]{1,0:T(8,128)S(1)}, f32[32,512]{1,0:T(8,128)S(1)}, f32[8,512]{1,0:T(8,128)S(1)}, f32[8,512]{1,0:T(8,128)S(1)}, f32[64,128]{1,0:T(8,1...) custom-call(f32[64,128]{1,0:T(8,128)S(1)} %bitcast.13, f32[64,128]{1,0:T(8,128)S(1)} %bitcast.15, ...), custom_call_target="tpu_custom_call" | custom-call | tf_op jit(solution)/shard_map/pallas_call | solution.py:637
  70.6 0.6 collective-permute-start.16
  71.2 0.0 collective-permute-start.17
  71.2 3.4 %all-to-all-start.2 = ((f32[32,2,128]{2,1,0:T(2,128)}), f32[32,2,128]{2,1,0:T(2,128)S(1)}, u32[]{:S(2)}, u32[]{:S(2)}) async-start(f32[32,2,128]{2,1,0:T(2,128)} %bitcast.6), calls=%async_computation.2 | async-start | bytes 65536 | tf_op jit(solution)/shard_map/all_to_all | solution.py:754
  74.6 0.3 collective-permute-start.18
  74.9 1.6 %collective-permute-start.19 = (f32[8,512]{1,0:T(8,128)S(1)}, f32[8,512]{1,0:T(8,128)S(1)}, u32[]{:S(2)}, u32[]{:S(2)}) collective-permute-start(f32[8,512]{1,0:T(8,128)S(1)} %get-tuple-element.71), channel_id=1, source_target_pairs={{1,2},{2,1},{3,0},{0,3},{5,6},{6,5},{7,4},{4,7},{9,10},{10,9},{11,... | collective-permute-start | bytes 49160 | tf_op jit(solution)/shard_map/ppermute | solution.py:659
  76.6 0.0 collective-permute-done.18.refs_13_
  76.6 1.6 %collective-permute-done.19.refs_14_ = f32[8,512]{1,0:T(8,128)S(1)} collective-permute-done((f32[8,512]{1,0:T(8,128)S(1)}, f32[8,512]{1,0:T(8,128)S(1)}, u32[]{:S(2)}, u32[]{:S(2)}) %collective-permute-start.19) | collective-permute-done | bytes 16416 | tf_op jit(solution)/shard_map/ppermute | solution.py:659
  78.1 3.7 %all-to-all-done.2 = f32[32,2,128]{2,1,0:T(2,128)S(1)} async-done(((f32[32,2,128]{2,1,0:T(2,128)}), f32[32,2,128]{2,1,0:T(2,128)S(1)}, u32[]{:S(2)}, u32[]{:S(2)}) %all-to-all-start.2) | async-done | bytes 32800 | tf_op jit(solution)/shard_map/all_to_all | solution.py:754
  81.9 0.0 collective-permute-done.16.refs_11_
  81.9 3.8 %shard_map.73 = (f32[32,128]{1,0:T(8,128)S(1)}, f32[10,32,512]{2,1,0:T(8,128)S(1)}, f32[8,32,512]{2,1,0:T(8,128)S(1)}, f32[8,32,512]{2,1,0:T(8,128)S(1)}, f32[8,...) custom-call(f32[64,128]{1,0:T(8,128)S(1)} %bitcast.14, f32[64,128]{1,0:T(8,128)S(1)} %bitcast.16, ...), custom_call_target="tpu_custom_call" | custom-call | tf_op jit(solution)/shard_map/pallas_call | solution.py:637
  85.6 8.9 %all_to_all.20 = f32[32,1,128]{2,1,0:T(1,128)S(1)} all-to-all(f32[32,1,128]{2,1,0:T(1,128)S(1)} %bitcast.23), channel_id=1, replica_groups=mesh['gz'=8,'gy'=4] {'gz','gy'}, dimensions={0} | all-to-all | bytes 32768 | tf_op jit(solution)/shard_map/all_to_all | solution.py:754
  94.6 1.3 %shard_map.74 = (f32[8,32,512]{2,1,0:T(8,128)}, f32[8,32,512]{2,1,0:T(8,128)}) custom-call(f32[64,128]{1,0:T(8,128)S(1)} %bitcast.17, f32[64,128]{1,0:T(8,128)S(1)} %bitcast.19, f32[32,128]{1,0:T(8,128)S(1)} %bitcast.22, f32[10,32,512]{2,1,0:T(8,128)S(1)} %get-tuple-element.76.z_ref, f32[8,32,512]{2,1,0:T(8,128)S(1)} %get-tuple-element.77.w_ref, ...), custom_call_target="tpu_custom_call" | custom-call | tf_op jit(solution)/shard_map/pallas_call | solution.py:637
  (10 shorter events, 0.0 us)
Async XLA Ops:
  1.8 5.2 %collective-permute-start.2 = (f32[8,3,512]{2,1,0:T(4,128)S(1)}, f32[8,3,512]{2,1,0:T(4,128)S(1)}, u32[]{:S(2)}, u32[]{:S(2)}) collective-permute-start(f32[8,3,512]{2,1,0:T(4,128)S(1)} %get-tuple-element.44), channel_id=1, source_target_pairs={{0,1},{1,0},{2,3},{3,2},{4,5},{5,4},{6,7},{7,6},{8,9},{9,8},{10,11... | collective-permute-start | bytes 147464 | tf_op jit(solution)/shard_map/ppermute | solution.py:659
  2.3 7.5 %collective-permute-start.3 = (f32[8,3,512]{2,1,0:T(4,128)S(1)}, f32[8,3,512]{2,1,0:T(4,128)S(1)}, u32[]{:S(2)}, u32[]{:S(2)}) collective-permute-start(f32[8,3,512]{2,1,0:T(4,128)S(1)} %get-tuple-element.45), channel_id=1, source_target_pairs={{1,2},{2,1},{3,0},{0,3},{5,6},{6,5},{7,4},{4,7},{9,10},{10,9},{11,... | collective-permute-start | bytes 147464 | tf_op jit(solution)/shard_map/ppermute | solution.py:659
  4.9 21.1 %collective-permute-start = (f32[3,32,512]{2,1,0:T(8,128)S(1)}, f32[3,32,512]{2,1,0:T(8,128)S(1)}, u32[]{:S(2)}, u32[]{:S(2)}) collective-permute-start(f32[3,32,512]{2,1,0:T(8,128)S(1)} %get-tuple-element.42), channel_id=1, source_target_pairs={{0,4},{4,0},{8,12},{12,8},{16,20},{20,16},{24,28},{28,24},{1,5},{5... | collective-permute-start | bytes 589832 | tf_op jit(solution)/shard_map/ppermute | solution.py:659
  6.4 19.6 %collective-permute-start.1 = (f32[3,32,512]{2,1,0:T(8,128)S(1)}, f32[3,32,512]{2,1,0:T(8,128)S(1)}, u32[]{:S(2)}, u32[]{:S(2)}) collective-permute-start(f32[3,32,512]{2,1,0:T(8,128)S(1)} %get-tuple-element.43), channel_id=1, source_target_pairs={{0,1},{1,0},{2,3},{3,2},{4,8},{5,9},{6,10},{7,11},{8,4},{9,5},{10,... | collective-permute-start | bytes 589832 | tf_op jit(solution)/shard_map/ppermute | solution.py:658
  6.4 15.4 %collective-permute-start.7 = (f32[16,640]{1,0:T(8,128)S(1)}, f32[16,640]{1,0:T(8,128)S(1)}, u32[]{:S(2)}, u32[]{:S(2)}) collective-permute-start(f32[16,640]{1,0:T(8,128)S(1)} %get-tuple-element.46), channel_id=1, source_target_pairs={{0,1},{1,0},{2,3},{3,2},{4,8},{5,9},{6,10},{7,11},{8,4},{9,5},{10,... | collective-permute-start | bytes 122888 | tf_op jit(solution)/shard_map/ppermute | solution.py:658
  6.9 10.9 %collective-permute-start.6 = (f32[16,640]{1,0:T(8,128)S(1)}, f32[16,640]{1,0:T(8,128)S(1)}, u32[]{:S(2)}, u32[]{:S(2)}) collective-permute-start(f32[16,640]{1,0:T(8,128)S(1)} %get-tuple-element.46), channel_id=1, source_target_pairs={{0,4},{4,0},{8,12},{12,8},{16,20},{20,16},{24,28},{28,24},{1,5},{5... | collective-permute-start | bytes 122888 | tf_op jit(solution)/shard_map/ppermute | solution.py:659
  9.9 16.1 %collective-permute-start.5 = (f32[2,3,3,512]{3,2,1,0:T(4,128)S(1)}, f32[2,3,3,512]{3,2,1,0:T(4,128)S(1)}, u32[]{:S(2)}, u32[]{:S(2)}) collective-permute-start(f32[2,3,3,512]{3,2,1,0:T(4,128)S(1)} %get-tuple-element.82), channel_id=1, source_target_pairs={{0,1},{1,0},{2,3},{3,2},{4,8},{5,9},{6,10},{7,11},{8,4},{9,5},{10,... | collective-permute-start | bytes 110600 | tf_op jit(solution)/shard_map/ppermute | solution.py:658
  17.9 8.1 %collective-permute-start.4 = (f32[2,3,3,512]{3,2,1,0:T(4,128)S(1)}, f32[2,3,3,512]{3,2,1,0:T(4,128)S(1)}, u32[]{:S(2)}, u32[]{:S(2)}) collective-permute-start(f32[2,3,3,512]{3,2,1,0:T(4,128)S(1)} %get-tuple-element.83), channel_id=1, source_target_pairs={{0,4},{4,0},{8,12},{12,8},{16,20},{20,16},{24,28},{28,24},{1,5},{5... | collective-permute-start | bytes 110600 | tf_op jit(solution)/shard_map/ppermute | solution.py:659
  34.1 13.3 %collective-permute-start.8 = (f32[2,32,512]{2,1,0:T(8,128)S(1)}, f32[2,32,512]{2,1,0:T(8,128)S(1)}, u32[]{:S(2)}, u32[]{:S(2)}) collective-permute-start(f32[2,32,512]{2,1,0:T(8,128)S(1)} %get-tuple-element.48), channel_id=1, source_target_pairs={{0,4},{4,0},{8,12},{12,8},{16,20},{20,16},{24,28},{28,24},{1,5},{5... | collective-permute-start | bytes 393224 | tf_op jit(solution)/shard_map/ppermute | solution.py:659
  34.2 13.2 %collective-permute-start.9 = (f32[2,32,512]{2,1,0:T(8,128)S(1)}, f32[2,32,512]{2,1,0:T(8,128)S(1)}, u32[]{:S(2)}, u32[]{:S(2)}) collective-permute-start(f32[2,32,512]{2,1,0:T(8,128)S(1)} %get-tuple-element.49), channel_id=1, source_target_pairs={{0,1},{1,0},{2,3},{3,2},{4,8},{5,9},{6,10},{7,11},{8,4},{9,5},{10,... | collective-permute-start | bytes 393224 | tf_op jit(solution)/shard_map/ppermute | solution.py:658
  34.3 13.1 %all-to-all-start = ((f32[32,2,128]{2,1,0:T(2,128)}), f32[32,2,128]{2,1,0:T(2,128)S(1)}, u32[]{:S(2)}, u32[]{:S(2)}) async-start(f32[32,2,128]{2,1,0:T(2,128)} %bitcast.2), calls=%async_computation | async-start | bytes 65536 | tf_op jit(solution)/shard_map/all_to_all | solution.py:754
  40.1 2.0 %collective-permute-start.10 = (f32[2,8,512]{2,1,0:T(8,128)S(1)}, f32[2,8,512]{2,1,0:T(8,128)S(1)}, u32[]{:S(2)}, u32[]{:S(2)}) collective-permute-start(f32[2,8,512]{2,1,0:T(8,128)S(1)} %get-tuple-element.50), channel_id=1, source_target_pairs={{0,1},{1,0},{2,3},{3,2},{4,5},{5,4},{6,7},{7,6},{8,9},{9,8},{10,11... | collective-permute-start | bytes 98312 | tf_op jit(solution)/shard_map/ppermute | solution.py:659
  40.5 3.4 %collective-permute-start.11 = (f32[2,8,512]{2,1,0:T(8,128)S(1)}, f32[2,8,512]{2,1,0:T(8,128)S(1)}, u32[]{:S(2)}, u32[]{:S(2)}) collective-permute-start(f32[2,8,512]{2,1,0:T(8,128)S(1)} %get-tuple-element.51), channel_id=1, source_target_pairs={{1,2},{2,1},{3,0},{0,3},{5,6},{6,5},{7,4},{4,7},{9,10},{10,9},{11,... | collective-permute-start | bytes 98312 | tf_op jit(solution)/shard_map/ppermute | solution.py:659
  53.0 11.5 %collective-permute-start.12 = (f32[32,512]{1,0:T(8,128)S(1)}, f32[32,512]{1,0:T(8,128)S(1)}, u32[]{:S(2)}, u32[]{:S(2)}) collective-permute-start(f32[32,512]{1,0:T(8,128)S(1)} %get-tuple-element.61), channel_id=1, source_target_pairs={{0,4},{4,0},{8,12},{12,8},{16,20},{20,16},{24,28},{28,24},{1,5},{5... | collective-permute-start | bytes 196616 | tf_op jit(solution)/shard_map/ppermute | solution.py:659
  53.6 10.9 %collective-permute-start.13 = (f32[32,512]{1,0:T(8,128)S(1)}, f32[32,512]{1,0:T(8,128)S(1)}, u32[]{:S(2)}, u32[]{:S(2)}) collective-permute-start(f32[32,512]{1,0:T(8,128)S(1)} %get-tuple-element.62), channel_id=1, source_target_pairs={{0,1},{1,0},{2,3},{3,2},{4,8},{5,9},{6,10},{7,11},{8,4},{9,5},{10,... | collective-permute-start | bytes 196616 | tf_op jit(solution)/shard_map/ppermute | solution.py:658
  53.6 10.8 %all-to-all-start.1 = ((f32[32,2,128]{2,1,0:T(2,128)}), f32[32,2,128]{2,1,0:T(2,128)S(1)}, u32[]{:S(2)}, u32[]{:S(2)}) async-start(f32[32,2,128]{2,1,0:T(2,128)} %bitcast.4), calls=%async_computation.1 | async-start | bytes 65536 | tf_op jit(solution)/shard_map/all_to_all | solution.py:754
  57.2 2.0 %collective-permute-start.14 = (f32[8,512]{1,0:T(8,128)S(1)}, f32[8,512]{1,0:T(8,128)S(1)}, u32[]{:S(2)}, u32[]{:S(2)}) collective-permute-start(f32[8,512]{1,0:T(8,128)S(1)} %get-tuple-element.63), channel_id=1, source_target_pairs={{0,1},{1,0},{2,3},{3,2},{4,5},{5,4},{6,7},{7,6},{8,9},{9,8},{10,11... | collective-permute-start | bytes 49160 | tf_op jit(solution)/shard_map/ppermute | solution.py:659
  57.5 3.2 %collective-permute-start.15 = (f32[8,512]{1,0:T(8,128)S(1)}, f32[8,512]{1,0:T(8,128)S(1)}, u32[]{:S(2)}, u32[]{:S(2)}) collective-permute-start(f32[8,512]{1,0:T(8,128)S(1)} %get-tuple-element.64), channel_id=1, source_target_pairs={{1,2},{2,1},{3,0},{0,3},{5,6},{6,5},{7,4},{4,7},{9,10},{10,9},{11,... | collective-permute-start | bytes 49160 | tf_op jit(solution)/shard_map/ppermute | solution.py:659
  70.6 11.3 %collective-permute-start.16 = (f32[32,512]{1,0:T(8,128)S(1)}, f32[32,512]{1,0:T(8,128)S(1)}, u32[]{:S(2)}, u32[]{:S(2)}) collective-permute-start(f32[32,512]{1,0:T(8,128)S(1)} %get-tuple-element.68), channel_id=1, source_target_pairs={{0,4},{4,0},{8,12},{12,8},{16,20},{20,16},{24,28},{28,24},{1,5},{5... | collective-permute-start | bytes 196616 | tf_op jit(solution)/shard_map/ppermute | solution.py:659
  71.2 10.7 %collective-permute-start.17 = (f32[32,512]{1,0:T(8,128)S(1)}, f32[32,512]{1,0:T(8,128)S(1)}, u32[]{:S(2)}, u32[]{:S(2)}) collective-permute-start(f32[32,512]{1,0:T(8,128)S(1)} %get-tuple-element.69), channel_id=1, source_target_pairs={{0,1},{1,0},{2,3},{3,2},{4,8},{5,9},{6,10},{7,11},{8,4},{9,5},{10,... | collective-permute-start | bytes 196616 | tf_op jit(solution)/shard_map/ppermute | solution.py:658
  71.2 10.7 %all-to-all-start.2 = ((f32[32,2,128]{2,1,0:T(2,128)}), f32[32,2,128]{2,1,0:T(2,128)S(1)}, u32[]{:S(2)}, u32[]{:S(2)}) async-start(f32[32,2,128]{2,1,0:T(2,128)} %bitcast.6), calls=%async_computation.2 | async-start | bytes 65536 | tf_op jit(solution)/shard_map/all_to_all | solution.py:754
  74.6 2.0 %collective-permute-start.18 = (f32[8,512]{1,0:T(8,128)S(1)}, f32[8,512]{1,0:T(8,128)S(1)}, u32[]{:S(2)}, u32[]{:S(2)}) collective-permute-start(f32[8,512]{1,0:T(8,128)S(1)} %get-tuple-element.70), channel_id=1, source_target_pairs={{0,1},{1,0},{2,3},{3,2},{4,5},{5,4},{6,7},{7,6},{8,9},{9,8},{10,11... | collective-permute-start | bytes 49160 | tf_op jit(solution)/shard_map/ppermute | solution.py:659
  74.9 3.2 %collective-permute-start.19 = (f32[8,512]{1,0:T(8,128)S(1)}, f32[8,512]{1,0:T(8,128)S(1)}, u32[]{:S(2)}, u32[]{:S(2)}) collective-permute-start(f32[8,512]{1,0:T(8,128)S(1)} %get-tuple-element.71), channel_id=1, source_target_pairs={{1,2},{2,1},{3,0},{0,3},{5,6},{6,5},{7,4},{4,7},{9,10},{10,9},{11,... | collective-permute-start | bytes 49160 | tf_op jit(solution)/shard_map/ppermute | solution.py:659
